TPU v7x, 32 devices: a whole 2x2x4 slice. The times are simulated.
32 devices in a mesh: stream: 8 (over z, y), span: 4 (over x, core).
Axes of the slice: x: 2, y: 2, z: 4, core: 2. Of those that a mesh axis runs over, the one named last changes fastest.
Arguments:
- records: bfloat16 [32, 9, 4, 512], P(('stream', 'span')), may hold values from -6 to 6
- cells: int32 [32, 9, 512], P(('stream', 'span')), may hold values from 0 to 524287
- counts: int32 [32, 9], P(('stream', 'span')), may hold values from 0 to 512, as said below
- background: float32 [3, 512], replicated, may hold values from -6 to 6
- field: float32 [3, 512], replicated, may hold values from -6 to 6
Outputs:
- density: float32 [4, 512, 64, 512], P(None, 'stream', 'span')
- velocity: float32 [32, 9, 3, 512], P(('stream', 'span'))
Inputs may be any that keep to these rules, and one draw needn't show every extreme that they name: counts[o, d] live records of device o go in direction d: slots j < counts[o, d] are live, the others unused; counts is 0 where the destination span index lies beyond a wall. In every draw some device receives 512 live records from every device that sends to it.
All inputs are finite; a program needn't handle non-finite values.
Results may differ from a plain program's by a relative error of at most 0.00105.
Values may be sent and summed in bfloat16 or wider, within the bound.
No kernel may reach another device: no remote copies, remote signals or barrier semaphores. Data moves between devices by JAX's collectives and lax.ppermute only.
A program may use at most 192 MiB of HBM per device.

v0:
```python
import jax
import jax.numpy as jnp
from jax import lax
from jax.sharding import PartitionSpec as P

CX = 64
CY = 16
NZ = 512


spread_width = 12.5


def passed_along(value, axis, steps):
    count = lax.axis_size(axis)
    pairs = [(source, (source + steps) % count) for source in range(count)]
    return lax.ppermute(value, axis, pairs)


def shifted(value, axis, steps):
    count = lax.axis_size(axis)
    initial, last = (max(0, -steps), min(count, count - steps))
    return lax.ppermute(value, axis, [(source, source + steps) for source in range(initial, last)])


def with_halo(array, sides, width, wrap):
    for axis, dim in sides:
        size, length = (lax.axis_size(axis), array.shape[dim])
        up = [(i, (i + 1) % size) for i in range(size if wrap else size - 1)]
        down = [(j, i) for i, j in up]
        last = lax.slice_in_dim(array, length - width, length, axis=dim)
        initial = lax.slice_in_dim(array, 0, width, axis=dim)
        before = lax.ppermute(last, axis, up)
        after = lax.ppermute(initial, axis, down)
        array = jnp.concatenate([before, array, after], axis=dim)
    return array


def kernel_taps():
    offsets = jnp.arange(-6, 7).astype(jnp.float32)
    return jnp.exp(-offsets * offsets / spread_width)


def filter_valid(values, taps, axis):
    length = values.shape[axis] - 12
    total = taps[0] * lax.slice_in_dim(values, 0, length, axis=axis)
    for offset in range(1, 13):
        total = total + taps[offset] * lax.slice_in_dim(values, offset, offset + length, axis=axis)
    return total


def filter_depth(values, taps):
    padded = jnp.pad(values, ((0, 0), (0, 0), (0, 0), (6, 6)))
    return filter_valid(padded, taps, 3)


def shift_stream_records(block, offset):
    return passed_along(block, "stream", offset)


def shift_stream_cells(block, offset):
    return passed_along(block, "stream", offset)


def shift_span_records(block, offset):
    return shifted(block, "span", offset)


def shift_span_cells(block, offset):
    return shifted(block, "span", offset)


def on_device(records, cells, counts, background, field):
    cap = records.shape[3]
    cx_cells = CX
    cy_cells = CY
    depth_n = NZ
    slots = jnp.arange(cap, dtype=jnp.int32)
    live = slots[None, :] < counts[0][:, None]
    outgoing = jnp.where(live[:, None, :], records[0], jnp.zeros((), jnp.bfloat16))
    tagged = jnp.where(live, cells[0] + 1, 0)
    rows_records = outgoing.reshape(3, 3, 4, cap)
    rows_tags = tagged.reshape(3, 3, cap)
    rows_records = jnp.stack(
        [
            shift_stream_records(rows_records[0], -1),
            rows_records[1],
            shift_stream_records(rows_records[2], 1),
        ]
    )
    rows_tags = jnp.stack(
        [shift_stream_cells(rows_tags[0], -1), rows_tags[1], shift_stream_cells(rows_tags[2], 1)]
    )
    moved_records = jnp.stack(
        [
            shift_span_records(rows_records[:, 0], -1),
            rows_records[:, 1],
            shift_span_records(rows_records[:, 2], 1),
        ],
        axis=1,
    )
    moved_tags = jnp.stack(
        [
            shift_span_cells(rows_tags[:, 0], -1),
            rows_tags[:, 1],
            shift_span_cells(rows_tags[:, 2], 1),
        ],
        axis=1,
    )
    inbound = moved_records.reshape(9, 4, cap)
    in_tags = moved_tags.reshape(9, cap)
    alive = in_tags > 0
    cell_ids = in_tags - 1
    plane_of = jnp.where(alive, cell_ids // depth_n, -1)
    depth_of = jnp.where(alive, cell_ids % depth_n, -1)
    planes = jnp.arange(cx_cells * cy_cells, dtype=jnp.int32)
    depths = jnp.arange(depth_n, dtype=jnp.int32)

    def add_block(total, parts):
        values, plane_ids, depth_ids = parts
        where_plane = (plane_ids[:, None] == planes[None, :]).astype(jnp.bfloat16)
        where_depth = (depth_ids[:, None] == depths[None, :]).astype(jnp.bfloat16)
        weighted = values[:, :, None] * where_depth[None, :, :]
        return total + jnp.einsum(
            "rx,crz->cxz", where_plane, weighted, preferred_element_type=jnp.float32
        )

    start = jnp.zeros((4, cx_cells * cy_cells, depth_n), jnp.float32)
    binned = lax.scan(
        lambda total, parts: (add_block(total, parts), None), start, (inbound, plane_of, depth_of)
    )[0]
    binned = binned.reshape(4, cx_cells, cy_cells, depth_n)
    raw_taps = kernel_taps()
    unit_taps = raw_taps / jnp.sum(raw_taps)
    along_depth = filter_depth(binned, raw_taps)
    widened = with_halo(along_depth, (("stream", 1),), 6, True)
    along_x = filter_valid(widened, raw_taps, 1)
    widened = with_halo(along_x, (("span", 2),), 6, False)
    spread = filter_valid(widened, raw_taps, 2)
    charge = spread[3]
    forces = spread[:3] + charge[None] * field[:, None, None, :]
    density = jnp.concatenate([forces, charge[None]], axis=0)
    flow = background[:, None, None, :] + forces
    smooth = filter_depth(flow, unit_taps)
    widened = with_halo(smooth.astype(jnp.bfloat16), (("stream", 1),), 6, True).astype(smooth.dtype)
    smooth = filter_valid(widened, unit_taps, 1)
    widened = with_halo(smooth, (("span", 2),), 6, False)
    smooth = filter_valid(widened, unit_taps, 2)
    flat_smooth = smooth.reshape(3, -1)
    index = jnp.clip(cell_ids, 0, cx_cells * cy_cells * depth_n - 1)
    sampled = jnp.take(flat_smooth, index.reshape(-1), axis=1).reshape(3, 9, cap)
    sampled = jnp.where(alive[None], sampled, jnp.float32(0.0))
    velocity = jnp.transpose(sampled, (1, 0, 2))[None]
    return (density, velocity)


def solution(mesh):
    return jax.shard_map(
        on_device,
        mesh=mesh,
        in_specs=(
            P(("stream", "span"), None, None, None),
            P(("stream", "span"), None, None),
            P(("stream", "span"), None),
            P(),
            P(),
        ),
        out_specs=(P(None, "stream", "span", None), P(("stream", "span"), None, None, None)),
        check_vma=False,
    )
```

profile of v0, /device:TPU:0, one launch (start us, length us, event | category | flops | bytes accessed | tf_op | source)
XLA Modules:
  0.0 713.3 jit_solution(11738879537821191112)
XLA Ops:
  0.6 0.7 iota_compare_fusion.2
  1.4 0.8 bitcast_select_fusion
  2.2 6.1 collective-permute-start
  8.3 0.8 bitcast_select_fusion.1
  9.1 4.8 collective-permute-start.4
  13.8 1.4 collective-permute-done.4
  15.2 5.0 collective-permute-done.5
  20.2 1.3 collective-permute-start.7
  21.5 1.3 collective-permute-start.6
  22.8 0.7 fusion.189
  23.5 2.8 collective-permute-done.6
  26.4 1.3 collective-permute-start.2
  27.7 4.9 collective-permute-start.3
  32.8 0.7 collective-permute-done.3
  33.5 82.5 %while.11 = (s32[]{:T(128)}, f32[4,1024,512]{1,2,0:T(8,128)}, bf16[9,4,512]{2,1,0:T(4,128)(2,1)S(1)}, s32[9,512]{1,0:T(8,128)S(1)}, s32[9,512]{1,0:T(8,128)S(1)}, /*index=5*/s32[]{:T(128)}, s32[]{:T(128)}) while((s32[]{:T(128)}, f32[4,1024,512]{1,2,0:T(8,128)}, bf16[9,4,512]{2,1,0:T(4,128)(2,1)S(1)}, s32[9,512]{1,0:T(8,128)S(1)}, ...), condition=%wide.region_1.2_spmd.clone, body=%wide.region_0.1_spmd.clone.sunk | while | flops 2153775104 | bytes 17850468 | solution.py:129
  33.7 6.0 bitcast_add_fusion.2
  39.9 9.4 %bitcast_add_fusion.2 = f32[4,1024,512]{1,2,0:T(8,128)} fusion(f32[4,1024,512]{1,2,0:T(8,128)} %get-tuple-element.177, pred[]{:T(512)S(6)} %compare.8, s32[512]{0:T(512)S(1)} %bitcast.94, bf16[512,512]{0,1:T(8,128)(2,1)S(1)} %fusion.195, bf16[4,512]{1,0:T(4,128)(2,1)S(1)} %dynamic-slice_bitcast_fusion.2), kind=kOutput, calls=%fused_computation.3.clone.1 | convolution fusion | flops 2153250816 | bytes 17307648 | tf_op jit(solution)/shard_map/while/body/eval_jaxpr/rx,crz->cxz/dot_general | solution.py:124
  49.4 9.4 %bitcast_add_fusion.2 = f32[4,1024,512]{1,2,0:T(8,128)} fusion(f32[4,1024,512]{1,2,0:T(8,128)} %get-tuple-element.177, pred[]{:T(512)S(6)} %compare.8, s32[512]{0:T(512)S(1)} %bitcast.94, bf16[512,512]{0,1:T(8,128)(2,1)S(1)} %fusion.195, bf16[4,512]{1,0:T(4,128)(2,1)S(1)} %dynamic-slice_bitcast_fusion.2), kind=kOutput, calls=%fused_computation.3.clone.1 | convolution fusion | flops 2153250816 | bytes 17307648 | tf_op jit(solution)/shard_map/while/body/eval_jaxpr/rx,crz->cxz/dot_general | solution.py:124
  59.0 9.4 %bitcast_add_fusion.2 = f32[4,1024,512]{1,2,0:T(8,128)} fusion(f32[4,1024,512]{1,2,0:T(8,128)} %get-tuple-element.177, pred[]{:T(512)S(6)} %compare.8, s32[512]{0:T(512)S(1)} %bitcast.94, bf16[512,512]{0,1:T(8,128)(2,1)S(1)} %fusion.195, bf16[4,512]{1,0:T(4,128)(2,1)S(1)} %dynamic-slice_bitcast_fusion.2), kind=kOutput, calls=%fused_computation.3.clone.1 | convolution fusion | flops 2153250816 | bytes 17307648 | tf_op jit(solution)/shard_map/while/body/eval_jaxpr/rx,crz->cxz/dot_general | solution.py:124
  68.5 9.4 %bitcast_add_fusion.2 = f32[4,1024,512]{1,2,0:T(8,128)} fusion(f32[4,1024,512]{1,2,0:T(8,128)} %get-tuple-element.177, pred[]{:T(512)S(6)} %compare.8, s32[512]{0:T(512)S(1)} %bitcast.94, bf16[512,512]{0,1:T(8,128)(2,1)S(1)} %fusion.195, bf16[4,512]{1,0:T(4,128)(2,1)S(1)} %dynamic-slice_bitcast_fusion.2), kind=kOutput, calls=%fused_computation.3.clone.1 | convolution fusion | flops 2153250816 | bytes 17307648 | tf_op jit(solution)/shard_map/while/body/eval_jaxpr/rx,crz->cxz/dot_general | solution.py:124
  78.0 9.4 %bitcast_add_fusion.2 = f32[4,1024,512]{1,2,0:T(8,128)} fusion(f32[4,1024,512]{1,2,0:T(8,128)} %get-tuple-element.177, pred[]{:T(512)S(6)} %compare.8, s32[512]{0:T(512)S(1)} %bitcast.94, bf16[512,512]{0,1:T(8,128)(2,1)S(1)} %fusion.195, bf16[4,512]{1,0:T(4,128)(2,1)S(1)} %dynamic-slice_bitcast_fusion.2), kind=kOutput, calls=%fused_computation.3.clone.1 | convolution fusion | flops 2153250816 | bytes 17307648 | tf_op jit(solution)/shard_map/while/body/eval_jaxpr/rx,crz->cxz/dot_general | solution.py:124
  87.6 9.4 %bitcast_add_fusion.2 = f32[4,1024,512]{1,2,0:T(8,128)} fusion(f32[4,1024,512]{1,2,0:T(8,128)} %get-tuple-element.177, pred[]{:T(512)S(6)} %compare.8, s32[512]{0:T(512)S(1)} %bitcast.94, bf16[512,512]{0,1:T(8,128)(2,1)S(1)} %fusion.195, bf16[4,512]{1,0:T(4,128)(2,1)S(1)} %dynamic-slice_bitcast_fusion.2), kind=kOutput, calls=%fused_computation.3.clone.1 | convolution fusion | flops 2153250816 | bytes 17307648 | tf_op jit(solution)/shard_map/while/body/eval_jaxpr/rx,crz->cxz/dot_general | solution.py:124
  97.1 9.4 %bitcast_add_fusion.2 = f32[4,1024,512]{1,2,0:T(8,128)} fusion(f32[4,1024,512]{1,2,0:T(8,128)} %get-tuple-element.177, pred[]{:T(512)S(6)} %compare.8, s32[512]{0:T(512)S(1)} %bitcast.94, bf16[512,512]{0,1:T(8,128)(2,1)S(1)} %fusion.195, bf16[4,512]{1,0:T(4,128)(2,1)S(1)} %dynamic-slice_bitcast_fusion.2), kind=kOutput, calls=%fused_computation.3.clone.1 | convolution fusion | flops 2153250816 | bytes 17307648 | tf_op jit(solution)/shard_map/while/body/eval_jaxpr/rx,crz->cxz/dot_general | solution.py:124
  106.6 9.4 %bitcast_add_fusion.2 = f32[4,1024,512]{1,2,0:T(8,128)} fusion(f32[4,1024,512]{1,2,0:T(8,128)} %get-tuple-element.177, pred[]{:T(512)S(6)} %compare.8, s32[512]{0:T(512)S(1)} %bitcast.94, bf16[512,512]{0,1:T(8,128)(2,1)S(1)} %fusion.195, bf16[4,512]{1,0:T(4,128)(2,1)S(1)} %dynamic-slice_bitcast_fusion.2), kind=kOutput, calls=%fused_computation.3.clone.1 | convolution fusion | flops 2153250816 | bytes 17307648 | tf_op jit(solution)/shard_map/while/body/eval_jaxpr/rx,crz->cxz/dot_general | solution.py:124
  116.0 8.8 %copy.48 = f32[4,1024,512]{2,1,0:T(8,128)} copy(f32[4,1024,512]{1,2,0:T(8,128)} %get-tuple-element.39) | data formatting | bytes 16777216 | tf_op jit(solution)/shard_map/while | solution.py:129
  124.8 55.9 %fusion.55 = f32[4,64,16,512]{3,2,1,0:T(8,128)} fusion(f32[4,64,16,512]{3,2,1,0:T(8,128)} %bitcast.91, f32[]{:T(128)} %bitcast.30, f32[]{:T(128)} %bitcast.29, f32[]{:T(128)} %bitcast.28, f32[]{:T(128)} %bitcast.27, f32[]{:T(128)} %bitcast.26, f32[]{:T(128)} %bitcast.25, f32[]{:T(128)} %bitcast.24, f32[]{:T(128)} %bitcast.23, f32[]{:T(128)} %bitcast.22, ...), kind=kLoop, calls=%fused_computation.143 | loop fusion | flops 52428800 | bytes 16777268 | tf_op jit(solution)/shard_map/add | solution.py:48
  180.7 1.5 fusion.183
  182.3 5.2 collective-permute-start.9
  187.4 28.3 %collective-permute-done.8 = f32[4,6,16,512]{3,2,1,0:T(8,128)S(1)} collective-permute-done((f32[4,6,16,512]{3,2,1,0:T(8,128)S(1)}, f32[4,6,16,512]{3,2,1,0:T(8,128)S(1)}, u32[]{:S(2)}, u32[]{:S(2)}) %collective-permute-start.8) | collective-permute-done | bytes 786464 | tf_op jit(solution)/shard_map/ppermute | solution.py:33
  215.7 3.6 collective-permute-done.9
  219.3 51.2 %fusion.14 = f32[4,64,16,512]{3,2,1,0:T(8,128)S(1)} fusion(f32[4,64,16,512]{3,2,1,0:T(8,128)} %fusion.55, f32[4,6,16,512]{3,2,1,0:T(8,128)S(1)} %collective-permute-done.9, f32[4,6,16,512]{3,2,1,0:T(8,128)S(1)} %collective-permute-done.8, f32[]{:T(128)} %bitcast.30, f32[]{:T(128)} %bitcast.29, f32[]{:T(128)} %bitcast.28, f32[]{:T(128)} %bitcast.27, ...), kind=kLoop, calls=%fused_computation.102 | loop fusion | flops 77594624 | bytes 18350132 | tf_op jit(solution)/shard_map/add | solution.py:48
  270.5 1.1 fusion.182
  271.6 2.3 copy-done
  273.9 1.8 copy.51
  275.7 1.3 collective-permute-start.11
  277.0 1.8 copy.49
  278.9 3.5 collective-permute-start.10
  282.3 0.6 fusion.181
  282.9 0.7 broadcast_divide_fusion
  283.6 0.7 fusion.188
  284.3 1.9 copy.52
  286.2 1.0 collective-permute-done.10
  287.2 3.9 copy.50
  291.1 78.8 %fusion.70 = f32[4,64,16,512]{3,2,1,0:T(8,128)} fusion(f32[4,64,16,512]{3,2,1,0:T(8,128)} %copy-done, f32[4,64,6,512]{3,2,1,0:T(8,128)S(1)} %copy.52, f32[4,64,6,512]{3,2,1,0:T(8,128)} %copy.50, f32[]{:T(128)} %bitcast.30, f32[]{:T(128)} %bitcast.29, f32[]{:T(128)} %bitcast.28, f32[]{:T(128)} %bitcast.27, f32[]{:T(128)} %bitcast.26, f32[]{:T(128)} %bitcast.25, ...), kind=kLoop, calls=%fused_computation.158 | loop fusion | flops 77594624 | bytes 23068724 | tf_op jit(solution)/shard_map/add | solution.py:48
  369.9 3.5 slice_bitcast_fusion.5
  373.4 10.2 %broadcast_add_fusion = (f32[3,64,16,512]{3,2,1,0:T(8,128)}, f32[3,64,16,512]{3,2,1,0:T(8,128)}) fusion(f32[3,512]{1,0:T(4,128)S(1)} %copy-done.1, f32[3,512]{1,0:T(4,128)S(1)} %copy-done.2, f32[64,16,512]{2,1,0:T(8,128)S(1)} %get-tuple-element.82, f32[4,64,16,512]{3,2,1,0:T(8,128)} %fusion.70), kind=kLoop, calls=%fused_computation.284 | loop fusion | flops 4718592 | bytes 20983808 | tf_op jit(solution)/shard_map/add | solution.py:143
  383.6 44.1 %fusion.173 = bf16[3,64,16,512]{3,2,1,0:T(8,128)(2,1)S(1)} fusion(f32[3,64,16,512]{3,2,1,0:T(8,128)} %get-tuple-element.78, f32[]{:T(128)} %bitcast.44, f32[]{:T(128)} %bitcast.43, f32[]{:T(128)} %bitcast.42, f32[]{:T(128)} %bitcast.41, f32[]{:T(128)} %bitcast.40, f32[]{:T(128)} %bitcast.39, f32[]{:T(128)} %bitcast.38, f32[]{:T(128)} %bitcast.37, ...), kind=kLoop, calls=%fused_computation.282 | loop fusion | flops 40894464 | bytes 9437236 | tf_op jit(solution)/shard_map/convert_element_type | solution.py:145
  427.8 4.7 collective-permute-start.13
  432.5 4.8 collective-permute-done.12
  437.4 0.4 collective-permute-done.13
  437.8 3.4 maximum_convert_fusion
  441.2 41.3 %fusion.161 = f32[3,64,16,512]{3,2,1,0:T(8,128)} fusion(f32[3,76,16,512]{3,2,1,0:T(8,128)} %maximum_convert_fusion, f32[]{:T(128)} %bitcast.44, f32[]{:T(128)} %bitcast.43, f32[]{:T(128)} %bitcast.42, f32[]{:T(128)} %bitcast.41, f32[]{:T(128)} %bitcast.40, f32[]{:T(128)} %bitcast.39, f32[]{:T(128)} %bitcast.38, f32[]{:T(128)} %bitcast.37, f32[]{:T(128)} %bitcast.36, ...), kind=kLoop, calls=%fused_computation.257 | loop fusion | flops 39321600 | bytes 88080432 | tf_op jit(solution)/shard_map/add | solution.py:48
  482.4 3.6 fusion.184
  486.0 2.8 copy.55
  488.8 1.5 collective-permute-start.15
  490.4 2.9 copy.53
  493.2 33.5 %collective-permute-start.14 = (f32[3,64,6,512]{3,1,2,0:T(8,128)}, f32[3,64,6,512]{3,1,2,0:T(8,128)}, u32[]{:S(2)}, u32[]{:S(2)}) collective-permute-start(f32[3,64,6,512]{3,1,2,0:T(8,128)} %copy.53), channel_id=1, source_target_pairs={{0,1},{1,2},{2,3},{4,5},{5,6},{6,7},{8,9},{9,10},{10,11},{12,13},{... | collective-permute-start | bytes 7077896 | tf_op jit(solution)/shard_map/ppermute | solution.py:33
  526.9 8.9 %pad_maximum_fusion.4 = f32[4,64,16,512]{3,2,1,0:T(8,128)} fusion(f32[1,64,16,512]{3,2,1,0:T(8,128)} %get-tuple-element.83, f32[3,64,16,512]{3,2,1,0:T(8,128)} %get-tuple-element.79), kind=kLoop, calls=%fused_computation.195 | loop fusion | flops 2097152 | bytes 16777216 | tf_op jit(solution)/shard_map/concatenate | solution.py:142
  535.8 4.7 copy.56
  540.5 4.7 copy.54
  545.2 35.4 %fusion.130 = f32[3,64,16,512]{3,2,1,0:T(8,128)} fusion(f32[3,64,16,512]{3,2,1,0:T(8,128)S(1)} %bitcast.89, f32[3,64,6,512]{3,2,1,0:T(8,128)} %copy.56, f32[3,64,6,512]{3,2,1,0:T(8,128)} %copy.54, f32[]{:T(128)} %bitcast.44, f32[]{:T(128)} %bitcast.43, f32[]{:T(128)} %bitcast.42, f32[]{:T(128)} %bitcast.41, f32[]{:T(128)} %bitcast.40, f32[]{:T(128)} %bitcast.39, ...), kind=kLoop, calls=%fused_computation.223 | loop fusion | flops 58195968 | bytes 17301556 | tf_op jit(solution)/shard_map/add | solution.py:48
  580.5 10.3 %copy.64 = f32[1,3,1024,512]{3,1,2,0:T(4,128)} copy(f32[1,3,1024,512]{3,2,1,0:T(8,128)} %bitcast.92) | data formatting | bytes 12582912
  590.9 121.3 %gather_fusion = f32[4608,3]{0,1:T(4,128)S(1)} fusion(f32[3,524288]{1,0:T(4,128)} %bitcast.90, s32[5120]{0:T(1024)S(1)} %pad_clamp_fusion), kind=kCustom, calls=%fused_computation | custom fusion | bytes 129024 | tf_op jit(solution)/shard_map/jit(_take)/gather | solution.py:151
  712.2 0.7 copy.58
  (75 shorter events, 2.0 us)
Async XLA Ops:
  2.2 24.2 %collective-permute-start = (bf16[3,4,512]{2,1,0:T(4,128)(2,1)S(1)}, bf16[3,4,512]{2,1,0:T(4,128)(2,1)S(1)}, u32[]{:S(2)}, u32[]{:S(2)}) collective-permute-start(bf16[3,4,512]{2,1,0:T(4,128)(2,1)S(1)} %get-tuple-element.97), channel_id=1, source_target_pairs={{0,28},{4,0},{8,4},{12,8},{16,12},{20,16},{24,20},{28,24},{1,29},{... | collective-permute-start | bytes 36872 | tf_op jit(solution)/shard_map/ppermute | solution.py:17
  8.2 18.1 %collective-permute-start.1 = (bf16[3,4,512]{2,1,0:T(4,128)(2,1)S(1)}, bf16[3,4,512]{2,1,0:T(4,128)(2,1)S(1)}, u32[]{:S(2)}, u32[]{:S(2)}) collective-permute-start(bf16[3,4,512]{2,1,0:T(4,128)(2,1)S(1)} %get-tuple-element.98), channel_id=1, source_target_pairs={{0,4},{4,8},{8,12},{12,16},{16,20},{20,24},{24,28},{28,0},{1,5},{5... | collective-permute-start | bytes 36872 | tf_op jit(solution)/shard_map/ppermute | solution.py:17
  9.1 6.1 collective-permute-start.4
  13.8 6.3 collective-permute-start.5
  20.2 3.3 collective-permute-start.7
  21.5 4.8 collective-permute-start.6
  26.4 6.4 collective-permute-start.2
  27.7 5.8 collective-permute-start.3
  182.2 33.5 %collective-permute-start.8 = (f32[4,6,16,512]{3,2,1,0:T(8,128)S(1)}, f32[4,6,16,512]{3,2,1,0:T(8,128)S(1)}, u32[]{:S(2)}, u32[]{:S(2)}) collective-permute-start(f32[4,6,16,512]{3,2,1,0:T(8,128)S(1)} %get-tuple-element.86), channel_id=1, source_target_pairs={{0,4},{4,8},{8,12},{12,16},{16,20},{20,24},{24,28},{28,0},{1,5},{5... | collective-permute-start | bytes 2359304 | tf_op jit(solution)/shard_map/ppermute | solution.py:33
  182.3 37.1 %collective-permute-start.9 = (f32[4,6,16,512]{3,2,1,0:T(8,128)S(1)}, f32[4,6,16,512]{3,2,1,0:T(8,128)S(1)}, u32[]{:S(2)}, u32[]{:S(2)}) collective-permute-start(f32[4,6,16,512]{3,2,1,0:T(8,128)S(1)} %get-tuple-element.87), channel_id=1, source_target_pairs={{4,0},{8,4},{12,8},{16,12},{20,16},{24,20},{28,24},{0,28},{5,1},{9... | collective-permute-start | bytes 2359304 | tf_op jit(solution)/shard_map/ppermute | solution.py:34
  270.5 3.4 copy-start
  275.7 8.6 %collective-permute-start.11 = (f32[4,64,6,512]{3,1,2,0:T(8,128)S(1)}, f32[4,64,6,512]{3,1,2,0:T(8,128)S(1)}, u32[]{:S(2)}, u32[]{:S(2)}) collective-permute-start(f32[4,64,6,512]{3,1,2,0:T(8,128)S(1)} %copy.51), channel_id=1, source_target_pairs={{1,0},{2,1},{3,2},{5,4},{6,5},{7,6},{9,8},{10,9},{11,10},{13,12},{... | collective-permute-start | bytes 9437192 | tf_op jit(solution)/shard_map/ppermute | solution.py:34
  278.9 8.4 %collective-permute-start.10 = (f32[4,64,6,512]{3,1,2,0:T(8,128)S(1)}, f32[4,64,6,512]{3,1,2,0:T(8,128)S(1)}, u32[]{:S(2)}, u32[]{:S(2)}) collective-permute-start(f32[4,64,6,512]{3,1,2,0:T(8,128)S(1)} %copy.49), channel_id=1, source_target_pairs={{0,1},{1,2},{2,3},{4,5},{5,6},{6,7},{8,9},{9,10},{10,11},{12,13},{... | collective-permute-start | bytes 9437192 | tf_op jit(solution)/shard_map/ppermute | solution.py:33
  291.1 82.3 %copy-start.1 = (f32[3,512]{1,0:T(4,128)S(1)}, f32[3,512]{1,0:T(4,128)}, u32[]{:S(2)}) copy-start(f32[3,512]{1,0:T(4,128)} %param.10) | copy-start | bytes 18436
  291.1 82.3 %copy-start.2 = (f32[3,512]{1,0:T(4,128)S(1)}, f32[3,512]{1,0:T(4,128)}, u32[]{:S(2)}) copy-start(f32[3,512]{1,0:T(4,128)} %param.11) | copy-start | bytes 18436
  427.8 9.6 %collective-permute-start.12 = (bf16[3,6,16,512]{3,2,1,0:T(8,128)(2,1)S(1)}, bf16[3,6,16,512]{3,2,1,0:T(8,128)(2,1)S(1)}, u32[]{:S(2)}, u32[]{:S(2)}) collective-permute-start(bf16[3,6,16,512]{3,2,1,0:T(8,128)(2,1)S(1)} %get-tuple-element.90), channel_id=1, source_target_pairs={{0,4},{4,8},{8,12},{12,16},{16,20},{20,24},{24,28},{28,0},{1,5},{5... | collective-permute-start | bytes 884744 | tf_op jit(solution)/shard_map/ppermute | solution.py:33
  427.8 9.9 %collective-permute-start.13 = (bf16[3,6,16,512]{3,2,1,0:T(8,128)(2,1)S(1)}, bf16[3,6,16,512]{3,2,1,0:T(8,128)(2,1)S(1)}, u32[]{:S(2)}, u32[]{:S(2)}) collective-permute-start(bf16[3,6,16,512]{3,2,1,0:T(8,128)(2,1)S(1)} %get-tuple-element.91), channel_id=1, source_target_pairs={{4,0},{8,4},{12,8},{16,12},{20,16},{24,20},{28,24},{0,28},{5,1},{9... | collective-permute-start | bytes 884744 | tf_op jit(solution)/shard_map/ppermute | solution.py:34
  488.8 47.0 %collective-permute-start.15 = (f32[3,64,6,512]{3,1,2,0:T(8,128)}, f32[3,64,6,512]{3,1,2,0:T(8,128)}, u32[]{:S(2)}, u32[]{:S(2)}) collective-permute-start(f32[3,64,6,512]{3,1,2,0:T(8,128)} %copy.55), channel_id=1, source_target_pairs={{1,0},{2,1},{3,2},{5,4},{6,5},{7,6},{9,8},{10,9},{11,10},{13,12},{... | collective-permute-start | bytes 7077896 | tf_op jit(solution)/shard_map/ppermute | solution.py:34
  493.2 47.2 %collective-permute-start.14 = (f32[3,64,6,512]{3,1,2,0:T(8,128)}, f32[3,64,6,512]{3,1,2,0:T(8,128)}, u32[]{:S(2)}, u32[]{:S(2)}) collective-permute-start(f32[3,64,6,512]{3,1,2,0:T(8,128)} %copy.53), channel_id=1, source_target_pairs={{0,1},{1,2},{2,3},{4,5},{5,6},{6,7},{8,9},{9,10},{10,11},{12,13},{... | collective-permute-start | bytes 7077896 | tf_op jit(solution)/shard_map/ppermute | solution.py:33
  526.9 18.3 %slice-start = ((s8[6291456]{0:T(1024)(128)(4,1)}), s8[4194304]{0:T(1024)(128)(4,1)S(1)}, s32[]{:S(2)}) async-start(s8[6291456]{0:T(1024)(128)(4,1)} %bitcast.88), calls=%async_computation | async-start | bytes 8388608
  526.9 18.3 %slice-start.1 = ((s8[6291456]{0:T(1024)(128)(4,1)}), s8[2097152]{0:T(1024)(128)(4,1)S(1)}, s32[]{:S(2)}) async-start(s8[6291456]{0:T(1024)(128)(4,1)} %bitcast.88), calls=%async_computation.1 | async-start | bytes 4194304
where the time goes:
time: 724 us; the launch traced here: 713 us
  other arithmetic  334 us (46%)
  local copies, waits for them, and re-layouts  179 us (25%)
  matrix products  81 us (11%)
  starting transfers between devices  69.4 us (10%)
  waiting for transfers between devices  48 us (7%)
    add x5, other arithmetic, filter_valid(): total + taps[offset] * lax.slice_in_dim(values, offset, offset + length,...  262 us
    gather x2, local copies, waits for them, and re-layouts, on_device(): jnp.take(flat_smooth, index.reshape(-1), axis=1).reshape(3, 9, cap)  121 us
    dot_general x9, matrix products, add_block(): jnp.einsum('rx,crz->cxz', where_plane, weighted, preferred_element_type=j...  81 us
    convert_element_type x1, other arithmetic, on_device(): smooth.astype(jnp.bfloat16)  44.1 us
    ppermute x4, starting transfers between devices, with_halo(): before = lax.ppermute(last, axis, up)  37.1 us
    ppermute x4, waiting for transfers between devices, with_halo(): before = lax.ppermute(last, axis, up)  34.1 us
  transfers between devices with their start and end apart: 16, of which 9 were waited for; matrix products, arithmetic and copies ran while one was open for 3% of the time, Pallas kernels for 0%

commit v1 on v0

v1 whole, which is shorter than its diff:
```python
import functools

import jax
import jax.numpy as jnp
from jax import lax
from jax.experimental import pallas as pl
from jax.experimental.pallas import tpu as pltpu
from jax.sharding import PartitionSpec as P

CX = 64
CY = 16
NZ = 512
REACH = 6
TILE = 256
BX = 8
NB = 10
BP = BX * CY
FAR = 255.0
ROWS = 16

spread_width = 12.5


def kernel_taps():
    offsets = jnp.arange(-6, 7).astype(jnp.float32)
    return jnp.exp(-offsets * offsets / spread_width)


def gauss(d):
    return jnp.where(jnp.abs(d) < REACH + 0.5, jnp.exp(d * d * (-1.0 / spread_width)), 0.0)


def hi_lo(v):
    hi = v.astype(jnp.bfloat16)
    lo = (v - hi.astype(jnp.float32)).astype(jnp.bfloat16)
    return hi, lo


def columns(xt, pick):
    return lax.dot_general(
        xt.astype(jnp.bfloat16), pick, (((0,), (0,)), ((), ())), preferred_element_type=jnp.float32
    )


def x_filtered(load, taps, count):
    outs = []
    ins = [load(i) for i in range(count + 12)]
    for o in range(count):
        total = taps[6] * ins[o + 6]
        for k in range(1, 7):
            total = total + taps[6 + k] * (ins[o + 6 - k] + ins[o + 6 + k])
        outs.append(total)
    return outs


def spread_kernel(lo_ref, hi_ref, taps_ref, tab_ref, pick_ref, field_ref, out_ref, acc, amat, zmat):
    step = pl.program_id(0)

    @pl.when(step == 0)
    def _():
        def clear(i, _):
            acc[i] = jnp.zeros(acc.shape[1:], jnp.float32)
            return 0

        lax.fori_loop(0, NB, clear, 0)

        def tile(i, _):
            first, last = lo_ref[i], hi_ref[i]

            @pl.when(first <= last)
            def _():
                xt = tab_ref[i]
                zrep = columns(xt, pick_ref[...])
                lane = lax.broadcasted_iota(jnp.int32, (TILE, 128), 1).astype(jnp.float32)
                for q in range(NZ // 128):
                    g = gauss(lane + (128.0 * q) - zrep)
                    hi, lo = hi_lo(g)
                    cols = slice(128 * q, 128 * (q + 1))
                    zmat[0:TILE, cols] = hi
                    zmat[TILE : 2 * TILE, cols] = hi
                    zmat[2 * TILE : 3 * TILE, cols] = lo
                ypl = lax.broadcasted_iota(jnp.int32, (CY, TILE), 0).astype(jnp.float32)
                gy = gauss(ypl - xt[5:6, :])
                parts = [hi_lo(gy * xt[c : c + 1, :]) for c in range(4)]

                def bucket(b, _):
                    for xx in range(BX):
                        at = (b * BX + xx).astype(jnp.float32)
                        m = jnp.where(xt[4:5, :] == at, 1.0, 0.0)
                        m = jnp.broadcast_to(m, (CY, TILE)).astype(jnp.bfloat16)
                        for c in range(4):
                            rows = slice(c * BP + xx * CY, c * BP + (xx + 1) * CY)
                            hi = parts[c][0] * m
                            amat[rows, 0:TILE] = hi
                            amat[rows, TILE : 2 * TILE] = parts[c][1] * m
                            amat[rows, 2 * TILE : 3 * TILE] = hi
                    acc[b] += jnp.dot(amat[...], zmat[...], preferred_element_type=jnp.float32)
                    return 0

                lax.fori_loop(first, last + 1, bucket, 0)

            return 0

        lax.fori_loop(0, tab_ref.shape[0], tile, 0)

    @pl.when(step > 0)
    def _():
        b = step - 1
        taps = [taps_ref[k] for k in range(13)]

        def chunk(j, _):
            cols = pl.ds(pl.multiple_of(j * 128, 128), 128)
            charge = None
            for c in (3, 0, 1, 2):

                def load(i, c=c):
                    start = c * BP + (i % BX) * CY
                    return acc[b + i // BX, start : start + CY, cols]

                outs = x_filtered(load, taps, BX)
                if c == 3:
                    charge = outs
                else:
                    f = field_ref[c : c + 1, cols]
                    outs = [v + q * f for v, q in zip(outs, charge)]
                for o in range(BX):
                    out_ref[c, o, :, cols] = outs[o]
            return 0

        lax.fori_loop(0, NZ // 128, chunk, 0)


def sample_kernel(
    lo_ref, hi_ref, taps_ref, tab_ref, pick_ref, ground_ref, dens_ref, out_ref, flow, fmat, gathered, scale_ref
):
    step = pl.program_id(0)
    last_step = pl.num_programs(0) - 1

    @pl.when(step == 0)
    def _():
        def clear(i, _):
            flow[:, i] = jnp.zeros((3, CY, NZ), jnp.float32)
            flow[:, 12 + CX + i] = jnp.zeros((3, CY, NZ), jnp.float32)
            return 0

        lax.fori_loop(0, 12, clear, 0)
        for i in range(12 + CX + 12, flow.shape[1]):
            flow[:, i] = jnp.zeros((3, CY, NZ), jnp.float32)

    @pl.when(step < last_step)
    def _():
        for c in range(3):
            g = ground_ref[c : c + 1, :]
            for i in range(BX):
                flow[c, 12 + step * BX + i] = dens_ref[c, i] + g

    @pl.when(step == last_step)
    def _():
        taps = [taps_ref[k] for k in range(13)]

        def block(b, _):
            for c in range(3):

                def chunk(j, _, c=c):
                    cols = pl.ds(pl.multiple_of(j * 128, 128), 128)
                    dest = pl.ds(pl.multiple_of(c * NZ + j * 128, 128), 128)
                    outs = x_filtered(lambda i: flow[c, b * BX + i, :, cols], taps, BX)
                    for o in range(BX):
                        hi, lo = hi_lo(outs[o])
                        fmat[b, o * CY : (o + 1) * CY, dest] = hi
                        fmat[b, BP + o * CY : BP + (o + 1) * CY, dest] = lo
                        fmat[b, 2 * BP + o * CY : 2 * BP + (o + 1) * CY, dest] = hi
                    return 0

                lax.fori_loop(0, NZ // 128, chunk, 0)
            return 0

        lax.fori_loop(0, NB, block, 0)
        scale = scale_ref[0]

        def tile(i, _):
            first, last = lo_ref[i], hi_ref[i]

            @pl.when(first > last)
            def _():
                out_ref[i] = jnp.zeros((8, TILE), jnp.float32)

            @pl.when(first <= last)
            def _():
                xt = tab_ref[i]
                cols = columns(xt, pick_ref[...])
                xrep, yrep, zrep = (cols[:, 128 * k : 128 * (k + 1)] for k in (2, 1, 0))
                lane_i = lax.broadcasted_iota(jnp.int32, (TILE, 128), 1)
                lane = lane_i.astype(jnp.float32)
                xpl = (lane_i // CY).astype(jnp.float32)
                ypl = (lane_i % CY).astype(jnp.float32)
                wy = gauss(ypl - yrep) * scale
                gathered[...] = jnp.zeros(gathered.shape, jnp.float32)

                def bucket(b, _):
                    a = jnp.where(xrep == xpl + (b * BX).astype(jnp.float32), wy, 0.0)
                    hi, lo = hi_lo(a)
                    full = jnp.concatenate([hi, hi, lo], axis=1)
                    gathered[...] += jnp.dot(full, fmat[b], preferred_element_type=jnp.float32)
                    return 0

                lax.fori_loop(first, last + 1, bucket, 0)
                sums = [None] * 3
                for q in range(NZ // 128):
                    wz = gauss(lane + (128.0 * q) - zrep) * scale
                    for c in range(3):
                        t = gathered[:, c * NZ + 128 * q : c * NZ + 128 * (q + 1)] * wz
                        sums[c] = t if sums[c] is None else sums[c] + t
                ones = jnp.ones((8, 256), jnp.bfloat16)
                for c in range(3):
                    hi, lo = hi_lo(sums[c])
                    both = jnp.concatenate([hi, lo], axis=1)
                    row = lax.dot_general(
                        ones, both, (((1,), (1,)), ((), ())), preferred_element_type=jnp.float32
                    )
                    out_ref[i, c : c + 1, :] = row[0:1, :]

            return 0

        lax.fori_loop(0, tab_ref.shape[0], tile, 0)


def smem():
    return pl.BlockSpec(memory_space=pltpu.SMEM)


def whole(shape):
    return pl.BlockSpec(shape, lambda i: (0,) * len(shape))


def spread_call(lo, hi, taps, table, pick, field):
    n = table.shape[0]
    steps = CX // BX
    return pl.pallas_call(
        spread_kernel,
        grid=(steps + 1,),
        in_specs=[smem(), smem(), smem(), whole(table.shape), whole(pick.shape), whole(field.shape)],
        out_specs=pl.BlockSpec((4, BX, CY, NZ), lambda i: (0, jnp.maximum(i - 1, 0), 0, 0)),
        out_shape=jax.ShapeDtypeStruct((4, CX, CY, NZ), jnp.float32),
        scratch_shapes=[
            pltpu.VMEM((NB, 4 * BP, NZ), jnp.float32),
            pltpu.VMEM((4 * BP, 3 * TILE), jnp.bfloat16),
            pltpu.VMEM((3 * TILE, NZ), jnp.bfloat16),
        ],
        compiler_params=pltpu.CompilerParams(vmem_limit_bytes=56 << 20),
        name="spread",
    )(lo, hi, taps, table, pick, field)


def sample_call(lo, hi, taps, table, pick, ground, density, scale):
    n = table.shape[0]
    steps = CX // BX
    return pl.pallas_call(
        sample_wrapped,
        grid=(steps + 1,),
        in_specs=[
            smem(),
            smem(),
            smem(),
            whole(table.shape),
            whole(pick.shape),
            whole(ground.shape),
            pl.BlockSpec((3, BX, CY, NZ), lambda i: (0, jnp.minimum(i, steps - 1), 0, 0)),
            smem(),
        ],
        out_specs=whole((n, 8, TILE)),
        out_shape=jax.ShapeDtypeStruct((n, 8, TILE), jnp.float32),
        scratch_shapes=[
            pltpu.VMEM((3, NB * BX + 12, CY, NZ), jnp.float32),
            pltpu.VMEM((NB, 3 * BP, 3 * NZ), jnp.bfloat16),
            pltpu.VMEM((TILE, 3 * NZ), jnp.float32),
        ],
        compiler_params=pltpu.CompilerParams(vmem_limit_bytes=56 << 20),
        name="sample",
    )(lo, hi, taps, table, pick, ground, density, scale)


def sample_wrapped(*refs):
    ins = refs[:8]
    sample_kernel(*ins[:7], *refs[8:], ins[7])


def ring(value, steps):
    count = lax.axis_size("stream")
    return lax.ppermute(value, "stream", [(i, (i + steps) % count) for i in range(count)])


def line(value, steps):
    count = lax.axis_size("span")
    first, last = max(0, -steps), min(count, count - steps)
    return lax.ppermute(value, "span", [(i, i + steps) for i in range(first, last)])


def on_device(records, cells, counts, background, field):
    cap = records.shape[3]
    total = 9 * cap
    tiles = total // TILE
    bf16, f32 = jnp.bfloat16, jnp.float32
    slots = jnp.arange(cap, dtype=jnp.int32)
    live = slots[None, :] < counts[0][:, None]
    cell = cells[0]
    z = cell % NZ
    x = jnp.where(live, cell // (CY * NZ), 255)
    y = (cell // NZ) % CY
    places = jnp.stack([x, y, z // 16, z % 16], axis=1).astype(bf16)
    outgoing = jnp.concatenate([records[0], places], axis=1).reshape(3, 3, 8, cap)
    dead = jnp.zeros((8,), bf16).at[4].set(255)[:, None]
    outgoing = jnp.stack([ring(outgoing[0], -1), outgoing[1], ring(outgoing[2], 1)])
    me = lax.axis_index("span")
    spans = lax.axis_size("span")
    has_low, has_high = me > 0, me < spans - 1
    from_high = jnp.where(has_high, line(outgoing[:, 0], -1), dead)
    from_low = jnp.where(has_low, line(outgoing[:, 2], 1), dead)
    inbound = jnp.stack([from_high, outgoing[:, 1], from_low], axis=1)
    inbound = inbound.transpose(2, 0, 1, 3).reshape(8, total)

    gi = inbound[4:].astype(jnp.int32)
    gx, gy, gz = gi[0], gi[1], gi[2] * 16 + gi[3]
    klass = (gy >= REACH).astype(jnp.int32) + (gy >= CY - REACH)
    klass = jnp.where(gx > 200, 3, klass)
    key = ((klass * 256 + gx) * CY + gy) * NZ + gz
    order = jnp.arange(total, dtype=jnp.int32)
    key, order, *vals = lax.sort((key, order) + tuple(inbound[c].astype(f32) for c in range(4)), num_keys=1)
    sz = key % NZ
    packed = jnp.stack(
        vals
        + [
            v.astype(f32)
            for v in (key // (CY * NZ) % 256, key // NZ % CY, sz // 16, sz % 16)
        ]
    ).astype(bf16)

    low = jnp.where(has_low, line(packed, 1), dead)
    high = jnp.where(has_high, line(packed, -1), dead)
    three = jnp.stack([low, packed, high])
    arrays = jnp.stack([ring(three, 1), three, ring(three, -1)]).astype(f32)
    shift = jnp.arange(-1, 2, dtype=f32)
    ax = arrays[:, :, 4]
    ax = jnp.where(ax > 200, FAR, ax + (CX * shift[:, None, None] + REACH))
    ay = arrays[:, :, 5] + CY * shift[None, :, None]
    table = jnp.concatenate(
        [arrays[:, :, :4], ax[:, :, None], ay[:, :, None], arrays[:, :, 6:], jnp.zeros((3, 3, 8, total), f32)], axis=2
    )
    table = table.reshape(9, ROWS, tiles, TILE).transpose(0, 2, 1, 3).reshape(9 * tiles, ROWS, TILE)
    near = (ax >= 0) & (ax < CX + 2 * REACH) & (ay >= -REACH) & (ay < CY + REACH)
    bucket = (ax.astype(jnp.int32) // BX).reshape(9 * tiles, TILE)
    near = near.reshape(9 * tiles, TILE)
    lo = jnp.min(jnp.where(near, bucket, 99), axis=1)
    hi = jnp.max(jnp.where(near, bucket, -1), axis=1)

    raw = kernel_taps()
    scale = 1.0 / jnp.sum(raw)
    unit = raw * scale
    rows = jnp.arange(ROWS)[:, None]
    lanes = jnp.arange(384)[None, :] // 128
    pick = jnp.where(lanes == 0, jnp.where(rows == 6, 16.0, jnp.where(rows == 7, 1.0, 0.0)), 0.0)
    pick = jnp.where((lanes == 1) & (rows == 5), 1.0, pick)
    pick = jnp.where((lanes == 2) & (rows == 4), 1.0, pick).astype(bf16)

    density = spread_call(lo, hi, raw, table, pick[:, :128], field)
    partial = sample_call(lo, hi, unit, table, pick, background, density, scale[None])
    partial = partial[:, :3].reshape(3, 3, tiles, 3, TILE).transpose(0, 1, 3, 2, 4).reshape(3, 3, 3, total)
    mine = partial[1] + ring(partial[2], 1) + ring(partial[0], -1)
    own = mine[1] + line(mine[2], 1) + line(mine[0], -1)
    _, *vel = lax.sort((order, own[0], own[1], own[2]), num_keys=1)
    velocity = jnp.stack([v.reshape(9, cap) for v in vel], axis=1)[None]
    return density, velocity


def solution(mesh):
    return jax.shard_map(
        on_device,
        mesh=mesh,
        in_specs=(
            P(("stream", "span"), None, None, None),
            P(("stream", "span"), None, None),
            P(("stream", "span"), None),
            P(),
            P(),
        ),
        out_specs=(P(None, "stream", "span", None), P(("stream", "span"), None, None, None)),
        check_vma=False,
    )
```

time: 724 us -> 263 us (0.36)
  the two profiles are of different devices: /device:TPU:0 before, /device:TPU:30 now
where the time goes in v1:
time: 263 us; the launch traced here: 259 us
  Pallas kernels  166 us (63%)
  waiting for transfers between devices  32.8 us (12%)
  starting transfers between devices  25.8 us (10%)
  other arithmetic  21 us (8%)
  local copies, waits for them, and re-layouts  11.5 us (4%)
    pallas_call x1, Pallas kernels, sample_call(): pl.pallas_call(sample_wrapped, grid=(steps + 1,), in_specs=[smem(), smem(...  90 us
    pallas_call x1, Pallas kernels, spread_call(): pl.pallas_call(spread_kernel, grid=(steps + 1,), in_specs=[smem(), smem()...  76.1 us
    ppermute x6, waiting for transfers between devices, ring(): lax.ppermute(value, 'stream', [(i, (i + steps) % count) for i in range(co...  27 us
    ppermute x6, starting transfers between devices, line(): lax.ppermute(value, 'span', [(i, i + steps) for i in range(first, last)])  14.2 us
    ppermute x6, starting transfers between devices, ring(): lax.ppermute(value, 'stream', [(i, (i + steps) % count) for i in range(co...  11.6 us
    sort x1, other arithmetic, on_device(): _, *vel = lax.sort((order, own[0], own[1], own[2]), num_keys=1)  7.64 us
    sort x5, other arithmetic, on_device(): lax.sort((key, order) + tuple((inbound[c].astype(f32) for c in range(4)))...  6.35 us
    ppermute x6, waiting for transfers between devices, line(): lax.ppermute(value, 'span', [(i, i + steps) for i in range(first, last)])  5.75 us
  transfers between devices with their start and end apart: 12, of which 8 were waited for; matrix products, arithmetic and copies ran while one was open for 1% of the time, Pallas kernels for 0%

profile of v1, /device:TPU:30, one launch (start us, length us, event | category | flops | bytes accessed | tf_op | source)
XLA Modules:
  0.0 259.2 jit_solution(521065058571296266)
XLA Ops:
  0.6 0.0 copy-start.2
  0.6 0.8 fusion.19
  1.5 1.1 fusion.21
  2.6 0.9 concatenate.26
  3.5 0.2 collective-permute-start.1
  3.7 1.9 collective-permute-start
  5.6 0.1 select_convert_fusion.refs_4_
  5.7 0.0 copy-start.1
  5.7 1.7 collective-permute-done.1
  7.3 2.9 %collective-permute-done = bf16[3,8,512]{2,1,0:T(8,128)(2,1)S(1)} collective-permute-done((bf16[3,8,512]{2,1,0:T(8,128)(2,1)S(1)}, bf16[3,8,512]{2,1,0:T(8,128)(2,1)S(1)}, u32[]{:S(2)}, u32[]{:S(2)}) %collective-permute-start) | collective-permute-done | bytes 24608 | tf_op jit(solution)/shard_map/ppermute | solution.py:290
  10.2 1.9 collective-permute-start.2
  12.2 2.4 collective-permute-start.3
  14.6 0.1 add.215
  14.7 0.1 add.216
  14.8 0.0 collective-permute-done.2
  14.8 2.5 collective-permute-done.3
  17.3 0.1 select_bitcast_fusion.3
  17.4 0.1 slice_convert_fusion.1
  17.5 0.1 fusion.36
  17.9 6.3 %sort.78 = (s32[4608]{0:T(1024)S(1)}, s32[4608]{0:T(1024)S(1)}, f32[4608]{0:T(1024)S(1)}, f32[4608]{0:T(1024)S(1)}, f32[4608]{0:T(1024)S(1)}, /*index=5*/f32[4608]{0:T(1024)S(1)}) sort(s32[4608]{0:T(1024)S(1)} %multiply_add_fusion, s32[4608]{0:T(1024)S(1)} %iota.58, f32[4608]{0:T(1024)S(1)} %reshape.596, f32[4608]{0:T(1024)S(1)} %reshape.597, ...), dimensions={0}, to_apply=%region_0.1 | sort | flops 59904 | bytes 221184 | tf_op jit(solution)/shard_map/sort | solution.py:328
  24.3 0.1 fusion.14
  24.5 0.2 stack.117
  24.7 1.9 collective-permute-start.4
  26.6 3.6 %collective-permute-start.5 = (bf16[8,4608]{1,0:T(8,128)(2,1)S(1)}, bf16[8,4608]{1,0:T(8,128)(2,1)S(1)}, u32[]{:S(2)}, u32[]{:S(2)}) collective-permute-start(bf16[8,4608]{1,0:T(8,128)(2,1)S(1)} %stack.117), channel_id=1, source_target_pairs={{1,0},{2,1},{3,2},{5,4},{6,5},{7,6},{9,8},{10,9},{11,10},{13,12},{... | collective-permute-start | bytes 221192 | tf_op jit(solution)/shard_map/ppermute | solution.py:296
  30.3 0.1 add.212
  30.4 0.1 add.213
  30.5 0.6 slice.163.pick_ref
  31.1 0.6 fusion.33
  32.6 0.2 stack.127
  32.8 0.0 collective-permute-done.4
  32.8 0.1 select_bitcast_fusion.1
  33.0 0.1 collective-permute-start.7
  33.0 4.7 %collective-permute-start.6 = (bf16[3,8,4608]{2,1,0:T(8,128)(2,1)S(1)}, bf16[3,8,4608]{2,1,0:T(8,128)(2,1)S(1)}, u32[]{:S(2)}, u32[]{:S(2)}) collective-permute-start(bf16[3,8,4608]{2,1,0:T(8,128)(2,1)S(1)} %get-tuple-element.68), channel_id=1, source_target_pairs={{0,4},{4,8},{8,12},{12,16},{16,20},{20,24},{24,28},{28,0},{1,5},{5... | collective-permute-start | bytes 663560 | tf_op jit(solution)/shard_map/ppermute | solution.py:290
  37.7 0.6 fusion.31.taps_ref
  38.3 0.6 broadcast_multiply_fusion.refs_2_
  38.9 3.0 %collective-permute-done.7 = bf16[3,8,4608]{2,1,0:T(8,128)(2,1)S(1)} collective-permute-done((bf16[3,8,4608]{2,1,0:T(8,128)(2,1)S(1)}, bf16[3,8,4608]{2,1,0:T(8,128)(2,1)S(1)}, u32[]{:S(2)}, u32[]{:S(2)}) %collective-permute-start.7) | collective-permute-done | bytes 221216 | tf_op jit(solution)/shard_map/ppermute | solution.py:290
  41.9 2.2 collective-permute-done.6
  44.1 0.5 compare_select_fusion
  44.6 0.1 maximum_convert_fusion
  44.7 0.0 copy-start
  44.8 0.1 maximum_convert_fusion.1
  44.9 1.0 convert_reduce_fusion
  45.9 0.1 squeeze.66
  46.0 0.1 squeeze.65
  46.1 0.8 select_reduce_fusion
  47.0 0.1 broadcast_in_dim.110
  47.1 1.0 slice-done.1
  48.1 5.5 %concatenate.31 = f32[9,16,18,256]{3,1,2,0:T(8,128)} concatenate(f32[9,4,18,256]{3,1,2,0:T(4,128)S(1)} %bitcast.78, f32[9,1,18,256]{3,1,2,0:T(1,128)S(1)} %bitcast.87, f32[9,1,18,256]{3,1,2,0:T(1,128)S(1)} %bitcast.88, f32[9,2,18,256]{3,1,2,0:T(2,128)S(1)} %bitcast.85, f32[9,8,18,256]{3,1,2,0:T(8,128)S(1)} %broadcast_in_dim.110), dimensions={1} | concatenate | bytes 5308416 | tf_op jit(solution)/shard_map/concatenate | solution.py:346
  53.5 76.1 %spread.1.refs_6_ = f32[4,64,16,512]{3,2,1,0:T(8,128)} custom-call(s32[162]{0:T(256)} %get-tuple-element.37.lo_ref.refs_0_, s32[162]{0:T(256)} %get-tuple-element.36.hi_ref.refs_1_, f32[13]{0:T(128)} %fusion.31.taps_ref, f32[162,16,256]{2,1,0:T(8,128)} %bitcast.75, bf16[16,128]{1,0:T(8,128)(2,1)} %slice.163.pick_ref, f32[3,512]{1,0:T(4,128)} %field_ref.1), custom_call_target="tpu_custom_call" | custom-call | tf_op jit(solution)/shard_map/spread/pallas_call | solution.py:239
  129.6 90.0 %sample.1 = f32[162,8,256]{2,1,0:T(8,128)} custom-call(s32[162]{0:T(256)} %get-tuple-element.37.lo_ref.refs_0_, s32[162]{0:T(256)} %get-tuple-element.36.hi_ref.refs_1_, f32[13]{0:T(128)} %broadcast_multiply_fusion.refs_2_, f32[162,16,256]{2,1,0:T(8,128)} %bitcast.76, bf16[16,384]{1,0:T(8,128)(2,1)} %copy-done.1, f32[3,512]{1,0:T(4,128)} %refs_5_.1, ...), custom_call_target="tpu_custom_call" | custom-call | tf_op jit(solution)/shard_map/sample/pallas_call | solution.py:258
  219.7 1.0 slice-done
  220.7 0.1 fusion.35
  220.8 0.1 collective-permute-start.9
  220.9 4.7 %collective-permute-start.8 = (f32[3,3,4608]{2,1,0:T(4,128)S(1)}, f32[3,3,4608]{2,1,0:T(4,128)S(1)}, u32[]{:S(2)}, u32[]{:S(2)}) collective-permute-start(f32[3,3,4608]{2,1,0:T(4,128)S(1)} %bitcast.89), channel_id=1, source_target_pairs={{0,4},{4,8},{8,12},{12,16},{16,20},{20,24},{24,28},{28,0},{1,5},{5... | collective-permute-start | bytes 497672 | tf_op jit(solution)/shard_map/ppermute | solution.py:290
  225.6 3.9 %collective-permute-done.9 = f32[3,3,4608]{2,1,0:T(4,128)S(1)} collective-permute-done((f32[3,3,4608]{2,1,0:T(4,128)S(1)}, f32[3,3,4608]{2,1,0:T(4,128)S(1)}, u32[]{:S(2)}, u32[]{:S(2)}) %collective-permute-start.9) | collective-permute-done | bytes 165920 | tf_op jit(solution)/shard_map/ppermute | solution.py:290
  229.5 13.4 %collective-permute-done.8 = f32[3,3,4608]{2,1,0:T(4,128)S(1)} collective-permute-done((f32[3,3,4608]{2,1,0:T(4,128)S(1)}, f32[3,3,4608]{2,1,0:T(4,128)S(1)}, u32[]{:S(2)}, u32[]{:S(2)}) %collective-permute-start.8) | collective-permute-done | bytes 165920 | tf_op jit(solution)/shard_map/ppermute | solution.py:290
  242.9 0.1 add_add_fusion
  243.0 1.9 collective-permute-start.11
  244.9 2.4 collective-permute-start.10
  247.4 3.2 %collective-permute-done.10 = f32[3,4608]{1,0:T(4,128)S(1)} collective-permute-done((f32[3,4608]{1,0:T(4,128)S(1)}, f32[3,4608]{1,0:T(4,128)S(1)}, u32[]{:S(2)}, u32[]{:S(2)}) %collective-permute-start.10) | collective-permute-done | bytes 55328 | tf_op jit(solution)/shard_map/ppermute | solution.py:296
  250.6 0.1 slice_reduce_fusion
  250.8 7.6 %sort.79 = (s32[4608]{0:T(1024)}, f32[4608]{0:T(1024)S(1)}, f32[4608]{0:T(1024)S(1)}, f32[4608]{0:T(1024)S(1)}, s32[4608]{0:T(1024)}) sort(s32[4608]{0:T(1024)S(1)} %get-tuple-element.32, f32[4608]{0:T(1024)S(1)} %get-tuple-element.40, f32[4608]{0:T(1024)S(1)} %get-tuple-element.39, f32[4608]{0:T(1024)S(1)} %get-tuple-element.38, s32[4608]{0:T(1024)S(1)} %iota.65), dimensions={0}, to_apply=%region_4.5 | sort | flops 59904 | bytes 184320 | tf_op jit(solution)/shard_map/sort | solution.py:370
  258.5 0.1 pad_maximum_fusion.4
  258.6 0.7 broadcast_in_dim.119
  (61 shorter events, 0.7 us)
Async XLA Ops:
  0.6 16.7 %copy-start.2 = (bf16[8]{0:T(256)(128)(2,1)S(1)}, bf16[8]{0:T(256)(128)(2,1)}, u32[]{:S(2)}) copy-start(bf16[8]{0:T(256)(128)(2,1)} %constant.218.clone.1) | copy-start | bytes 52
  3.5 3.9 %collective-permute-start.1 = (bf16[3,8,512]{2,1,0:T(8,128)(2,1)S(1)}, bf16[3,8,512]{2,1,0:T(8,128)(2,1)S(1)}, u32[]{:S(2)}, u32[]{:S(2)}) collective-permute-start(bf16[3,8,512]{2,1,0:T(8,128)(2,1)S(1)} %get-tuple-element.80), channel_id=1, source_target_pairs={{0,4},{4,8},{8,12},{12,16},{16,20},{20,24},{24,28},{28,0},{1,5},{5... | collective-permute-start | bytes 73736 | tf_op jit(solution)/shard_map/ppermute | solution.py:290
  3.7 6.5 %collective-permute-start = (bf16[3,8,512]{2,1,0:T(8,128)(2,1)S(1)}, bf16[3,8,512]{2,1,0:T(8,128)(2,1)S(1)}, u32[]{:S(2)}, u32[]{:S(2)}) collective-permute-start(bf16[3,8,512]{2,1,0:T(8,128)(2,1)S(1)} %get-tuple-element.79), channel_id=1, source_target_pairs={{0,28},{4,0},{8,4},{12,8},{16,12},{20,16},{24,20},{28,24},{1,29},{... | collective-permute-start | bytes 73736 | tf_op jit(solution)/shard_map/ppermute | solution.py:290
  5.7 24.8 %copy-start.1 = (bf16[16,384]{1,0:T(8,128)(2,1)}, bf16[16,384]{1,0:T(8,128)(2,1)S(1)}, u32[]{:S(2)}) copy-start(bf16[16,384]{1,0:T(8,128)(2,1)S(1)} %select_convert_fusion.refs_4_) | copy-start | bytes 36868
  10.2 4.6 %collective-permute-start.2 = (bf16[3,8,512]{2,1,0:T(8,128)(2,1)S(1)}, bf16[3,8,512]{2,1,0:T(8,128)(2,1)S(1)}, u32[]{:S(2)}, u32[]{:S(2)}) collective-permute-start(bf16[3,8,512]{2,1,0:T(8,128)(2,1)S(1)} %get-tuple-element.76), channel_id=1, source_target_pairs={{1,0},{2,1},{3,2},{5,4},{6,5},{7,6},{9,8},{10,9},{11,10},{13,12},{... | collective-permute-start | bytes 73736 | tf_op jit(solution)/shard_map/ppermute | solution.py:296
  12.2 5.1 %collective-permute-start.3 = (bf16[3,8,512]{2,1,0:T(8,128)(2,1)S(1)}, bf16[3,8,512]{2,1,0:T(8,128)(2,1)S(1)}, u32[]{:S(2)}, u32[]{:S(2)}) collective-permute-start(bf16[3,8,512]{2,1,0:T(8,128)(2,1)S(1)} %get-tuple-element.77), channel_id=1, source_target_pairs={{0,1},{1,2},{2,3},{4,5},{5,6},{6,7},{8,9},{9,10},{10,11},{12,13},{... | collective-permute-start | bytes 73736 | tf_op jit(solution)/shard_map/ppermute | solution.py:296
  24.7 8.1 %collective-permute-start.4 = (bf16[8,4608]{1,0:T(8,128)(2,1)S(1)}, bf16[8,4608]{1,0:T(8,128)(2,1)S(1)}, u32[]{:S(2)}, u32[]{:S(2)}) collective-permute-start(bf16[8,4608]{1,0:T(8,128)(2,1)S(1)} %stack.117), channel_id=1, source_target_pairs={{0,1},{1,2},{2,3},{4,5},{5,6},{6,7},{8,9},{9,10},{10,11},{12,13},{... | collective-permute-start | bytes 221192 | tf_op jit(solution)/shard_map/ppermute | solution.py:296
  26.6 6.2 %collective-permute-start.5 = (bf16[8,4608]{1,0:T(8,128)(2,1)S(1)}, bf16[8,4608]{1,0:T(8,128)(2,1)S(1)}, u32[]{:S(2)}, u32[]{:S(2)}) collective-permute-start(bf16[8,4608]{1,0:T(8,128)(2,1)S(1)} %stack.117), channel_id=1, source_target_pairs={{1,0},{2,1},{3,2},{5,4},{6,5},{7,6},{9,8},{10,9},{11,10},{13,12},{... | collective-permute-start | bytes 221192 | tf_op jit(solution)/shard_map/ppermute | solution.py:296
  33.0 9.0 %collective-permute-start.7 = (bf16[3,8,4608]{2,1,0:T(8,128)(2,1)S(1)}, bf16[3,8,4608]{2,1,0:T(8,128)(2,1)S(1)}, u32[]{:S(2)}, u32[]{:S(2)}) collective-permute-start(bf16[3,8,4608]{2,1,0:T(8,128)(2,1)S(1)} %get-tuple-element.68), channel_id=1, source_target_pairs={{0,28},{4,0},{8,4},{12,8},{16,12},{20,16},{24,20},{28,24},{1,29},{... | collective-permute-start | bytes 663560 | tf_op jit(solution)/shard_map/ppermute | solution.py:290
  33.0 11.1 %collective-permute-start.6 = (bf16[3,8,4608]{2,1,0:T(8,128)(2,1)S(1)}, bf16[3,8,4608]{2,1,0:T(8,128)(2,1)S(1)}, u32[]{:S(2)}, u32[]{:S(2)}) collective-permute-start(bf16[3,8,4608]{2,1,0:T(8,128)(2,1)S(1)} %get-tuple-element.68), channel_id=1, source_target_pairs={{0,4},{4,8},{8,12},{12,16},{16,20},{20,24},{24,28},{28,0},{1,5},{5... | collective-permute-start | bytes 663560 | tf_op jit(solution)/shard_map/ppermute | solution.py:290
  44.7 1.4 copy-start
  47.0 1.1 slice-start.1
  219.6 1.0 slice-start
  220.8 8.7 %collective-permute-start.9 = (f32[3,3,4608]{2,1,0:T(4,128)S(1)}, f32[3,3,4608]{2,1,0:T(4,128)S(1)}, u32[]{:S(2)}, u32[]{:S(2)}) collective-permute-start(f32[3,3,4608]{2,1,0:T(4,128)S(1)} %bitcast.90), channel_id=1, source_target_pairs={{0,28},{4,0},{8,4},{12,8},{16,12},{20,16},{24,20},{28,24},{1,29},{... | collective-permute-start | bytes 497672 | tf_op jit(solution)/shard_map/ppermute | solution.py:290
  220.9 22.0 %collective-permute-start.8 = (f32[3,3,4608]{2,1,0:T(4,128)S(1)}, f32[3,3,4608]{2,1,0:T(4,128)S(1)}, u32[]{:S(2)}, u32[]{:S(2)}) collective-permute-start(f32[3,3,4608]{2,1,0:T(4,128)S(1)} %bitcast.89), channel_id=1, source_target_pairs={{0,4},{4,8},{8,12},{12,16},{16,20},{20,24},{24,28},{28,0},{1,5},{5... | collective-permute-start | bytes 497672 | tf_op jit(solution)/shard_map/ppermute | solution.py:290
  243.0 4.3 %collective-permute-start.11 = (f32[3,4608]{1,0:T(4,128)S(1)}, f32[3,4608]{1,0:T(4,128)S(1)}, u32[]{:S(2)}, u32[]{:S(2)}) collective-permute-start(f32[3,4608]{1,0:T(4,128)S(1)} %get-tuple-element.66), channel_id=1, source_target_pairs={{1,0},{2,1},{3,2},{5,4},{6,5},{7,6},{9,8},{10,9},{11,10},{13,12},{... | collective-permute-start | bytes 165896 | tf_op jit(solution)/shard_map/ppermute | solution.py:296
  244.9 5.7 %collective-permute-start.10 = (f32[3,4608]{1,0:T(4,128)S(1)}, f32[3,4608]{1,0:T(4,128)S(1)}, u32[]{:S(2)}, u32[]{:S(2)}) collective-permute-start(f32[3,4608]{1,0:T(4,128)S(1)} %get-tuple-element.65), channel_id=1, source_target_pairs={{0,1},{1,2},{2,3},{4,5},{5,6},{6,7},{8,9},{9,10},{10,11},{12,13},{... | collective-permute-start | bytes 165896 | tf_op jit(solution)/shard_map/ppermute | solution.py:296

commit v2 on v1

v2 whole, which is shorter than its diff:
```python
import functools

import jax
import jax.numpy as jnp
from jax import lax
from jax.experimental import pallas as pl
from jax.experimental.pallas import tpu as pltpu
from jax.sharding import PartitionSpec as P

CX = 64
CY = 16
NZ = 512
REACH = 6
TILE = 128
BX = 8
XO = 8
XROWS = 84
BP = BX * CY

spread_width = 12.5


def kernel_taps():
    offsets = jnp.arange(-6, 7).astype(jnp.float32)
    return jnp.exp(-offsets * offsets / spread_width)


def gauss(d):
    return jnp.where(jnp.abs(d) < REACH + 0.5, jnp.exp(d * d * (-1.0 / spread_width)), 0.0)


def hi_lo(v):
    hi = v.astype(jnp.bfloat16)
    lo = (v - hi.astype(jnp.float32)).astype(jnp.bfloat16)
    return hi, lo


def columns(xt, pick):
    return lax.dot_general(
        xt.astype(jnp.bfloat16), pick, (((0,), (0,)), ((), ())), preferred_element_type=jnp.float32
    )


def x_filtered(load, taps, count):
    outs = []
    ins = [load(i) for i in range(count + 12)]
    for o in range(count):
        total = taps[6] * ins[o + 6]
        for k in range(1, 7):
            total = total + taps[6 + k] * (ins[o + 6 - k] + ins[o + 6 + k])
        outs.append(total)
    return outs


def tile_codes(list_ref, tab_ref, k):
    code = list_ref[k + 1]
    i = code >> 14
    per = list_ref[0]
    n = jnp.where(per == 0, 4, lax.div(i, jnp.maximum(per, 1)))
    return i, n, (code >> 7) & 127, code & 127


def framed(tab_ref, i, n):
    xt = tab_ref[i].astype(jnp.float32)
    row, col = lax.div(n, 3), lax.rem(n, 3)
    sx = ((row - 1) * CX + REACH).astype(jnp.float32)
    sy = ((col - 1) * CY).astype(jnp.float32)
    return xt, sx, sy


def accumulate(count_ref, list_ref, tab_ref, pick_ref, acc, amat, zmat):
    def tile(k, _):
        i, n, first, last = tile_codes(list_ref, tab_ref, k)
        xt, sx, sy = framed(tab_ref, i, n)
        zrep = columns(xt, pick_ref[...])
        lane = lax.broadcasted_iota(jnp.int32, (TILE, 128), 1).astype(jnp.float32)
        for q in range(NZ // 128):
            hit = jnp.where(lane + (128.0 * q) == zrep, 1.0, 0.0).astype(jnp.bfloat16)
            cols = slice(128 * q, 128 * (q + 1))
            zmat[0:TILE, cols] = hit
            zmat[TILE : 2 * TILE, cols] = hit
        ypl = lax.broadcasted_iota(jnp.int32, (CY, TILE), 0).astype(jnp.float32)
        gy = gauss(ypl - (xt[5:6, :] + sy))
        xrow = xt[4:5, :] + sx
        parts = [hi_lo(gy * xt[c : c + 1, :]) for c in range(4)]

        def window(w, _):
            x0 = first + w * BX
            for xx in range(BX):
                at = (x0 + xx).astype(jnp.float32)
                m = jnp.where(xrow == at, 1.0, 0.0)
                m = jnp.broadcast_to(m, (CY, TILE)).astype(jnp.bfloat16)
                for c in range(4):
                    rows = slice((xx * 4 + c) * CY, (xx * 4 + c + 1) * CY)
                    amat[rows, 0:TILE] = parts[c][0] * m
                    amat[rows, TILE : 2 * TILE] = parts[c][1] * m
            part = jnp.dot(amat[...], zmat[...], preferred_element_type=jnp.float32)
            acc[pl.ds(x0, BX)] += part.reshape(BX, 4 * CY, NZ)
            return 0

        lax.fori_loop(0, (last - first) // BX + 1, window, 0)
        return 0

    lax.fori_loop(0, count_ref[0], tile, 0)


def spread_own_kernel(count_ref, list_ref, tab_ref, pick_ref, out_ref, acc, amat, zmat, sem):
    def clear(i, _):
        acc[i] = jnp.zeros(acc.shape[1:], jnp.float32)
        return 0

    lax.fori_loop(0, XROWS, clear, 0)
    accumulate(count_ref, list_ref, tab_ref, pick_ref, acc, amat, zmat)
    copy = pltpu.make_async_copy(acc, out_ref, sem)
    copy.start()
    copy.wait()


def spread_kernel(
    count_ref, list_ref, taps_ref, tab_ref, pick_ref, field_ref, band_ref, old_ref, out_ref, acc, amat, zmat, wide, sem
):
    step = pl.program_id(0)

    @pl.when(step == 0)
    def _():
        copy = pltpu.make_async_copy(old_ref, acc, sem)
        copy.start()
        copy.wait()
        accumulate(count_ref, list_ref, tab_ref, pick_ref, acc, amat, zmat)

    @pl.when(step > 0)
    def _():
        base = (step - 1) * XO
        taps = [taps_ref[k] for k in range(13)]

        def chunk(j, _):
            cols = pl.ds(pl.multiple_of(j * 128, 128), 128)
            for c in range(4):
                outs = x_filtered(lambda i: acc[base + i, c * CY : (c + 1) * CY, cols], taps, XO)
                for o in range(XO):
                    hi, lo = hi_lo(outs[o])
                    rows = slice((c * XO + o) * CY, (c * XO + o + 1) * CY)
                    wide[0, rows, cols] = hi
                    wide[1, rows, cols] = lo
            return 0

        lax.fori_loop(0, NZ // 128, chunk, 0)
        hi, lo = wide[0], wide[1]
        full = jnp.concatenate([hi, hi, lo], axis=1)
        dens = jnp.dot(full, band_ref[...], preferred_element_type=jnp.float32)
        dens = dens.reshape(4, XO, CY, NZ)
        out_ref[3] = dens[3]
        for c in range(3):
            out_ref[c] = dens[c] + dens[3] * field_ref[c : c + 1, :][None]


def sampled(count_ref, list_ref, scale_ref, tab_ref, pick_ref, fmat, out_ref, gathered):
    scale = scale_ref[0]
    out_ref[...] = jnp.zeros(out_ref.shape, jnp.float32)

    def tile(k, _):
        i, n, first, last = tile_codes(list_ref, tab_ref, k)
        xt, sx, sy = framed(tab_ref, i, n)
        cols = columns(xt, pick_ref[...])
        xrep, yrep, zrep = (cols[:, 128 * k : 128 * (k + 1)] for k in (2, 1, 0))
        lane_i = lax.broadcasted_iota(jnp.int32, (TILE, 128), 1)
        lane = lane_i.astype(jnp.float32)
        xpl = (lane_i // CY).astype(jnp.float32)
        ypl = (lane_i % CY).astype(jnp.float32)
        wy = gauss(ypl - (yrep + sy)) * scale
        xoff = xrep - xpl

        def part(w):
            x0 = first + w * BX
            a = jnp.where(xoff == x0.astype(jnp.float32) - sx, wy, 0.0)
            full = jnp.concatenate(hi_lo(a), axis=1)
            f = fmat[pl.ds(x0, BX)].reshape(BP, 3 * NZ)
            return jnp.dot(full, jnp.concatenate([f, f], axis=0), preferred_element_type=jnp.float32)

        gathered[...] = part(jnp.int32(0))

        def window(w, _):
            gathered[...] += part(w)
            return 0

        lax.fori_loop(1, (last - first) // BX + 1, window, 0)
        sums = [None] * 3
        for q in range(NZ // 128):
            wz = gauss(lane + (128.0 * q) - zrep) * scale
            for c in range(3):
                t = gathered[:, c * NZ + 128 * q : c * NZ + 128 * (q + 1)] * wz
                sums[c] = t if sums[c] is None else sums[c] + t
        ones = jnp.ones((8, 256), jnp.bfloat16)
        for c in range(3):
            both = jnp.concatenate(hi_lo(sums[c]), axis=1)
            row = lax.dot_general(ones, both, (((1,), (1,)), ((), ())), preferred_element_type=jnp.float32)
            out_ref[i, c : c + 1, :] = row[0:1, :]
        return 0

    lax.fori_loop(0, count_ref[0], tile, 0)


def sample_kernel(
    count_ref,
    list_ref,
    taps_ref,
    scale_ref,
    tab_ref,
    pick_ref,
    ground_ref,
    dens_ref,
    out_ref,
    fmat,
    flow,
    gathered,
):
    step = pl.program_id(0)
    last_step = pl.num_programs(0) - 1

    @pl.when(step == 0)
    def _():
        def clear(i, _):
            flow[:, i] = jnp.zeros((3, CY, NZ), jnp.float32)
            flow[:, 12 + CX + i] = jnp.zeros((3, CY, NZ), jnp.float32)
            return 0

        lax.fori_loop(0, 12, clear, 0)
        for i in range(12 + CX + 12, flow.shape[1]):
            flow[:, i] = jnp.zeros((3, CY, NZ), jnp.float32)

    @pl.when(step < last_step)
    def _():
        for c in range(3):
            g = ground_ref[c : c + 1, :]
            for i in range(XO):
                flow[c, 12 + step * XO + i] = dens_ref[c, i] + g

    @pl.when(step == last_step)
    def _():
        taps = [taps_ref[k] for k in range(13)]

        def block(b, _):
            for c in range(3):

                def chunk(j, _, c=c):
                    cols = pl.ds(pl.multiple_of(j * 128, 128), 128)
                    dest = pl.ds(pl.multiple_of(c * NZ + j * 128, 128), 128)
                    outs = x_filtered(lambda i: flow[c, b * 4 + i, :, cols], taps, 4)
                    for o in range(4):
                        fmat[b * 4 + o, :, dest] = outs[o].astype(jnp.bfloat16)
                    return 0

                lax.fori_loop(0, NZ // 128, chunk, 0)
            return 0

        lax.fori_loop(0, XROWS // 4, block, 0)
        sampled(count_ref, list_ref, scale_ref, tab_ref, pick_ref, fmat, out_ref, gathered)


def sample_own_kernel(count_ref, list_ref, scale_ref, tab_ref, pick_ref, fmat, out_ref, gathered):
    sampled(count_ref, list_ref, scale_ref, tab_ref, pick_ref, fmat, out_ref, gathered)


def smem():
    return pl.BlockSpec(memory_space=pltpu.SMEM)


def whole(shape):
    return pl.BlockSpec(shape, lambda i: (0,) * len(shape))


PARAMS = pltpu.CompilerParams(vmem_limit_bytes=56 << 20)


def spread_own_call(listing, table, pick):
    acc = (XROWS, 4 * CY, NZ)
    return pl.pallas_call(
        spread_own_kernel,
        grid=(1,),
        in_specs=[smem(), smem(), whole(table.shape), whole(pick.shape)],
        out_specs=pl.BlockSpec(memory_space=pl.ANY),
        out_shape=jax.ShapeDtypeStruct(acc, jnp.float32),
        scratch_shapes=[
            pltpu.VMEM(acc, jnp.float32),
            pltpu.VMEM((4 * BP, 2 * TILE), jnp.bfloat16),
            pltpu.VMEM((2 * TILE, NZ), jnp.bfloat16),
            pltpu.SemaphoreType.DMA,
        ],
        compiler_params=PARAMS,
        cost_estimate=pl.CostEstimate(flops=10**10, transcendentals=0, bytes_accessed=3 * 10**7),
        name="spread_own",
    )(*listing, table, pick)


def spread_call(listing, taps, table, pick, field, band, old):
    steps = CX // XO
    return pl.pallas_call(
        spread_kernel,
        grid=(steps + 1,),
        in_specs=[smem(), smem(), smem(), whole(table.shape), whole(pick.shape), whole(field.shape), whole(band.shape)]
        + [pl.BlockSpec(memory_space=pl.ANY)],
        out_specs=pl.BlockSpec((4, XO, CY, NZ), lambda i: (0, jnp.maximum(i - 1, 0), 0, 0)),
        out_shape=jax.ShapeDtypeStruct((4, CX, CY, NZ), jnp.float32),
        scratch_shapes=[
            pltpu.VMEM(old.shape, jnp.float32),
            pltpu.VMEM((4 * BP, 2 * TILE), jnp.bfloat16),
            pltpu.VMEM((2 * TILE, NZ), jnp.bfloat16),
            pltpu.VMEM((2, 4 * XO * CY, NZ), jnp.bfloat16),
            pltpu.SemaphoreType.DMA,
        ],
        compiler_params=PARAMS,
        cost_estimate=pl.CostEstimate(flops=2 * 10**10, transcendentals=0, bytes_accessed=3 * 10**7),
        name="spread_rest",
    )(*listing, taps, table, pick, field, band, old)


def sample_call(listing, taps, scale, table, pick, ground, density):
    n = table.shape[0]
    steps = CX // XO
    fshape = (XROWS, CY, 3 * NZ)
    return pl.pallas_call(
        sample_kernel,
        grid=(steps + 1,),
        in_specs=[
            smem(),
            smem(),
            smem(),
            smem(),
            whole(table.shape),
            whole(pick.shape),
            whole(ground.shape),
            pl.BlockSpec((3, XO, CY, NZ), lambda i: (0, jnp.minimum(i, steps - 1), 0, 0)),
        ],
        out_specs=[whole((n, 8, TILE)), whole(fshape)],
        out_shape=[jax.ShapeDtypeStruct((n, 8, TILE), jnp.float32), jax.ShapeDtypeStruct(fshape, jnp.bfloat16)],
        scratch_shapes=[
            pltpu.VMEM((3, XROWS + 12, CY, NZ), jnp.float32),
            pltpu.VMEM((TILE, 3 * NZ), jnp.float32),
        ],
        compiler_params=PARAMS,
        cost_estimate=pl.CostEstimate(flops=2 * 10**10, transcendentals=0, bytes_accessed=3 * 10**7),
        name="sample_rest",
    )(*listing, taps, scale, table, pick, ground, density)


def sample_own_call(listing, scale, table, pick, fmat):
    n = table.shape[0]
    return pl.pallas_call(
        sample_own_kernel,
        grid=(1,),
        in_specs=[smem(), smem(), smem(), whole(table.shape), whole(pick.shape), whole(fmat.shape)],
        out_specs=whole((n, 8, TILE)),
        out_shape=jax.ShapeDtypeStruct((n, 8, TILE), jnp.float32),
        scratch_shapes=[pltpu.VMEM((TILE, 3 * NZ), jnp.float32)],
        compiler_params=PARAMS,
        cost_estimate=pl.CostEstimate(flops=10**10, transcendentals=0, bytes_accessed=3 * 10**7),
        name="sample_own",
    )(*listing, scale, table, pick, fmat)


def listed(x, y, exists, sx, sy, per):
    ax, ay = x + sx, y + sy
    near = (ax >= 0) & (ax < CX + 2 * REACH) & (ay >= -REACH) & (ay < CY + REACH) & exists
    lo = jnp.min(jnp.where(near, ax, 127), axis=-1).reshape(-1)
    hi = jnp.max(jnp.where(near, ax, -1), axis=-1).reshape(-1)
    active = hi >= 0
    at = jnp.arange(lo.shape[0], dtype=jnp.int32)
    pos = jnp.sum((at[None, :] < at[:, None]) & active[None, :], axis=1, dtype=jnp.int32)
    code = ((at * 128) + lo) * 128 + hi
    rows = jnp.sum(jnp.where((pos[None, :] == at[:, None]) & active[None, :], code[None, :], 0), axis=1)
    count = jnp.sum(active, dtype=jnp.int32)
    return count[None], jnp.concatenate([jnp.array([per], jnp.int32), rows])


def ring(value, steps):
    count = lax.axis_size("stream")
    return lax.ppermute(value, "stream", [(i, (i + steps) % count) for i in range(count)])


def line(value, steps):
    count = lax.axis_size("span")
    first, last = max(0, -steps), min(count, count - steps)
    return lax.ppermute(value, "span", [(i, i + steps) for i in range(first, last)])


def on_device(records, cells, counts, background, field):
    cap = records.shape[3]
    total = 9 * cap
    tiles = total // TILE
    bf16, f32 = jnp.bfloat16, jnp.float32
    slots = jnp.arange(cap, dtype=jnp.int32)
    live = slots[None, :] < counts[0][:, None]
    cell = cells[0]
    z = cell % NZ
    x = jnp.where(live, cell // (CY * NZ), 255)
    y = (cell // NZ) % CY
    places = jnp.stack([x, y, z // 16, z % 16], axis=1).astype(bf16)
    outgoing = jnp.concatenate([records[0], places], axis=1).reshape(3, 3, 8, cap)
    dead = jnp.zeros((8,), bf16).at[4].set(255)[:, None]
    outgoing = jnp.stack([ring(outgoing[0], -1), outgoing[1], ring(outgoing[2], 1)])
    me = lax.axis_index("span")
    spans = lax.axis_size("span")
    has_low, has_high = me > 0, me < spans - 1
    from_high = jnp.where(has_high, line(outgoing[:, 0], -1), dead)
    from_low = jnp.where(has_low, line(outgoing[:, 2], 1), dead)
    inbound = jnp.stack([from_high, outgoing[:, 1], from_low], axis=1)
    inbound = inbound.transpose(2, 0, 1, 3).reshape(8, total)

    gi = inbound[4:].astype(jnp.int32)
    gx, gy, gz = gi[0], gi[1], gi[2] * 16 + gi[3]
    klass = (gy >= REACH).astype(jnp.int32) + (gy >= CY - REACH)
    klass = jnp.where(gx > 200, 3, klass)
    kx = jnp.where(klass == 1, CX - 1 - gx, gx)
    key = ((klass * 256 + kx) * CY + gy) * NZ + gz
    order = jnp.arange(total, dtype=jnp.int32)
    key, order, *vals = lax.sort((key, order) + tuple(inbound[c].astype(f32) for c in range(4)), num_keys=1)
    sz = key % NZ
    sy = key // NZ % CY
    sx = key // (CY * NZ) % 256
    sx = jnp.where(key // (CY * NZ * 256) == 1, CX - 1 - sx, sx)
    packed = jnp.stack(vals + [v.astype(f32) for v in (sx, sy, sz // 16, sz % 16)]).astype(bf16)
    packed = packed.reshape(8, tiles, TILE).transpose(1, 0, 2)

    low = line(packed, 1)
    high = line(packed, -1)
    three = jnp.stack([low, packed, high])
    arrays = jnp.stack([ring(three, 1), three, ring(three, -1)])
    own_list = listed(
        sx.reshape(tiles, TILE), sy.reshape(tiles, TILE), sx.reshape(tiles, TILE) < 200, REACH, 0, 0
    )
    places = arrays[:, :, :, 4:6].astype(jnp.int32)
    shift = jnp.arange(-1, 2, dtype=jnp.int32)
    exists = jnp.stack([has_low, jnp.array(True), has_high])
    exists = exists[None, :] & ~((shift[:, None] == 0) & (shift[None, :] == 0))
    rest_list = listed(
        places[:, :, :, 0],
        places[:, :, :, 1],
        exists[:, :, None, None],
        CX * shift[:, None, None, None] + REACH,
        CY * shift[None, :, None, None],
        tiles,
    )
    table = arrays.reshape(9 * tiles, 8, TILE)

    raw = kernel_taps()
    scale = 1.0 / jnp.sum(raw)
    unit = raw * scale
    rows = jnp.arange(8)[:, None]
    lanes = jnp.arange(384)[None, :] // 128
    pick = jnp.where(lanes == 0, jnp.where(rows == 6, 16.0, jnp.where(rows == 7, 1.0, 0.0)), 0.0)
    pick = jnp.where((lanes == 1) & (rows == 5), 1.0, pick)
    pick = jnp.where((lanes == 2) & (rows == 4), 1.0, pick).astype(bf16)

    zs = jnp.arange(NZ)
    exact = gauss((zs[:, None] - zs[None, :]).astype(f32))
    coarse = lax.reduce_precision(exact, 8, 7)
    band = jnp.concatenate([coarse, exact - coarse, coarse], axis=0).astype(bf16)

    half = spread_own_call(own_list, packed, pick[:, :128])
    density = spread_call(rest_list, raw, table, pick[:, :128], field, band, half)
    partial, fmat = sample_call(rest_list, unit, scale[None], table, pick, background, density)
    mine = sample_own_call(own_list, scale[None], packed, pick, fmat)[:, :3]
    partial = partial[:, :3].reshape(3, 3, tiles, 3, TILE)
    mixed = partial[1] + ring(partial[2], 1) + ring(partial[0], -1)
    own = mixed[1] + mine + line(mixed[2], 1) + line(mixed[0], -1)
    own = own.transpose(1, 0, 2).reshape(3, total)
    _, *vel = lax.sort((order, own[0], own[1], own[2]), num_keys=1)
    velocity = jnp.stack([v.reshape(9, cap) for v in vel], axis=1)[None]
    return density, velocity


def solution(mesh):
    return jax.shard_map(
        on_device,
        mesh=mesh,
        in_specs=(
            P(("stream", "span"), None, None, None),
            P(("stream", "span"), None, None),
            P(("stream", "span"), None),
            P(),
            P(),
        ),
        out_specs=(P(None, "stream", "span", None), P(("stream", "span"), None, None, None)),
        check_vma=False,
    )
```

time: 263 us -> 199 us (0.76)
  the two profiles are of different devices: /device:TPU:30 before, /device:TPU:1 now
where the time goes in v2:
time: 199 us; the launch traced here: 196 us
  Pallas kernels  125 us (63%)
  starting transfers between devices  32.2 us (16%)
  other arithmetic  25.4 us (13%)
  waiting for transfers between devices  6.91 us (3%)
  local copies, waits for them, and re-layouts  4.72 us (2%)
    pallas_call x1, Pallas kernels, sample_call(): pl.pallas_call(sample_kernel, grid=(steps + 1,), in_specs=[smem(), smem()...  39.6 us
    pallas_call x1, Pallas kernels, spread_call(): pl.pallas_call(spread_kernel, grid=(steps + 1,), in_specs=[smem(), smem()...  39.4 us
    pallas_call x1, Pallas kernels, sample_own_call(): pl.pallas_call(sample_own_kernel, grid=(1,), in_specs=[smem(), smem(), sm...  23.4 us
    pallas_call x1, Pallas kernels, spread_own_call(): pl.pallas_call(spread_own_kernel, grid=(1,), in_specs=[smem(), smem(), wh...  22.6 us
    ppermute x6, starting transfers between devices, line(): lax.ppermute(value, 'span', [(i, i + steps) for i in range(first, last)])  18.7 us
    ppermute x6, starting transfers between devices, ring(): lax.ppermute(value, 'stream', [(i, (i + steps) % count) for i in range(co...  13.6 us
    sort x1, other arithmetic, on_device(): _, *vel = lax.sort((order, own[0], own[1], own[2]), num_keys=1)  7.64 us
    sort x5, other arithmetic, on_device(): lax.sort((key, order) + tuple((inbound[c].astype(f32) for c in range(4)))...  6.36 us
  transfers between devices with their start and end apart: 12, of which 3 were waited for; matrix products, arithmetic and copies ran while one was open for 3% of the time, Pallas kernels for 23%

profile of v2, /device:TPU:1, one launch (start us, length us, event | category | flops | bytes accessed | tf_op | source)
XLA Modules:
  0.0 196.2 jit_solution(12512293721299085189)
XLA Ops:
  0.6 0.0 copy-start.3
  0.6 0.8 fusion.35
  1.5 1.1 fusion.37
  2.6 0.9 concatenate.18
  3.5 5.2 %collective-permute-start = (bf16[3,8,512]{2,1,0:T(8,128)(2,1)S(1)}, bf16[3,8,512]{2,1,0:T(8,128)(2,1)S(1)}, u32[]{:S(2)}, u32[]{:S(2)}) collective-permute-start(bf16[3,8,512]{2,1,0:T(8,128)(2,1)S(1)} %get-tuple-element.83), channel_id=1, source_target_pairs={{0,28},{4,0},{8,4},{12,8},{16,12},{20,16},{24,20},{28,24},{1,29},{... | collective-permute-start | bytes 73736 | tf_op jit(solution)/shard_map/ppermute | solution.py:377
  8.6 0.0 collective-permute-start.1
  8.7 0.5 reduce-precision_convert_fusion
  9.2 0.1 pad_add_fusion.1
  9.2 0.1 not_and_fusion
  9.3 1.3 pad_maximum_fusion.band_ref
  10.6 0.1 select_convert_fusion.pick_ref
  10.7 0.6 fusion.51.taps_ref
  11.2 0.7 fusion.54
  12.6 0.0 collective-permute-done
  12.6 1.4 collective-permute-done.1
  14.0 4.0 %collective-permute-start.2 = (bf16[3,8,512]{2,1,0:T(8,128)(2,1)S(1)}, bf16[3,8,512]{2,1,0:T(8,128)(2,1)S(1)}, u32[]{:S(2)}, u32[]{:S(2)}) collective-permute-start(bf16[3,8,512]{2,1,0:T(8,128)(2,1)S(1)} %get-tuple-element.80), channel_id=1, source_target_pairs={{1,0},{2,1},{3,2},{5,4},{6,5},{7,6},{9,8},{10,9},{11,10},{13,12},{... | collective-permute-start | bytes 73736 | tf_op jit(solution)/shard_map/ppermute | solution.py:383
  18.1 3.0 %collective-permute-start.3 = (bf16[3,8,512]{2,1,0:T(8,128)(2,1)S(1)}, bf16[3,8,512]{2,1,0:T(8,128)(2,1)S(1)}, u32[]{:S(2)}, u32[]{:S(2)}) collective-permute-start(bf16[3,8,512]{2,1,0:T(8,128)(2,1)S(1)} %get-tuple-element.81), channel_id=1, source_target_pairs={{0,1},{1,2},{2,3},{4,5},{5,6},{6,7},{8,9},{9,10},{10,11},{12,13},{... | collective-permute-start | bytes 73736 | tf_op jit(solution)/shard_map/ppermute | solution.py:383
  21.1 0.6 broadcast_multiply_fusion.taps_ref
  21.7 0.6 slice.171.pick_ref
  22.3 0.1 select_bitcast_fusion.1
  22.4 0.1 slice_convert_fusion.2
  22.5 0.1 fusion.58
  22.8 6.3 %sort.78 = (s32[4608]{0:T(1024)S(1)}, s32[4608]{0:T(1024)S(1)}, f32[4608]{0:T(1024)S(1)}, f32[4608]{0:T(1024)S(1)}, f32[4608]{0:T(1024)S(1)}, /*index=5*/f32[4608]{0:T(1024)S(1)}) sort(s32[4608]{0:T(1024)S(1)} %fusion.11, s32[4608]{0:T(1024)S(1)} %iota.103, f32[4608]{0:T(1024)S(1)} %reshape.597, f32[4608]{0:T(1024)S(1)} %reshape.598, f32[4608]{0:T(1024)S(1)} %reshape.599, ...), dimensions={0}, to_apply=%region_0.1 | sort | flops 59904 | bytes 221184 | tf_op jit(solution)/shard_map/sort | solution.py:416
  29.1 0.2 fusion.22
  29.6 0.2 stack.101
  29.8 4.0 %collective-permute-start.4 = (bf16[36,8,128]{2,1,0:T(8,128)(2,1)S(1)}, bf16[36,8,128]{2,1,0:T(8,128)(2,1)S(1)}, u32[]{:S(2)}, u32[]{:S(2)}) collective-permute-start(bf16[36,8,128]{2,1,0:T(8,128)(2,1)S(1)} %bitcast.152), channel_id=1, source_target_pairs={{0,1},{1,2},{2,3},{4,5},{5,6},{6,7},{8,9},{9,10},{10,11},{12,13},{... | collective-permute-start | bytes 221192 | tf_op jit(solution)/shard_map/ppermute | solution.py:383
  33.8 1.9 collective-permute-start.5
  35.8 0.7 multiply_add_fusion.1
  36.4 0.1 convert_reduce_fusion.1
  36.6 0.1 select_reduce_fusion.3
  36.7 0.6 pad_add_fusion.2.list_ref
  37.3 0.0 collective-permute-done.4
  37.3 2.2 %collective-permute-done.5 = bf16[36,8,128]{2,1,0:T(8,128)(2,1)S(1)} collective-permute-done((bf16[36,8,128]{2,1,0:T(8,128)(2,1)S(1)}, bf16[36,8,128]{2,1,0:T(8,128)(2,1)S(1)}, u32[]{:S(2)}, u32[]{:S(2)}) %collective-permute-start.5) | collective-permute-done | bytes 73760 | tf_op jit(solution)/shard_map/ppermute | solution.py:383
  39.5 0.1 collective-permute-start.6
  39.6 4.1 %collective-permute-start.7 = (bf16[3,36,8,128]{3,2,1,0:T(8,128)(2,1)S(1)}, bf16[3,36,8,128]{3,2,1,0:T(8,128)(2,1)S(1)}, u32[]{:S(2)}, u32[]{:S(2)}) collective-permute-start(bf16[3,36,8,128]{3,2,1,0:T(8,128)(2,1)S(1)} %get-tuple-element.72), channel_id=1, source_target_pairs={{0,28},{4,0},{8,4},{12,8},{16,12},{20,16},{24,20},{28,24},{1,29},{... | collective-permute-start | bytes 663560 | tf_op jit(solution)/shard_map/ppermute | solution.py:377
  43.7 22.6 %spread_own.1.old_ref = f32[84,64,512]{2,1,0:T(8,128)} custom-call(s32[1]{0:T(128)} %bitcast.35.count_ref, s32[37]{0:T(128)} %pad_add_fusion.2.list_ref, bf16[36,8,128]{2,1,0:T(8,128)(2,1)} %bitcast.155, bf16[8,128]{1,0:T(8,128)(2,1)} %slice.171.pick_ref), custom_call_target="tpu_custom_call" | custom-call | flops 10000000000 | bytes 30000000 | tf_op jit(solution)/shard_map/spread_own/pallas_call | solution.py:277
  66.4 0.0 collective-permute-done.6
  66.4 0.0 collective-permute-done.7
  66.4 0.1 pad_maximum_fusion.1
  66.5 0.3 slice_convert_fusion
  66.8 0.3 fusion.57
  67.0 0.5 select_reduce_fusion.1
  67.5 0.1 reshape.594
  67.6 0.7 convert_reduce_fusion.2
  68.3 0.1 reshape.595
  68.4 0.1 convert_reduce_fusion
  68.5 0.2 select_reduce_fusion
  68.7 0.7 pad_add_fusion.list_ref
  69.4 39.4 %spread_rest.1.dens_ref = f32[4,64,16,512]{3,2,1,0:T(8,128)} custom-call(s32[1]{0:T(128)} %bitcast.29.count_ref, s32[325]{0:T(512)} %pad_add_fusion.list_ref, f32[13]{0:T(128)} %fusion.51.taps_ref, bf16[324,8,128]{2,1,0:T(8,128)(2,1)} %bitcast.149, bf16[8,128]{1,0:T(8,128)(2,1)} %slice.171.pick_ref, f32[3,512]{1,0:T(4,128)} %field_ref.1, ...), custom_call_target="tpu_custom_call" | custom-call | flops 20000000000 | bytes 30000000 | tf_op jit(solution)/shard_map/spread_rest/pallas_call | solution.py:297
  108.8 39.6 %sample_rest.1 = (f32[324,8,128]{2,1,0:T(8,128)}, bf16[84,16,1536]{2,1,0:T(8,128)(2,1)}) custom-call(s32[1]{0:T(128)} %bitcast.29.count_ref, s32[325]{0:T(512)} %pad_add_fusion.list_ref, f32[13]{0:T(128)} %broadcast_multiply_fusion.taps_ref, f32[1]{0:T(128)} %bitcast.36.scale_ref, bf16[324,8,128]{2,1,0:T(8,128)(2,1)} %bitcast.150, bf16[8,384]{1,0:T(8,128)(2,1)} %copy-done.2, ...), custom_call_target="tpu_custom_call" | custom-call | flops 20000000000 | bytes 30000000 | tf_op jit(solution)/shard_map/sample_rest/pallas_call | solution.py:321
  148.4 1.4 fusion.56
  149.8 0.1 collective-permute-start.8
  149.9 4.1 %collective-permute-start.9 = (f32[3,36,3,128]{3,2,1,0:T(4,128)S(1)}, f32[3,36,3,128]{3,2,1,0:T(4,128)S(1)}, u32[]{:S(2)}, u32[]{:S(2)}) collective-permute-start(f32[3,36,3,128]{3,2,1,0:T(4,128)S(1)} %bitcast.158), channel_id=1, source_target_pairs={{0,28},{4,0},{8,4},{12,8},{16,12},{20,16},{24,20},{28,24},{1,29},{... | collective-permute-start | bytes 497672 | tf_op jit(solution)/shard_map/ppermute | solution.py:377
  154.0 3.3 %collective-permute-done.8 = f32[3,36,3,128]{3,2,1,0:T(4,128)S(1)} collective-permute-done((f32[3,36,3,128]{3,2,1,0:T(4,128)S(1)}, f32[3,36,3,128]{3,2,1,0:T(4,128)S(1)}, u32[]{:S(2)}, u32[]{:S(2)}) %collective-permute-start.8) | collective-permute-done | bytes 165920 | tf_op jit(solution)/shard_map/ppermute | solution.py:377
  157.3 0.0 collective-permute-done.9
  157.3 0.1 add_add_fusion
  157.5 3.8 %collective-permute-start.10 = (f32[36,3,128]{2,1,0:T(4,128)S(1)}, f32[36,3,128]{2,1,0:T(4,128)S(1)}, u32[]{:S(2)}, u32[]{:S(2)}) collective-permute-start(f32[36,3,128]{2,1,0:T(4,128)S(1)} %get-tuple-element.69), channel_id=1, source_target_pairs={{0,1},{1,2},{2,3},{4,5},{5,6},{6,7},{8,9},{9,10},{10,11},{12,13},{... | collective-permute-start | bytes 165896 | tf_op jit(solution)/shard_map/ppermute | solution.py:383
  161.3 1.9 collective-permute-start.11
  163.2 23.4 %sample_own.1 = f32[36,8,128]{2,1,0:T(8,128)} custom-call(s32[1]{0:T(128)} %bitcast.35.count_ref, s32[37]{0:T(128)} %pad_add_fusion.2.list_ref, f32[1]{0:T(128)} %bitcast.36.scale_ref, bf16[36,8,128]{2,1,0:T(8,128)(2,1)} %bitcast.156, bf16[8,384]{1,0:T(8,128)(2,1)} %copy-done.2, bf16[84,16,1536]{2,1,0:T(8,128)(2,1)} %get-tuple-element.36.fmat), custom_call_target="tpu_custom_call" | custom-call | flops 10000000000 | bytes 30000000 | tf_op jit(solution)/shard_map/sample_own/pallas_call | solution.py:348
  186.7 1.0 fusion.6
  187.6 0.1 slice_reduce_fusion
  187.8 7.6 %sort.79 = (s32[4608]{0:T(1024)}, f32[4608]{0:T(1024)S(1)}, f32[4608]{0:T(1024)S(1)}, f32[4608]{0:T(1024)S(1)}, s32[4608]{0:T(1024)}) sort(s32[4608]{0:T(1024)S(1)} %get-tuple-element.34, f32[4608]{0:T(1024)S(1)} %bitcast.163, f32[4608]{0:T(1024)S(1)} %bitcast.162, f32[4608]{0:T(1024)S(1)} %bitcast.161, s32[4608]{0:T(1024)S(1)} %iota.112), dimensions={0}, to_apply=%region_12.13 | sort | flops 59904 | bytes 184320 | tf_op jit(solution)/shard_map/sort | solution.py:467
  195.5 0.1 pad_maximum_fusion.4
  195.6 0.7 broadcast_in_dim.173
  (60 shorter events, 0.6 us)
Async XLA Ops:
  0.6 21.6 %copy-start.3 = (bf16[8]{0:T(256)(128)(2,1)S(1)}, bf16[8]{0:T(256)(128)(2,1)}, u32[]{:S(2)}) copy-start(bf16[8]{0:T(256)(128)(2,1)} %constant.232.clone.1) | copy-start | bytes 52
  3.5 9.2 %collective-permute-start = (bf16[3,8,512]{2,1,0:T(8,128)(2,1)S(1)}, bf16[3,8,512]{2,1,0:T(8,128)(2,1)S(1)}, u32[]{:S(2)}, u32[]{:S(2)}) collective-permute-start(bf16[3,8,512]{2,1,0:T(8,128)(2,1)S(1)} %get-tuple-element.83), channel_id=1, source_target_pairs={{0,28},{4,0},{8,4},{12,8},{16,12},{20,16},{24,20},{28,24},{1,29},{... | collective-permute-start | bytes 73736 | tf_op jit(solution)/shard_map/ppermute | solution.py:377
  8.6 5.4 %collective-permute-start.1 = (bf16[3,8,512]{2,1,0:T(8,128)(2,1)S(1)}, bf16[3,8,512]{2,1,0:T(8,128)(2,1)S(1)}, u32[]{:S(2)}, u32[]{:S(2)}) collective-permute-start(bf16[3,8,512]{2,1,0:T(8,128)(2,1)S(1)} %get-tuple-element.84), channel_id=1, source_target_pairs={{0,4},{4,8},{8,12},{12,16},{16,20},{20,24},{24,28},{28,0},{1,5},{5... | collective-permute-start | bytes 73736 | tf_op jit(solution)/shard_map/ppermute | solution.py:377
  10.7 55.7 %copy-start.2 = (bf16[8,384]{1,0:T(8,128)(2,1)}, bf16[8,384]{1,0:T(8,128)(2,1)S(1)}, u32[]{:S(2)}) copy-start(bf16[8,384]{1,0:T(8,128)(2,1)S(1)} %select_convert_fusion.pick_ref) | copy-start | bytes 18436
  14.0 8.2 %collective-permute-start.2 = (bf16[3,8,512]{2,1,0:T(8,128)(2,1)S(1)}, bf16[3,8,512]{2,1,0:T(8,128)(2,1)S(1)}, u32[]{:S(2)}, u32[]{:S(2)}) collective-permute-start(bf16[3,8,512]{2,1,0:T(8,128)(2,1)S(1)} %get-tuple-element.80), channel_id=1, source_target_pairs={{1,0},{2,1},{3,2},{5,4},{6,5},{7,6},{9,8},{10,9},{11,10},{13,12},{... | collective-permute-start | bytes 73736 | tf_op jit(solution)/shard_map/ppermute | solution.py:383
  18.1 4.2 %collective-permute-start.3 = (bf16[3,8,512]{2,1,0:T(8,128)(2,1)S(1)}, bf16[3,8,512]{2,1,0:T(8,128)(2,1)S(1)}, u32[]{:S(2)}, u32[]{:S(2)}) collective-permute-start(bf16[3,8,512]{2,1,0:T(8,128)(2,1)S(1)} %get-tuple-element.81), channel_id=1, source_target_pairs={{0,1},{1,2},{2,3},{4,5},{5,6},{6,7},{8,9},{9,10},{10,11},{12,13},{... | collective-permute-start | bytes 73736 | tf_op jit(solution)/shard_map/ppermute | solution.py:383
  29.8 13.9 %copy-start.1 = (bf16[8,36,128]{2,0,1:T(8,128)(2,1)}, bf16[8,36,128]{2,0,1:T(8,128)(2,1)S(1)}, u32[]{:S(2)}) copy-start(bf16[8,36,128]{2,0,1:T(8,128)(2,1)S(1)} %stack.101) | copy-start | bytes 221188
  29.8 7.4 %collective-permute-start.4 = (bf16[36,8,128]{2,1,0:T(8,128)(2,1)S(1)}, bf16[36,8,128]{2,1,0:T(8,128)(2,1)S(1)}, u32[]{:S(2)}, u32[]{:S(2)}) collective-permute-start(bf16[36,8,128]{2,1,0:T(8,128)(2,1)S(1)} %bitcast.152), channel_id=1, source_target_pairs={{0,1},{1,2},{2,3},{4,5},{5,6},{6,7},{8,9},{9,10},{10,11},{12,13},{... | collective-permute-start | bytes 221192 | tf_op jit(solution)/shard_map/ppermute | solution.py:383
  33.8 5.7 %collective-permute-start.5 = (bf16[36,8,128]{2,1,0:T(8,128)(2,1)S(1)}, bf16[36,8,128]{2,1,0:T(8,128)(2,1)S(1)}, u32[]{:S(2)}, u32[]{:S(2)}) collective-permute-start(bf16[36,8,128]{2,1,0:T(8,128)(2,1)S(1)} %bitcast.153), channel_id=1, source_target_pairs={{1,0},{2,1},{3,2},{5,4},{6,5},{7,6},{9,8},{10,9},{11,10},{13,12},{... | collective-permute-start | bytes 221192 | tf_op jit(solution)/shard_map/ppermute | solution.py:383
  39.5 26.8 %collective-permute-start.6 = (bf16[3,36,8,128]{3,2,1,0:T(8,128)(2,1)S(1)}, bf16[3,36,8,128]{3,2,1,0:T(8,128)(2,1)S(1)}, u32[]{:S(2)}, u32[]{:S(2)}) collective-permute-start(bf16[3,36,8,128]{3,2,1,0:T(8,128)(2,1)S(1)} %get-tuple-element.72), channel_id=1, source_target_pairs={{0,4},{4,8},{8,12},{12,16},{16,20},{20,24},{24,28},{28,0},{1,5},{5... | collective-permute-start | bytes 663560 | tf_op jit(solution)/shard_map/ppermute | solution.py:377
  39.6 26.8 %collective-permute-start.7 = (bf16[3,36,8,128]{3,2,1,0:T(8,128)(2,1)S(1)}, bf16[3,36,8,128]{3,2,1,0:T(8,128)(2,1)S(1)}, u32[]{:S(2)}, u32[]{:S(2)}) collective-permute-start(bf16[3,36,8,128]{3,2,1,0:T(8,128)(2,1)S(1)} %get-tuple-element.72), channel_id=1, source_target_pairs={{0,28},{4,0},{8,4},{12,8},{16,12},{20,16},{24,20},{28,24},{1,29},{... | collective-permute-start | bytes 663560 | tf_op jit(solution)/shard_map/ppermute | solution.py:377
  66.5 2.9 %copy-start = (bf16[3,3,36,8,128]{4,3,2,1,0:T(8,128)(2,1)}, bf16[3,3,36,8,128]{4,3,2,1,0:T(8,128)(2,1)S(1)}, u32[]{:S(2)}) copy-start(bf16[3,3,36,8,128]{4,3,2,1,0:T(8,128)(2,1)S(1)} %pad_maximum_fusion.1) | copy-start | bytes 1990660
  149.8 7.5 %collective-permute-start.8 = (f32[3,36,3,128]{3,2,1,0:T(4,128)S(1)}, f32[3,36,3,128]{3,2,1,0:T(4,128)S(1)}, u32[]{:S(2)}, u32[]{:S(2)}) collective-permute-start(f32[3,36,3,128]{3,2,1,0:T(4,128)S(1)} %bitcast.160), channel_id=1, source_target_pairs={{0,4},{4,8},{8,12},{12,16},{16,20},{20,24},{24,28},{28,0},{1,5},{5... | collective-permute-start | bytes 497672 | tf_op jit(solution)/shard_map/ppermute | solution.py:377
  149.9 7.5 %collective-permute-start.9 = (f32[3,36,3,128]{3,2,1,0:T(4,128)S(1)}, f32[3,36,3,128]{3,2,1,0:T(4,128)S(1)}, u32[]{:S(2)}, u32[]{:S(2)}) collective-permute-start(f32[3,36,3,128]{3,2,1,0:T(4,128)S(1)} %bitcast.158), channel_id=1, source_target_pairs={{0,28},{4,0},{8,4},{12,8},{16,12},{20,16},{24,20},{28,24},{1,29},{... | collective-permute-start | bytes 497672 | tf_op jit(solution)/shard_map/ppermute | solution.py:377
  157.5 29.2 %collective-permute-start.10 = (f32[36,3,128]{2,1,0:T(4,128)S(1)}, f32[36,3,128]{2,1,0:T(4,128)S(1)}, u32[]{:S(2)}, u32[]{:S(2)}) collective-permute-start(f32[36,3,128]{2,1,0:T(4,128)S(1)} %get-tuple-element.69), channel_id=1, source_target_pairs={{0,1},{1,2},{2,3},{4,5},{5,6},{6,7},{8,9},{9,10},{10,11},{12,13},{... | collective-permute-start | bytes 165896 | tf_op jit(solution)/shard_map/ppermute | solution.py:383
  161.3 25.4 %collective-permute-start.11 = (f32[36,3,128]{2,1,0:T(4,128)S(1)}, f32[36,3,128]{2,1,0:T(4,128)S(1)}, u32[]{:S(2)}, u32[]{:S(2)}) collective-permute-start(f32[36,3,128]{2,1,0:T(4,128)S(1)} %get-tuple-element.70), channel_id=1, source_target_pairs={{1,0},{2,1},{3,2},{5,4},{6,5},{7,6},{9,8},{10,9},{11,10},{13,12},{... | collective-permute-start | bytes 165896 | tf_op jit(solution)/shard_map/ppermute | solution.py:383

commit v3 on v2

--- a/solution.py
+++ b/solution.py
@@ -15,6 +15,8 @@
 BX = 8
 XO = 8
 XROWS = 84
+BUCKETS = 10
+FROWS = 92
 BP = BX * CY
 
 spread_width = 12.5
@@ -68,11 +70,11 @@
     return xt, sx, sy
 
 
-def accumulate(count_ref, list_ref, tab_ref, pick_ref, acc, amat, zmat):
+def accumulate(bounds_ref, list_ref, tab_ref, pick_ref, acc, amat, zmat):
     def tile(k, _):
         i, n, first, last = tile_codes(list_ref, tab_ref, k)
         xt, sx, sy = framed(tab_ref, i, n)
-        zrep = columns(xt, pick_ref[...])
+        zrep = columns(xt, pick_ref[:, 0:128])
         lane = lax.broadcasted_iota(jnp.int32, (TILE, 128), 1).astype(jnp.float32)
         for q in range(NZ // 128):
             hit = jnp.where(lane + (128.0 * q) == zrep, 1.0, 0.0).astype(jnp.bfloat16)
@@ -101,60 +103,22 @@
         lax.fori_loop(0, (last - first) // BX + 1, window, 0)
         return 0
 
-    lax.fori_loop(0, count_ref[0], tile, 0)
-
-
-def spread_own_kernel(count_ref, list_ref, tab_ref, pick_ref, out_ref, acc, amat, zmat, sem):
+    lax.fori_loop(bounds_ref[0], bounds_ref[1], tile, 0)
+
+
+def spread_own_kernel(bounds_ref, list_ref, tab_ref, pick_ref, out_ref, acc, amat, zmat, sem):
     def clear(i, _):
         acc[i] = jnp.zeros(acc.shape[1:], jnp.float32)
         return 0
 
     lax.fori_loop(0, XROWS, clear, 0)
-    accumulate(count_ref, list_ref, tab_ref, pick_ref, acc, amat, zmat)
+    accumulate(bounds_ref, list_ref, tab_ref, pick_ref, acc, amat, zmat)
     copy = pltpu.make_async_copy(acc, out_ref, sem)
     copy.start()
     copy.wait()
 
 
-def spread_kernel(
-    count_ref, list_ref, taps_ref, tab_ref, pick_ref, field_ref, band_ref, old_ref, out_ref, acc, amat, zmat, wide, sem
-):
-    step = pl.program_id(0)
-
-    @pl.when(step == 0)
-    def _():
-        copy = pltpu.make_async_copy(old_ref, acc, sem)
-        copy.start()
-        copy.wait()
-        accumulate(count_ref, list_ref, tab_ref, pick_ref, acc, amat, zmat)
-
-    @pl.when(step > 0)
-    def _():
-        base = (step - 1) * XO
-        taps = [taps_ref[k] for k in range(13)]
-
-        def chunk(j, _):
-            cols = pl.ds(pl.multiple_of(j * 128, 128), 128)
-            for c in range(4):
-                outs = x_filtered(lambda i: acc[base + i, c * CY : (c + 1) * CY, cols], taps, XO)
-                for o in range(XO):
-                    hi, lo = hi_lo(outs[o])
-                    rows = slice((c * XO + o) * CY, (c * XO + o + 1) * CY)
-                    wide[0, rows, cols] = hi
-                    wide[1, rows, cols] = lo
-            return 0
-
-        lax.fori_loop(0, NZ // 128, chunk, 0)
-        hi, lo = wide[0], wide[1]
-        full = jnp.concatenate([hi, hi, lo], axis=1)
-        dens = jnp.dot(full, band_ref[...], preferred_element_type=jnp.float32)
-        dens = dens.reshape(4, XO, CY, NZ)
-        out_ref[3] = dens[3]
-        for c in range(3):
-            out_ref[c] = dens[c] + dens[3] * field_ref[c : c + 1, :][None]
-
-
-def sampled(count_ref, list_ref, scale_ref, tab_ref, pick_ref, fmat, out_ref, gathered):
+def sampled(bounds_ref, list_ref, scale_ref, tab_ref, pick_ref, fmat, out_ref, gathered):
     scale = scale_ref[0]
     out_ref[...] = jnp.zeros(out_ref.shape, jnp.float32)
 
@@ -170,74 +134,122 @@
         wy = gauss(ypl - (yrep + sy)) * scale
         xoff = xrep - xpl
 
-        def part(w):
-            x0 = first + w * BX
-            a = jnp.where(xoff == x0.astype(jnp.float32) - sx, wy, 0.0)
-            full = jnp.concatenate(hi_lo(a), axis=1)
-            f = fmat[pl.ds(x0, BX)].reshape(BP, 3 * NZ)
-            return jnp.dot(full, jnp.concatenate([f, f], axis=0), preferred_element_type=jnp.float32)
-
-        gathered[...] = part(jnp.int32(0))
-
-        def window(w, _):
-            gathered[...] += part(w)
-            return 0
-
-        lax.fori_loop(1, (last - first) // BX + 1, window, 0)
+        def part(x0, blocks):
+            lhs, rhs = [], []
+            for k in range(blocks):
+                a = jnp.where(xoff == (x0 + k * BX).astype(jnp.float32) - sx, wy, 0.0)
+                lhs.extend(hi_lo(a))
+                f = fmat[pl.ds(x0 + k * BX, BX)].reshape(BP, 3 * NZ)
+                rhs.extend([f, f])
+            return jnp.dot(
+                jnp.concatenate(lhs, axis=1), jnp.concatenate(rhs, axis=0), preferred_element_type=jnp.float32
+            )
+
+        @pl.when(last - first < BX)
+        def _():
+            gathered[...] = part(first, 1)
+
+        @pl.when(last - first >= BX)
+        def _():
+            gathered[...] = part(first, 2)
+
+            def window(w, _):
+                gathered[...] += part(first + w * (2 * BX), 2)
+                return 0
+
+            lax.fori_loop(1, (last - first) // (2 * BX) + 1, window, 0)
+
         sums = [None] * 3
         for q in range(NZ // 128):
             wz = gauss(lane + (128.0 * q) - zrep) * scale
             for c in range(3):
                 t = gathered[:, c * NZ + 128 * q : c * NZ + 128 * (q + 1)] * wz
                 sums[c] = t if sums[c] is None else sums[c] + t
-        ones = jnp.ones((8, 256), jnp.bfloat16)
         for c in range(3):
-            both = jnp.concatenate(hi_lo(sums[c]), axis=1)
-            row = lax.dot_general(ones, both, (((1,), (1,)), ((), ())), preferred_element_type=jnp.float32)
-            out_ref[i, c : c + 1, :] = row[0:1, :]
+            out_ref[i, c : c + 1, :] = jnp.sum(sums[c].T, axis=0, keepdims=True)
         return 0
 
-    lax.fori_loop(0, count_ref[0], tile, 0)
-
-
-def sample_kernel(
-    count_ref,
+    lax.fori_loop(bounds_ref[0], bounds_ref[1], tile, 0)
+
+
+def main_kernel(
+    bounds_ref,
     list_ref,
-    taps_ref,
+    raw_ref,
+    unit_ref,
     scale_ref,
     tab_ref,
     pick_ref,
+    field_ref,
     ground_ref,
+    band_ref,
+    old_ref,
     dens_ref,
     out_ref,
     fmat,
+    acc,
+    amat,
+    zmat,
+    wide_a,
+    wide_b,
     flow,
     gathered,
+    sem,
 ):
     step = pl.program_id(0)
-    last_step = pl.num_programs(0) - 1
+    steps = CX // XO
+    raw = [raw_ref[k] for k in range(13)]
+
+    def filtered(b, wide):
+        base = b * XO
+        for q in range(NZ // 128):
+            cols = slice(q * 128, (q + 1) * 128)
+            for c in range(4):
+                outs = x_filtered(lambda i: acc[base + i, c * CY : (c + 1) * CY, cols], raw, XO)
+                for o in range(XO):
+                    hi, lo = hi_lo(outs[o])
+                    rows = slice((c * XO + o) * CY, (c * XO + o + 1) * CY)
+                    wide[0, rows, cols] = hi
+                    wide[1, rows, cols] = lo
+
+    def finish(b, wide):
+        hi, lo = wide[0], wide[1]
+        full = jnp.concatenate([hi, hi, lo], axis=1)
+        dens = jnp.dot(full, band_ref[...], preferred_element_type=jnp.float32)
+        dens = dens.reshape(4, XO, CY, NZ)
+        dens_ref[3] = dens[3]
+        for c in range(3):
+            d = dens[c] + dens[3] * field_ref[c : c + 1, :][None]
+            dens_ref[c] = d
+            flow[c, pl.ds(12 + b * XO, XO)] = d + ground_ref[c : c + 1, :][None]
 
     @pl.when(step == 0)
     def _():
+        copy = pltpu.make_async_copy(old_ref, acc, sem)
+        copy.start()
+
         def clear(i, _):
             flow[:, i] = jnp.zeros((3, CY, NZ), jnp.float32)
             flow[:, 12 + CX + i] = jnp.zeros((3, CY, NZ), jnp.float32)
             return 0
 
-        lax.fori_loop(0, 12, clear, 0)
-        for i in range(12 + CX + 12, flow.shape[1]):
-            flow[:, i] = jnp.zeros((3, CY, NZ), jnp.float32)
-
-    @pl.when(step < last_step)
+        lax.fori_loop(0, 16, clear, 0)
+        for i in range(BUCKETS * BX, FROWS):
+            fmat[i] = jnp.zeros(fmat.shape[1:], jnp.bfloat16)
+        copy.wait()
+        accumulate(bounds_ref, list_ref, tab_ref, pick_ref, acc, amat, zmat)
+        filtered(0, wide_a)
+
+    for parity, now, later in ((1, wide_a, wide_b), (0, wide_b, wide_a)):
+
+        @pl.when((step > 0) & (step <= steps) & (step % 2 == parity))
+        def _(now=now, later=later):
+            finish(step - 1, now)
+            filtered(jnp.minimum(step, steps - 1), later)
+
+    @pl.when(step > steps)
     def _():
-        for c in range(3):
-            g = ground_ref[c : c + 1, :]
-            for i in range(XO):
-                flow[c, 12 + step * XO + i] = dens_ref[c, i] + g
-
-    @pl.when(step == last_step)
-    def _():
-        taps = [taps_ref[k] for k in range(13)]
+        taps = [unit_ref[k] for k in range(13)]
 
         def block(b, _):
             for c in range(3):
@@ -245,20 +257,20 @@
                 def chunk(j, _, c=c):
                     cols = pl.ds(pl.multiple_of(j * 128, 128), 128)
                     dest = pl.ds(pl.multiple_of(c * NZ + j * 128, 128), 128)
-                    outs = x_filtered(lambda i: flow[c, b * 4 + i, :, cols], taps, 4)
-                    for o in range(4):
-                        fmat[b * 4 + o, :, dest] = outs[o].astype(jnp.bfloat16)
+                    outs = x_filtered(lambda i: flow[c, b * BX + i, :, cols], taps, BX)
+                    for o in range(BX):
+                        fmat[b * BX + o, :, dest] = outs[o].astype(jnp.bfloat16)
                     return 0
 
                 lax.fori_loop(0, NZ // 128, chunk, 0)
             return 0
 
-        lax.fori_loop(0, XROWS // 4, block, 0)
-        sampled(count_ref, list_ref, scale_ref, tab_ref, pick_ref, fmat, out_ref, gathered)
-
-
-def sample_own_kernel(count_ref, list_ref, scale_ref, tab_ref, pick_ref, fmat, out_ref, gathered):
-    sampled(count_ref, list_ref, scale_ref, tab_ref, pick_ref, fmat, out_ref, gathered)
+        lax.fori_loop(0, BUCKETS, block, 0)
+        sampled(bounds_ref, list_ref, scale_ref, tab_ref, pick_ref, fmat, out_ref, gathered)
+
+
+def sample_own_kernel(bounds_ref, list_ref, scale_ref, tab_ref, pick_ref, fmat, out_ref, gathered):
+    sampled(bounds_ref, list_ref, scale_ref, tab_ref, pick_ref, fmat, out_ref, gathered)
 
 
 def smem():
@@ -292,55 +304,40 @@
     )(*listing, table, pick)
 
 
-def spread_call(listing, taps, table, pick, field, band, old):
+def main_call(listing, raw, unit, scale, table, pick, field, ground, band, old):
     steps = CX // XO
+    n = table.shape[0]
+    fshape = (FROWS, CY, 3 * NZ)
     return pl.pallas_call(
-        spread_kernel,
-        grid=(steps + 1,),
-        in_specs=[smem(), smem(), smem(), whole(table.shape), whole(pick.shape), whole(field.shape), whole(band.shape)]
+        main_kernel,
+        grid=(steps + 2,),
+        in_specs=[smem()] * 5
+        + [whole(v.shape) for v in (table, pick, field, ground, band)]
         + [pl.BlockSpec(memory_space=pl.ANY)],
-        out_specs=pl.BlockSpec((4, XO, CY, NZ), lambda i: (0, jnp.maximum(i - 1, 0), 0, 0)),
-        out_shape=jax.ShapeDtypeStruct((4, CX, CY, NZ), jnp.float32),
+        out_specs=[
+            pl.BlockSpec((4, XO, CY, NZ), lambda i: (0, jnp.clip(i - 1, 0, steps - 1), 0, 0)),
+            whole((n, 8, TILE)),
+            whole(fshape),
+        ],
+        out_shape=[
+            jax.ShapeDtypeStruct((4, CX, CY, NZ), jnp.float32),
+            jax.ShapeDtypeStruct((n, 8, TILE), jnp.float32),
+            jax.ShapeDtypeStruct(fshape, jnp.bfloat16),
+        ],
         scratch_shapes=[
             pltpu.VMEM(old.shape, jnp.float32),
             pltpu.VMEM((4 * BP, 2 * TILE), jnp.bfloat16),
             pltpu.VMEM((2 * TILE, NZ), jnp.bfloat16),
             pltpu.VMEM((2, 4 * XO * CY, NZ), jnp.bfloat16),
+            pltpu.VMEM((2, 4 * XO * CY, NZ), jnp.bfloat16),
+            pltpu.VMEM((3, BUCKETS * BX + 12, CY, NZ), jnp.float32),
+            pltpu.VMEM((TILE, 3 * NZ), jnp.float32),
             pltpu.SemaphoreType.DMA,
         ],
         compiler_params=PARAMS,
-        cost_estimate=pl.CostEstimate(flops=2 * 10**10, transcendentals=0, bytes_accessed=3 * 10**7),
-        name="spread_rest",
-    )(*listing, taps, table, pick, field, band, old)
-
-
-def sample_call(listing, taps, scale, table, pick, ground, density):
-    n = table.shape[0]
-    steps = CX // XO
-    fshape = (XROWS, CY, 3 * NZ)
-    return pl.pallas_call(
-        sample_kernel,
-        grid=(steps + 1,),
-        in_specs=[
-            smem(),
-            smem(),
-            smem(),
-            smem(),
-            whole(table.shape),
-            whole(pick.shape),
-            whole(ground.shape),
-            pl.BlockSpec((3, XO, CY, NZ), lambda i: (0, jnp.minimum(i, steps - 1), 0, 0)),
-        ],
-        out_specs=[whole((n, 8, TILE)), whole(fshape)],
-        out_shape=[jax.ShapeDtypeStruct((n, 8, TILE), jnp.float32), jax.ShapeDtypeStruct(fshape, jnp.bfloat16)],
-        scratch_shapes=[
-            pltpu.VMEM((3, XROWS + 12, CY, NZ), jnp.float32),
-            pltpu.VMEM((TILE, 3 * NZ), jnp.float32),
-        ],
-        compiler_params=PARAMS,
-        cost_estimate=pl.CostEstimate(flops=2 * 10**10, transcendentals=0, bytes_accessed=3 * 10**7),
-        name="sample_rest",
-    )(*listing, taps, scale, table, pick, ground, density)
+        cost_estimate=pl.CostEstimate(flops=4 * 10**10, transcendentals=0, bytes_accessed=6 * 10**7),
+        name="main",
+    )(*listing, raw, unit, scale, table, pick, field, ground, band, old)
 
 
 def sample_own_call(listing, scale, table, pick, fmat):
@@ -369,7 +366,7 @@
     code = ((at * 128) + lo) * 128 + hi
     rows = jnp.sum(jnp.where((pos[None, :] == at[:, None]) & active[None, :], code[None, :], 0), axis=1)
     count = jnp.sum(active, dtype=jnp.int32)
-    return count[None], jnp.concatenate([jnp.array([per], jnp.int32), rows])
+    return jnp.stack([jnp.zeros((), jnp.int32), count]), jnp.concatenate([jnp.array([per], jnp.int32), rows])
 
 
 def ring(value, steps):
@@ -456,12 +453,18 @@
     coarse = lax.reduce_precision(exact, 8, 7)
     band = jnp.concatenate([coarse, exact - coarse, coarse], axis=0).astype(bf16)
 
-    half = spread_own_call(own_list, packed, pick[:, :128])
-    density = spread_call(rest_list, raw, table, pick[:, :128], field, band, half)
-    partial, fmat = sample_call(rest_list, unit, scale[None], table, pick, background, density)
-    mine = sample_own_call(own_list, scale[None], packed, pick, fmat)[:, :3]
+    half = spread_own_call(own_list, packed, pick)
+    density, partial, fmat = main_call(
+        rest_list, raw, unit, scale[None], table, pick, field, background, band, half
+    )
+    bounds, codes = own_list
+    middle = (bounds[1] + 1) // 2
+    early = sample_own_call((jnp.stack([bounds[0], middle]), codes), scale[None], packed, pick, fmat)
     partial = partial[:, :3].reshape(3, 3, tiles, 3, TILE)
     mixed = partial[1] + ring(partial[2], 1) + ring(partial[0], -1)
+    mixed, rest = lax.optimization_barrier((mixed, jnp.stack([middle, bounds[1]])))
+    late = sample_own_call((rest, codes), scale[None], packed, pick, fmat)
+    mine = (early + late)[:, :3]
     own = mixed[1] + mine + line(mixed[2], 1) + line(mixed[0], -1)
     own = own.transpose(1, 0, 2).reshape(3, total)
     _, *vel = lax.sort((order, own[0], own[1], own[2]), num_keys=1)

time: 199 us -> 192 us (0.965)
  Pallas kernels: 125 us -> 117 us
  other arithmetic: 25.4 us -> 30.7 us
    pallas_call x2 -> x1, Pallas kernels: 79 us -> 70.5 us  [main_call(): pl.pallas_call(main_kernel, grid=(steps + 2,), in_specs=[smem()] * 5 + [w...]
    another operation x3 -> x7, other arithmetic: 2.38 us -> 6.96 us  [the longest x2 2.62 us: listed(): jnp.stack([jnp.zeros((), jnp.int32), count])]
    ppermute x6, starting transfers between devices: 13.6 us -> 9.38 us  [ring(): lax.ppermute(value, 'stream', [(i, (i + steps) % count) for i in range(co...]
    ppermute x6, starting transfers between devices: 18.7 us -> 21.5 us  [line(): lax.ppermute(value, 'span', [(i, i + steps) for i in range(first, last)])]
    pallas_call x1 -> x2, Pallas kernels: 23.4 us -> 24.5 us  [sample_own_call(): pl.pallas_call(sample_own_kernel, grid=(1,), in_specs=[smem(), smem(), sm...]
  transfers between devices with their start and end apart: 12 -> 12, of which waited for: 3 -> 3; matrix products, arithmetic and copies ran while one was open for 3% -> 4% of each run, Pallas kernels for 23% -> 24%
where the time goes in v3:
time: 192 us; the launch traced here: 191 us
  Pallas kernels  117 us (61%)
  starting transfers between devices  30.8 us (16%)
  other arithmetic  30.7 us (16%)
  waiting for transfers between devices  5.89 us (3%)
  local copies, waits for them, and re-layouts  4.13 us (2%)
  between operations  2.51 us (1%)
    pallas_call x1, Pallas kernels, main_call(): pl.pallas_call(main_kernel, grid=(steps + 2,), in_specs=[smem()] * 5 + [w...  70.5 us
    pallas_call x2, Pallas kernels, sample_own_call(): pl.pallas_call(sample_own_kernel, grid=(1,), in_specs=[smem(), smem(), sm...  24.5 us
    pallas_call x1, Pallas kernels, spread_own_call(): pl.pallas_call(spread_own_kernel, grid=(1,), in_specs=[smem(), smem(), wh...  21.9 us
    ppermute x6, starting transfers between devices, line(): lax.ppermute(value, 'span', [(i, i + steps) for i in range(first, last)])  21.5 us
    ppermute x6, starting transfers between devices, ring(): lax.ppermute(value, 'stream', [(i, (i + steps) % count) for i in range(co...  9.38 us
    sort x1, other arithmetic, on_device(): _, *vel = lax.sort((order, own[0], own[1], own[2]), num_keys=1)  7.64 us
    sort x5, other arithmetic, on_device(): lax.sort((key, order) + tuple((inbound[c].astype(f32) for c in range(4)))...  6.36 us
    ppermute x6, waiting for transfers between devices, ring(): lax.ppermute(value, 'stream', [(i, (i + steps) % count) for i in range(co...  5.52 us
  transfers between devices with their start and end apart: 12, of which 3 were waited for; matrix products, arithmetic and copies ran while one was open for 4% of the time, Pallas kernels for 24%

profile of v3, /device:TPU:1, one launch (start us, length us, event | category | flops | bytes accessed | tf_op | source)
XLA Modules:
  0.0 190.9 jit_solution(2514672627078090564)
XLA Ops:
  0.6 0.0 copy-start.3
  0.6 0.8 fusion.36
  1.5 1.1 fusion.38
  2.6 0.9 concatenate.18
  3.5 2.1 %collective-permute-start.1 = (bf16[3,8,512]{2,1,0:T(8,128)(2,1)S(1)}, bf16[3,8,512]{2,1,0:T(8,128)(2,1)S(1)}, u32[]{:S(2)}, u32[]{:S(2)}) collective-permute-start(bf16[3,8,512]{2,1,0:T(8,128)(2,1)S(1)} %get-tuple-element.90), channel_id=1, source_target_pairs={{0,4},{4,8},{8,12},{12,16},{16,20},{20,24},{24,28},{28,0},{1,5},{5... | collective-permute-start | bytes 73736 | tf_op jit(solution)/shard_map/ppermute | solution.py:374
  5.6 3.1 %collective-permute-start = (bf16[3,8,512]{2,1,0:T(8,128)(2,1)S(1)}, bf16[3,8,512]{2,1,0:T(8,128)(2,1)S(1)}, u32[]{:S(2)}, u32[]{:S(2)}) collective-permute-start(bf16[3,8,512]{2,1,0:T(8,128)(2,1)S(1)} %get-tuple-element.89), channel_id=1, source_target_pairs={{0,28},{4,0},{8,4},{12,8},{16,12},{20,16},{24,20},{28,24},{1,29},{... | collective-permute-start | bytes 73736 | tf_op jit(solution)/shard_map/ppermute | solution.py:374
  8.7 0.5 reduce-precision_convert_fusion
  9.2 0.1 pad_add_fusion.1
  9.3 0.1 not_and_fusion
  9.4 1.3 pad_maximum_fusion.band_ref
  10.6 0.7 select_convert_fusion.pick_ref
  11.3 0.6 fusion.55
  12.6 0.0 collective-permute-done.1
  12.7 2.9 %collective-permute-start.2 = (bf16[3,8,512]{2,1,0:T(8,128)(2,1)S(1)}, bf16[3,8,512]{2,1,0:T(8,128)(2,1)S(1)}, u32[]{:S(2)}, u32[]{:S(2)}) collective-permute-start(bf16[3,8,512]{2,1,0:T(8,128)(2,1)S(1)} %get-tuple-element.86), channel_id=1, source_target_pairs={{1,0},{2,1},{3,2},{5,4},{6,5},{7,6},{9,8},{10,9},{11,10},{13,12},{... | collective-permute-start | bytes 73736 | tf_op jit(solution)/shard_map/ppermute | solution.py:380
  15.5 3.1 %collective-permute-start.3 = (bf16[3,8,512]{2,1,0:T(8,128)(2,1)S(1)}, bf16[3,8,512]{2,1,0:T(8,128)(2,1)S(1)}, u32[]{:S(2)}, u32[]{:S(2)}) collective-permute-start(bf16[3,8,512]{2,1,0:T(8,128)(2,1)S(1)} %get-tuple-element.87), channel_id=1, source_target_pairs={{0,1},{1,2},{2,3},{4,5},{5,6},{6,7},{8,9},{9,10},{10,11},{12,13},{... | collective-permute-start | bytes 73736 | tf_op jit(solution)/shard_map/ppermute | solution.py:380
  18.7 0.6 fusion.52
  19.2 0.0 collective-permute-done.2
  19.2 0.4 collective-permute-done.3
  19.6 0.1 select_bitcast_fusion.1
  19.7 0.1 slice_convert_fusion.2
  19.8 0.1 fusion.59
  20.1 6.3 %sort.78 = (s32[4608]{0:T(1024)S(1)}, s32[4608]{0:T(1024)S(1)}, f32[4608]{0:T(1024)S(1)}, f32[4608]{0:T(1024)S(1)}, f32[4608]{0:T(1024)S(1)}, /*index=5*/f32[4608]{0:T(1024)S(1)}) sort(s32[4608]{0:T(1024)S(1)} %fusion.12, s32[4608]{0:T(1024)S(1)} %iota.103, f32[4608]{0:T(1024)S(1)} %reshape.597, f32[4608]{0:T(1024)S(1)} %reshape.598, f32[4608]{0:T(1024)S(1)} %reshape.599, ...), dimensions={0}, to_apply=%region_0.1 | sort | flops 59904 | bytes 221184 | tf_op jit(solution)/shard_map/sort | solution.py:413
  26.5 0.2 fusion.23
  26.9 0.2 stack.123
  27.2 1.9 %collective-permute-start.5 = (bf16[36,8,128]{2,1,0:T(8,128)(2,1)S(1)}, bf16[36,8,128]{2,1,0:T(8,128)(2,1)S(1)}, u32[]{:S(2)}, u32[]{:S(2)}) collective-permute-start(bf16[36,8,128]{2,1,0:T(8,128)(2,1)S(1)} %bitcast.150), channel_id=1, source_target_pairs={{1,0},{2,1},{3,2},{5,4},{6,5},{7,6},{9,8},{10,9},{11,10},{13,12},{... | collective-permute-start | bytes 221192 | tf_op jit(solution)/shard_map/ppermute | solution.py:380
  29.1 4.2 %collective-permute-start.4 = (bf16[36,8,128]{2,1,0:T(8,128)(2,1)S(1)}, bf16[36,8,128]{2,1,0:T(8,128)(2,1)S(1)}, u32[]{:S(2)}, u32[]{:S(2)}) collective-permute-start(bf16[36,8,128]{2,1,0:T(8,128)(2,1)S(1)} %bitcast.151), channel_id=1, source_target_pairs={{0,1},{1,2},{2,3},{4,5},{5,6},{6,7},{8,9},{9,10},{10,11},{12,13},{... | collective-permute-start | bytes 221192 | tf_op jit(solution)/shard_map/ppermute | solution.py:380
  33.3 0.6 multiply_add_fusion.1
  34.0 0.1 convert_reduce_fusion.1
  34.1 1.3 pad_add_fusion.3.bounds_ref
  35.4 0.1 select_reduce_fusion.3
  35.5 0.6 pad_add_fusion.5.list_ref
  36.1 21.9 %spread_own.1.old_ref = f32[84,64,512]{2,1,0:T(8,128)} custom-call(s32[2]{0:T(128)} %pad_add_fusion.3.bounds_ref, s32[37]{0:T(128)} %pad_add_fusion.5.list_ref, bf16[36,8,128]{2,1,0:T(8,128)(2,1)} %bitcast.152, bf16[8,384]{1,0:T(8,128)(2,1)} %select_convert_fusion.pick_ref), custom_call_target="tpu_custom_call" | custom-call | flops 10000000000 | bytes 30000000 | tf_op jit(solution)/shard_map/spread_own/pallas_call | solution.py:289
  58.6 0.0 collective-permute-done.5
  58.7 0.9 fusion.56
  59.6 2.2 %collective-permute-start.7 = (bf16[3,36,8,128]{3,2,1,0:T(8,128)(2,1)S(1)}, bf16[3,36,8,128]{3,2,1,0:T(8,128)(2,1)S(1)}, u32[]{:S(2)}, u32[]{:S(2)}) collective-permute-start(bf16[3,36,8,128]{3,2,1,0:T(8,128)(2,1)S(1)} %get-tuple-element.78), channel_id=1, source_target_pairs={{0,28},{4,0},{8,4},{12,8},{16,12},{20,16},{24,20},{28,24},{1,29},{... | collective-permute-start | bytes 663560 | tf_op jit(solution)/shard_map/ppermute | solution.py:374
  61.8 0.0 collective-permute-start.6
  61.8 1.3 pad_add_fusion.6.bounds_ref
  63.1 0.7 pad_add_fusion.2.bounds_ref
  63.8 2.2 %collective-permute-done.7 = bf16[3,36,8,128]{3,2,1,0:T(8,128)(2,1)S(1)} collective-permute-done((bf16[3,36,8,128]{3,2,1,0:T(8,128)(2,1)S(1)}, bf16[3,36,8,128]{3,2,1,0:T(8,128)(2,1)S(1)}, u32[]{:S(2)}, u32[]{:S(2)}) %collective-permute-start.7) | collective-permute-done | bytes 221216 | tf_op jit(solution)/shard_map/ppermute | solution.py:374
  66.0 3.3 %collective-permute-done.6 = bf16[3,36,8,128]{3,2,1,0:T(8,128)(2,1)S(1)} collective-permute-done((bf16[3,36,8,128]{3,2,1,0:T(8,128)(2,1)S(1)}, bf16[3,36,8,128]{3,2,1,0:T(8,128)(2,1)S(1)}, u32[]{:S(2)}, u32[]{:S(2)}) %collective-permute-start.6) | collective-permute-done | bytes 221216 | tf_op jit(solution)/shard_map/ppermute | solution.py:374
  69.3 0.1 pad_maximum_fusion.1
  69.4 0.3 slice_convert_fusion
  69.7 0.3 fusion.58
  70.0 0.5 select_reduce_fusion.1
  70.4 0.6 convert_reduce_fusion.2
  71.1 0.1 reshape.594
  71.1 1.3 pad_add_fusion.4.bounds_ref
  72.5 0.1 reshape.595
  72.6 0.1 convert_reduce_fusion
  72.7 0.2 select_reduce_fusion
  72.9 0.7 pad_add_fusion.list_ref
  73.6 70.5 %main.1 = (f32[4,64,16,512]{3,2,1,0:T(8,128)}, f32[324,8,128]{2,1,0:T(8,128)}, bf16[92,16,1536]{2,1,0:T(8,128)(2,1)}) custom-call(s32[2]{0:T(128)} %pad_add_fusion.4.bounds_ref, s32[325]{0:T(512)} %pad_add_fusion.list_ref, f32[13]{0:T(128)} %get-tuple-element.113.raw_ref, f32[13]{0:T(128)} %get-tuple-element.114.unit_ref, f32[1]{0:T(128)} %bitcast.30.scale_ref, ...), custom_call_target="tpu_custom_call" | custom-call | flops 40000000000 | bytes 60000000 | tf_op jit(solution)/shard_map/main/pallas_call | solution.py:311
  144.1 1.4 fusion.57
  145.4 1.9 collective-permute-start.9
  147.3 12.0 %sample_own.2 = f32[36,8,128]{2,1,0:T(8,128)} custom-call(s32[2]{0:T(128)} %pad_add_fusion.2.bounds_ref, s32[37]{0:T(128)} %pad_add_fusion.5.list_ref, f32[1]{0:T(128)} %bitcast.30.scale_ref, bf16[36,8,128]{2,1,0:T(8,128)(2,1)} %bitcast.154, bf16[8,384]{1,0:T(8,128)(2,1)} %select_convert_fusion.pick_ref, bf16[92,16,1536]{2,1,0:T(8,128)(2,1)} %get-tuple-element.41.fmat), custom_call_target="tpu_custom_call" | custom-call | flops 10000000000 | bytes 30000000 | tf_op jit(solution)/shard_map/sample_own/pallas_call | solution.py:345
  159.4 0.1 add_add_fusion
  159.5 1.9 %collective-permute-start.11 = (f32[36,3,128]{2,1,0:T(4,128)S(1)}, f32[36,3,128]{2,1,0:T(4,128)S(1)}, u32[]{:S(2)}, u32[]{:S(2)}) collective-permute-start(f32[36,3,128]{2,1,0:T(4,128)S(1)} %get-tuple-element.76), channel_id=1, source_target_pairs={{1,0},{2,1},{3,2},{5,4},{6,5},{7,6},{9,8},{10,9},{11,10},{13,12},{... | collective-permute-start | bytes 165896 | tf_op jit(solution)/shard_map/ppermute | solution.py:380
  161.5 7.4 %collective-permute-start.10 = (f32[36,3,128]{2,1,0:T(4,128)S(1)}, f32[36,3,128]{2,1,0:T(4,128)S(1)}, u32[]{:S(2)}, u32[]{:S(2)}) collective-permute-start(f32[36,3,128]{2,1,0:T(4,128)S(1)} %get-tuple-element.75), channel_id=1, source_target_pairs={{0,1},{1,2},{2,3},{4,5},{5,6},{6,7},{8,9},{9,10},{10,11},{12,13},{... | collective-permute-start | bytes 165896 | tf_op jit(solution)/shard_map/ppermute | solution.py:380
  168.9 12.5 %sample_own.3 = f32[36,8,128]{2,1,0:T(8,128)} custom-call(s32[2]{0:T(128)} %pad_add_fusion.6.bounds_ref, s32[37]{0:T(128)} %pad_add_fusion.5.list_ref, f32[1]{0:T(128)} %bitcast.30.scale_ref, bf16[36,8,128]{2,1,0:T(8,128)(2,1)} %bitcast.155, bf16[8,384]{1,0:T(8,128)(2,1)} %select_convert_fusion.pick_ref, bf16[92,16,1536]{2,1,0:T(8,128)(2,1)} %get-tuple-element.41.fmat), custom_call_target="tpu_custom_call" | custom-call | flops 10000000000 | bytes 30000000 | tf_op jit(solution)/shard_map/sample_own/pallas_call | solution.py:345
  181.4 1.0 fusion.7
  182.3 0.1 slice_reduce_fusion
  182.5 7.6 %sort.79 = (s32[4608]{0:T(1024)}, f32[4608]{0:T(1024)S(1)}, f32[4608]{0:T(1024)S(1)}, f32[4608]{0:T(1024)S(1)}, s32[4608]{0:T(1024)}) sort(s32[4608]{0:T(1024)S(1)} %get-tuple-element.38, f32[4608]{0:T(1024)S(1)} %bitcast.162, f32[4608]{0:T(1024)S(1)} %bitcast.161, f32[4608]{0:T(1024)S(1)} %bitcast.160, s32[4608]{0:T(1024)S(1)} %iota.112), dimensions={0}, to_apply=%region_12.13 | sort | flops 59904 | bytes 184320 | tf_op jit(solution)/shard_map/sort | solution.py:470
  190.2 0.1 pad_maximum_fusion.4
  190.3 0.7 broadcast_in_dim.166
  (62 shorter events, 0.6 us)
Async XLA Ops:
  0.6 18.9 %copy-start.3 = (bf16[8]{0:T(256)(128)(2,1)S(1)}, bf16[8]{0:T(256)(128)(2,1)}, u32[]{:S(2)}) copy-start(bf16[8]{0:T(256)(128)(2,1)} %constant.246.clone.1) | copy-start | bytes 52
  3.5 9.1 %collective-permute-start.1 = (bf16[3,8,512]{2,1,0:T(8,128)(2,1)S(1)}, bf16[3,8,512]{2,1,0:T(8,128)(2,1)S(1)}, u32[]{:S(2)}, u32[]{:S(2)}) collective-permute-start(bf16[3,8,512]{2,1,0:T(8,128)(2,1)S(1)} %get-tuple-element.90), channel_id=1, source_target_pairs={{0,4},{4,8},{8,12},{12,16},{16,20},{20,24},{24,28},{28,0},{1,5},{5... | collective-permute-start | bytes 73736 | tf_op jit(solution)/shard_map/ppermute | solution.py:374
  5.6 7.0 %collective-permute-start = (bf16[3,8,512]{2,1,0:T(8,128)(2,1)S(1)}, bf16[3,8,512]{2,1,0:T(8,128)(2,1)S(1)}, u32[]{:S(2)}, u32[]{:S(2)}) collective-permute-start(bf16[3,8,512]{2,1,0:T(8,128)(2,1)S(1)} %get-tuple-element.89), channel_id=1, source_target_pairs={{0,28},{4,0},{8,4},{12,8},{16,12},{20,16},{24,20},{28,24},{1,29},{... | collective-permute-start | bytes 73736 | tf_op jit(solution)/shard_map/ppermute | solution.py:374
  12.7 6.6 %collective-permute-start.2 = (bf16[3,8,512]{2,1,0:T(8,128)(2,1)S(1)}, bf16[3,8,512]{2,1,0:T(8,128)(2,1)S(1)}, u32[]{:S(2)}, u32[]{:S(2)}) collective-permute-start(bf16[3,8,512]{2,1,0:T(8,128)(2,1)S(1)} %get-tuple-element.86), channel_id=1, source_target_pairs={{1,0},{2,1},{3,2},{5,4},{6,5},{7,6},{9,8},{10,9},{11,10},{13,12},{... | collective-permute-start | bytes 73736 | tf_op jit(solution)/shard_map/ppermute | solution.py:380
  15.5 4.0 %collective-permute-start.3 = (bf16[3,8,512]{2,1,0:T(8,128)(2,1)S(1)}, bf16[3,8,512]{2,1,0:T(8,128)(2,1)S(1)}, u32[]{:S(2)}, u32[]{:S(2)}) collective-permute-start(bf16[3,8,512]{2,1,0:T(8,128)(2,1)S(1)} %get-tuple-element.87), channel_id=1, source_target_pairs={{0,1},{1,2},{2,3},{4,5},{5,6},{6,7},{8,9},{9,10},{10,11},{12,13},{... | collective-permute-start | bytes 73736 | tf_op jit(solution)/shard_map/ppermute | solution.py:380
  27.2 8.9 %copy-start.1 = (bf16[8,36,128]{2,0,1:T(8,128)(2,1)}, bf16[8,36,128]{2,0,1:T(8,128)(2,1)S(1)}, u32[]{:S(2)}) copy-start(bf16[8,36,128]{2,0,1:T(8,128)(2,1)S(1)} %stack.123) | copy-start | bytes 221188
  27.2 31.5 %collective-permute-start.5 = (bf16[36,8,128]{2,1,0:T(8,128)(2,1)S(1)}, bf16[36,8,128]{2,1,0:T(8,128)(2,1)S(1)}, u32[]{:S(2)}, u32[]{:S(2)}) collective-permute-start(bf16[36,8,128]{2,1,0:T(8,128)(2,1)S(1)} %bitcast.150), channel_id=1, source_target_pairs={{1,0},{2,1},{3,2},{5,4},{6,5},{7,6},{9,8},{10,9},{11,10},{13,12},{... | collective-permute-start | bytes 221192 | tf_op jit(solution)/shard_map/ppermute | solution.py:380
  29.1 29.6 %collective-permute-start.4 = (bf16[36,8,128]{2,1,0:T(8,128)(2,1)S(1)}, bf16[36,8,128]{2,1,0:T(8,128)(2,1)S(1)}, u32[]{:S(2)}, u32[]{:S(2)}) collective-permute-start(bf16[36,8,128]{2,1,0:T(8,128)(2,1)S(1)} %bitcast.151), channel_id=1, source_target_pairs={{0,1},{1,2},{2,3},{4,5},{5,6},{6,7},{8,9},{9,10},{10,11},{12,13},{... | collective-permute-start | bytes 221192 | tf_op jit(solution)/shard_map/ppermute | solution.py:380
  59.6 6.4 %collective-permute-start.7 = (bf16[3,36,8,128]{3,2,1,0:T(8,128)(2,1)S(1)}, bf16[3,36,8,128]{3,2,1,0:T(8,128)(2,1)S(1)}, u32[]{:S(2)}, u32[]{:S(2)}) collective-permute-start(bf16[3,36,8,128]{3,2,1,0:T(8,128)(2,1)S(1)} %get-tuple-element.78), channel_id=1, source_target_pairs={{0,28},{4,0},{8,4},{12,8},{16,12},{20,16},{24,20},{28,24},{1,29},{... | collective-permute-start | bytes 663560 | tf_op jit(solution)/shard_map/ppermute | solution.py:374
  61.8 7.5 %collective-permute-start.6 = (bf16[3,36,8,128]{3,2,1,0:T(8,128)(2,1)S(1)}, bf16[3,36,8,128]{3,2,1,0:T(8,128)(2,1)S(1)}, u32[]{:S(2)}, u32[]{:S(2)}) collective-permute-start(bf16[3,36,8,128]{3,2,1,0:T(8,128)(2,1)S(1)} %get-tuple-element.78), channel_id=1, source_target_pairs={{0,4},{4,8},{8,12},{12,16},{16,20},{20,24},{24,28},{28,0},{1,5},{5... | collective-permute-start | bytes 663560 | tf_op jit(solution)/shard_map/ppermute | solution.py:374
  69.4 4.2 %copy-start = (bf16[3,3,36,8,128]{4,3,2,1,0:T(8,128)(2,1)}, bf16[3,3,36,8,128]{4,3,2,1,0:T(8,128)(2,1)S(1)}, u32[]{:S(2)}) copy-start(bf16[3,3,36,8,128]{4,3,2,1,0:T(8,128)(2,1)S(1)} %pad_maximum_fusion.1) | copy-start | bytes 1990660
  145.4 13.9 %collective-permute-start.9 = (f32[3,36,3,128]{3,2,1,0:T(4,128)S(1)}, f32[3,36,3,128]{3,2,1,0:T(4,128)S(1)}, u32[]{:S(2)}, u32[]{:S(2)}) collective-permute-start(f32[3,36,3,128]{3,2,1,0:T(4,128)S(1)} %bitcast.159), channel_id=1, source_target_pairs={{0,28},{4,0},{8,4},{12,8},{16,12},{20,16},{24,20},{28,24},{1,29},{... | collective-permute-start | bytes 497672 | tf_op jit(solution)/shard_map/ppermute | solution.py:374
  147.3 12.0 %collective-permute-start.8 = (f32[3,36,3,128]{3,2,1,0:T(4,128)S(1)}, f32[3,36,3,128]{3,2,1,0:T(4,128)S(1)}, u32[]{:S(2)}, u32[]{:S(2)}) collective-permute-start(f32[3,36,3,128]{3,2,1,0:T(4,128)S(1)} %bitcast.157), channel_id=1, source_target_pairs={{0,4},{4,8},{8,12},{12,16},{16,20},{20,24},{24,28},{28,0},{1,5},{5... | collective-permute-start | bytes 497672 | tf_op jit(solution)/shard_map/ppermute | solution.py:374
  159.5 21.8 %collective-permute-start.11 = (f32[36,3,128]{2,1,0:T(4,128)S(1)}, f32[36,3,128]{2,1,0:T(4,128)S(1)}, u32[]{:S(2)}, u32[]{:S(2)}) collective-permute-start(f32[36,3,128]{2,1,0:T(4,128)S(1)} %get-tuple-element.76), channel_id=1, source_target_pairs={{1,0},{2,1},{3,2},{5,4},{6,5},{7,6},{9,8},{10,9},{11,10},{13,12},{... | collective-permute-start | bytes 165896 | tf_op jit(solution)/shard_map/ppermute | solution.py:380
  161.4 19.9 %copy-start.2 = (f32[36,8,128]{2,1,0:T(8,128)S(1)}, f32[36,8,128]{2,1,0:T(8,128)}, u32[]{:S(2)}) copy-start(f32[36,8,128]{2,1,0:T(8,128)} %sample_own.2) | copy-start | bytes 442372
  161.5 19.9 %collective-permute-start.10 = (f32[36,3,128]{2,1,0:T(4,128)S(1)}, f32[36,3,128]{2,1,0:T(4,128)S(1)}, u32[]{:S(2)}, u32[]{:S(2)}) collective-permute-start(f32[36,3,128]{2,1,0:T(4,128)S(1)} %get-tuple-element.75), channel_id=1, source_target_pairs={{0,1},{1,2},{2,3},{4,5},{5,6},{6,7},{8,9},{9,10},{10,11},{12,13},{... | collective-permute-start | bytes 165896 | tf_op jit(solution)/shard_map/ppermute | solution.py:380

commit v4 on v3

v4 whole, which is shorter than its diff:
```python
import jax
import jax.numpy as jnp
import numpy as np
from jax import lax
from jax.experimental import pallas as pl
from jax.experimental.pallas import tpu as pltpu
from jax.sharding import PartitionSpec as P

CX = 64
CY = 16
NZ = 512
REACH = 6
TILE = 128
BX = 8
XO = 8
XROWS = 84
BUCKETS = 10
FROWS = 92
BP = BX * CY

spread_width = 12.5


OFFSETS = np.arange(-6, 7).astype(np.float32)
RAW = np.exp(-OFFSETS * OFFSETS / np.float32(spread_width))
SCALE = np.float32(1.0) / np.sum(RAW)
UNIT = RAW * SCALE
PICK = np.zeros((8, 384), np.float32)
PICK[6, :128], PICK[7, :128], PICK[5, 128:256], PICK[4, 256:] = 16.0, 1.0, 1.0, 1.0


def gauss(d):
    return jnp.where(jnp.abs(d) < REACH + 0.5, jnp.exp(d * d * (-1.0 / spread_width)), 0.0)


def hi_lo(v):
    hi = v.astype(jnp.bfloat16)
    lo = (v - hi.astype(jnp.float32)).astype(jnp.bfloat16)
    return hi, lo


def columns(xt, pick):
    return lax.dot_general(
        xt.astype(jnp.bfloat16), pick, (((0,), (0,)), ((), ())), preferred_element_type=jnp.float32
    )


def x_filtered(load, taps, count):
    taps = [float(t) for t in taps]
    outs = []
    ins = [load(i) for i in range(count + 12)]
    for o in range(count):
        total = taps[6] * ins[o + 6]
        for k in range(1, 7):
            total = total + taps[6 + k] * (ins[o + 6 - k] + ins[o + 6 + k])
        outs.append(total)
    return outs


def tile_codes(list_ref, k):
    code = list_ref[k + 2]
    i = code >> 14
    per = list_ref[0]
    n = jnp.where(per == 0, 4, lax.div(i, jnp.maximum(per, 1)))
    return i, n, (code >> 7) & 127, code & 127


def in_pairs(list_ref, part, width, visit):
    count = list_ref[1]
    middle = (count + 1) // 2
    begin = middle if part == 2 else 0
    end = middle if part == 1 else count

    def pair(p, _):
        k = begin + 2 * p
        visit([tile_codes(list_ref, k)[:3], tile_codes(list_ref, jnp.minimum(k + 1, end - 1))[:3]], k + 1 < end)

        def leftover(t, _):
            i, n, first, last = tile_codes(list_ref, k + t)

            def window(w, _):
                visit([(i, n, first + w * width)], None)
                return 0

            lax.fori_loop(1, (last - first) // width + 1, window, 0)
            return 0

        lax.fori_loop(0, jnp.minimum(end - k, 2), leftover, 0)
        return 0

    lax.fori_loop(0, (end - begin + 1) // 2, pair, 0)


def framed(tab_ref, i, n):
    xt = tab_ref[i].astype(jnp.float32)
    row, col = lax.div(n, 3), lax.rem(n, 3)
    sx = ((row - 1) * CX + REACH).astype(jnp.float32)
    sy = ((col - 1) * CY).astype(jnp.float32)
    return xt, sx, sy


def accumulate(list_ref, tab_ref, pick_ref, acc, amats, zmats):
    def factors(i, n, x0, amat, zmat, keep):
        xt, sx, sy = framed(tab_ref, i, n)
        zrep = columns(xt, pick_ref[:, 0:128])
        lane = lax.broadcasted_iota(jnp.int32, (TILE, 128), 1).astype(jnp.float32)
        for q in range(NZ // 128):
            hit = jnp.where(lane + (128.0 * q) == zrep, 1.0, 0.0).astype(jnp.bfloat16)
            cols = slice(128 * q, 128 * (q + 1))
            zmat[0:TILE, cols] = hit
            zmat[TILE : 2 * TILE, cols] = hit
        ypl = lax.broadcasted_iota(jnp.int32, (CY, TILE), 0).astype(jnp.float32)
        gy = gauss(ypl - (xt[5:6, :] + sy))
        if keep is not None:
            gy = jnp.where(keep, gy, 0.0)
        xrow = jnp.broadcast_to(xt[4:5, :] + sx, (CY, TILE))
        parts = [hi_lo(gy * xt[c : c + 1, :]) for c in range(4)]
        for xx in range(BX):
            m = jnp.where(xrow == (x0 + xx).astype(jnp.float32), 1.0, 0.0).astype(jnp.bfloat16)
            for c in range(4):
                rows = slice((xx * 4 + c) * CY, (xx * 4 + c + 1) * CY)
                amat[rows, 0:TILE] = parts[c][0] * m
                amat[rows, TILE : 2 * TILE] = parts[c][1] * m

    def visit(entries, second):
        for j, (i, n, x0) in enumerate(entries):
            factors(i, n, x0, amats[j], zmats[j], second if j == 1 else None)
        for j, (i, n, x0) in enumerate(entries):
            part = jnp.dot(amats[j][...], zmats[j][...], preferred_element_type=jnp.float32)
            acc[pl.ds(x0, BX)] += part.reshape(BX, 4 * CY, NZ)

    in_pairs(list_ref, 0, BX, visit)


def spread_own_kernel(list_ref, tab_ref, pick_ref, acc, amat_a, amat_b, zmat_a, zmat_b):
    def clear(i, _):
        acc[i] = jnp.zeros(acc.shape[1:], jnp.float32)
        return 0

    lax.fori_loop(0, XROWS, clear, 0)
    accumulate(list_ref, tab_ref, pick_ref, acc, (amat_a, amat_b), (zmat_a, zmat_b))


def sampled(list_ref, part, tab_ref, pick_ref, fmat, out_ref):
    scale = float(SCALE)
    out_ref[...] = jnp.zeros(out_ref.shape, jnp.float32)

    def contribution(i, n, x0):
        xt, sx, sy = framed(tab_ref, i, n)
        cols = columns(xt, pick_ref[...])
        xrep, yrep, zrep = (cols[:, 128 * k : 128 * (k + 1)] for k in (2, 1, 0))
        lane_i = lax.broadcasted_iota(jnp.int32, (TILE, 128), 1)
        lane = lane_i.astype(jnp.float32)
        xpl = (lane_i // CY).astype(jnp.float32)
        ypl = (lane_i % CY).astype(jnp.float32)
        wy = gauss(ypl - (yrep + sy)) * scale
        xoff = xrep - xpl
        lhs, rhs = [], []
        for k in range(2):
            a = jnp.where(xoff == (x0 + k * BX).astype(jnp.float32) - sx, wy, 0.0)
            lhs.extend(hi_lo(a))
            f = fmat[pl.ds(x0 + k * BX, BX)].reshape(BP, 3 * NZ)
            rhs.extend([f, f])
        g = jnp.dot(jnp.concatenate(lhs, axis=1), jnp.concatenate(rhs, axis=0), preferred_element_type=jnp.float32)
        sums = [None] * 3
        for q in range(NZ // 128):
            wz = gauss(lane + (128.0 * q) - zrep) * scale
            for c in range(3):
                t = g[:, c * NZ + 128 * q : c * NZ + 128 * (q + 1)] * wz
                sums[c] = t if sums[c] is None else sums[c] + t
        return [jnp.sum(v.T, axis=0, keepdims=True) for v in sums]

    def visit(entries, second):
        got = [contribution(*e) for e in entries]
        for (i, n, x0), rows in zip(entries, got):
            for c in range(3):
                if second is None:
                    out_ref[i, c : c + 1, :] += rows[c]
                else:
                    out_ref[i, c : c + 1, :] = rows[c]

    in_pairs(list_ref, part, 2 * BX, visit)


def main_kernel(
    units_ref,
    list_ref,
    tab_ref,
    pick_ref,
    field_ref,
    ground_ref,
    old_ref,
    acc,
    dens_ref,
    out_ref,
    fmat,
    amat_a,
    amat_b,
    zmat_a,
    zmat_b,
    wide_a,
    wide_b,
    band_ref,
    flow,
):
    step = pl.program_id(0)
    steps = CX // XO

    def filtered(b, wide, chans=(0, 1, 2, 3)):
        base = b * XO
        for q in range(NZ // 128):
            cols = slice(q * 128, (q + 1) * 128)
            for c in chans:
                outs = x_filtered(lambda i: acc[base + i, c * CY : (c + 1) * CY, cols], RAW, XO)
                for o in range(XO):
                    hi, lo = hi_lo(outs[o])
                    rows = slice((c * XO + o) * CY, (c * XO + o + 1) * CY)
                    wide[0, rows, cols] = hi
                    wide[1, rows, cols] = lo

    def finish(b, wide, h):
        cols = slice(h * 256, (h + 1) * 256)
        full = jnp.concatenate([wide[0], wide[0], wide[1]], axis=1)
        dens = jnp.dot(full, band_ref[:, cols], preferred_element_type=jnp.float32)
        dens = dens.reshape(4, XO, CY, 256)
        dens_ref[3, :, :, cols] = dens[3]
        for c in range(3):
            d = dens[c] + dens[3] * field_ref[c : c + 1, cols][None]
            dens_ref[c, :, :, cols] = d
            flow[c, pl.ds(12 + b * XO, XO), :, cols] = d + ground_ref[c : c + 1, cols][None]

    @pl.when(step == 0)
    def _():
        def clear(i, _):
            flow[:, i] = jnp.zeros((3, CY, NZ), jnp.float32)
            flow[:, 12 + CX + i] = jnp.zeros((3, CY, NZ), jnp.float32)
            return 0

        lax.fori_loop(0, 16, clear, 0)
        for i in range(BUCKETS * BX, FROWS):
            fmat[i] = jnp.zeros(fmat.shape[1:], jnp.bfloat16)
        for q in range(NZ // 128):
            row = lax.broadcasted_iota(jnp.int32, (128, NZ), 0) + 128 * q
            col = lax.broadcasted_iota(jnp.int32, (128, NZ), 1)
            hi, lo = hi_lo(gauss((row - col).astype(jnp.float32)))
            band_ref[q * 128 : (q + 1) * 128, :] = hi
            band_ref[NZ + q * 128 : NZ + (q + 1) * 128, :] = lo
            band_ref[2 * NZ + q * 128 : 2 * NZ + (q + 1) * 128, :] = hi
        accumulate(units_ref, tab_ref, pick_ref, acc, (amat_a, amat_b), (zmat_a, zmat_b))
        filtered(0, wide_a)

    for parity, now, later in ((1, wide_a, wide_b), (0, wide_b, wide_a)):

        @pl.when((step > 0) & (step <= steps) & (step % 2 == parity))
        def _(now=now, later=later):
            ahead = jnp.minimum(step, steps - 1)
            finish(step - 1, now, 0)
            filtered(ahead, later, (0, 1))
            finish(step - 1, now, 1)
            filtered(ahead, later, (2, 3))

    @pl.when(step > steps)
    def _():
        def block(b, _):
            for c in range(3):

                def chunk(j, _, c=c):
                    cols = pl.ds(pl.multiple_of(j * 128, 128), 128)
                    dest = pl.ds(pl.multiple_of(c * NZ + j * 128, 128), 128)
                    outs = x_filtered(lambda i: flow[c, b * BX + i, :, cols], UNIT, BX)
                    for o in range(BX):
                        fmat[b * BX + o, :, dest] = outs[o].astype(jnp.bfloat16)
                    return 0

                lax.fori_loop(0, NZ // 128, chunk, 0)
            return 0

        lax.fori_loop(0, BUCKETS, block, 0)
        sampled(list_ref, 0, tab_ref, pick_ref, fmat, out_ref)


def sample_own_kernel(part, list_ref, tab_ref, pick_ref, fmat, out_ref):
    sampled(list_ref, part, tab_ref, pick_ref, fmat, out_ref)


def smem():
    return pl.BlockSpec(memory_space=pltpu.SMEM)


def whole(shape):
    return pl.BlockSpec(shape, lambda i: (0,) * len(shape))


PARAMS = pltpu.CompilerParams(vmem_limit_bytes=16 << 20)
MAIN_PARAMS = pltpu.CompilerParams(vmem_limit_bytes=32 << 20)


def factor_scratch():
    return [pltpu.VMEM((4 * BP, 2 * TILE), jnp.bfloat16)] * 2 + [pltpu.VMEM((2 * TILE, NZ), jnp.bfloat16)] * 2


def spread_own_call(listing, table, pick):
    return pl.pallas_call(
        spread_own_kernel,
        grid=(1,),
        in_specs=[smem(), whole(table.shape), whole(pick.shape)],
        out_specs=pl.BlockSpec(memory_space=pltpu.VMEM),
        out_shape=pltpu.VMEM((XROWS, 4 * CY, NZ), jnp.float32),
        scratch_shapes=factor_scratch(),
        compiler_params=PARAMS,
        cost_estimate=pl.CostEstimate(flops=10**10, transcendentals=0, bytes_accessed=3 * 10**7),
        name="spread_own",
    )(listing, table, pick)


def main_call(units, listing, table, pick, field, ground, old):
    steps = CX // XO
    n = table.shape[0]
    fshape = (FROWS, CY, 3 * NZ)
    return pl.pallas_call(
        main_kernel,
        grid=(steps + 2,),
        in_specs=[smem()] * 2
        + [whole(v.shape) for v in (table, pick, field, ground)]
        + [pl.BlockSpec(memory_space=pltpu.VMEM)],
        out_specs=[
            pl.BlockSpec(memory_space=pltpu.VMEM),
            pl.BlockSpec((4, XO, CY, NZ), lambda i: (0, jnp.clip(i - 1, 0, steps - 1), 0, 0)),
            whole((n, 8, TILE)),
            whole(fshape),
        ],
        input_output_aliases={6: 0},
        out_shape=[
            pltpu.VMEM(old.shape, jnp.float32),
            jax.ShapeDtypeStruct((4, CX, CY, NZ), jnp.float32),
            jax.ShapeDtypeStruct((n, 8, TILE), jnp.float32),
            jax.ShapeDtypeStruct(fshape, jnp.bfloat16),
        ],
        scratch_shapes=factor_scratch()
        + [
            pltpu.VMEM((2, 4 * XO * CY, NZ), jnp.bfloat16),
            pltpu.VMEM((2, 4 * XO * CY, NZ), jnp.bfloat16),
            pltpu.VMEM((3 * NZ, NZ), jnp.bfloat16),
            pltpu.VMEM((3, BUCKETS * BX + 12, CY, NZ), jnp.float32),
        ],
        compiler_params=MAIN_PARAMS,
        cost_estimate=pl.CostEstimate(flops=4 * 10**10, transcendentals=0, bytes_accessed=6 * 10**7),
        name="main",
    )(units, listing, table, pick, field, ground, old)


def sample_own_call(part, listing, table, pick, fmat):
    n = table.shape[0]

    def kernel(*refs):
        sample_own_kernel(part, *refs)

    return pl.pallas_call(
        kernel,
        grid=(1,),
        in_specs=[smem(), whole(table.shape), whole(pick.shape), whole(fmat.shape)],
        out_specs=whole((n, 8, TILE)),
        out_shape=jax.ShapeDtypeStruct((n, 8, TILE), jnp.float32),
        compiler_params=PARAMS,
        cost_estimate=pl.CostEstimate(flops=10**10, transcendentals=0, bytes_accessed=3 * 10**7),
        name="sample_own",
    )(listing, table, pick, fmat)


def reached(x, y, exists, sx, sy):
    ax, ay = x + sx, y + sy
    near = (ax >= 0) & (ax < CX + 2 * REACH) & (ay >= -REACH) & (ay < CY + REACH) & exists
    lo = jnp.min(jnp.where(near, ax, 127), axis=-1).reshape(-1)
    hi = jnp.max(jnp.where(near, ax, -1), axis=-1).reshape(-1)
    return lo, hi


def listed(at, lo, hi, per):
    active = lo <= hi
    k = jnp.arange(lo.shape[0] + 2, dtype=jnp.int32)
    i = k[:-2]
    pos = jnp.sum((i[None, :] < i[:, None]) & active[None, :], axis=1, dtype=jnp.int32)
    code = jnp.where(active, (at * 128 + lo) * 128 + hi, 0)
    spot = jnp.where(active, pos + 2, -1)
    grid = jnp.where(spot[None, :] == k[:, None], code[None, :], 0)
    grid = jnp.where(k[:, None] == 1, active[None, :].astype(jnp.int32), grid)
    return jnp.sum(grid, axis=1) + jnp.where(k == 0, per, 0)


def both_lists(lo, hi, per):
    at = jnp.arange(lo.shape[0], dtype=jnp.int32)
    split = listed(
        jnp.concatenate([at, at]),
        jnp.concatenate([lo, lo + BX]),
        jnp.concatenate([jnp.minimum(hi, lo + BX - 1), hi]),
        per,
    )
    return split, listed(at, lo, hi, per)


def ring(value, steps):
    count = lax.axis_size("stream")
    return lax.ppermute(value, "stream", [(i, (i + steps) % count) for i in range(count)])


def line(value, steps):
    count = lax.axis_size("span")
    first, last = max(0, -steps), min(count, count - steps)
    return lax.ppermute(value, "span", [(i, i + steps) for i in range(first, last)])


def on_device(records, cells, counts, background, field):
    cap = records.shape[3]
    total = 9 * cap
    tiles = total // TILE
    bf16, f32 = jnp.bfloat16, jnp.float32
    slots = jnp.arange(cap, dtype=jnp.int32)
    live = slots[None, :] < counts[0][:, None]
    cell = cells[0]
    z = cell % NZ
    x = jnp.where(live, cell // (CY * NZ), 255)
    y = (cell // NZ) % CY
    row = jnp.arange(8)[None, :, None]
    places = jnp.where(row == 4, x[:, None], jnp.where(row == 5, y[:, None], jnp.where(row == 6, z[:, None] // 16, z[:, None] % 16)))
    outgoing = jnp.where(row < 4, jnp.pad(records[0], ((0, 0), (0, 4), (0, 0))), places.astype(bf16))
    outgoing = outgoing.reshape(3, 3, 8, cap)
    dead = jnp.zeros((8,), bf16).at[4].set(255)[:, None]
    outgoing = jnp.stack([ring(outgoing[0], -1), outgoing[1], ring(outgoing[2], 1)])
    me = lax.axis_index("span")
    spans = lax.axis_size("span")
    has_low, has_high = me > 0, me < spans - 1
    from_high = jnp.where(has_high, line(outgoing[:, 0], -1), dead)
    from_low = jnp.where(has_low, line(outgoing[:, 2], 1), dead)
    inbound = jnp.stack([from_high, outgoing[:, 1], from_low], axis=1)
    inbound = inbound.transpose(2, 0, 1, 3).reshape(8, total)

    gi = inbound[4:].astype(jnp.int32)
    gx, gy, gz = gi[0], gi[1], gi[2] * 16 + gi[3]
    klass = (gy >= REACH).astype(jnp.int32) + (gy >= CY - REACH)
    klass = jnp.where(gx > 200, 3, klass)
    kx = jnp.where(klass == 1, CX - 1 - gx, gx)
    key = ((klass * 256 + kx) * CY + gy) * NZ + gz
    order = jnp.arange(total, dtype=jnp.int32)
    key, order, *vals = lax.sort((key, order) + tuple(inbound[c].astype(f32) for c in range(4)), num_keys=1)
    sz = key % NZ
    sy = key // NZ % CY
    sx = key // (CY * NZ) % 256
    sx = jnp.where(key // (CY * NZ * 256) == 1, CX - 1 - sx, sx)
    packed = jnp.stack(vals + [v.astype(f32) for v in (sx, sy, sz // 16, sz % 16)]).astype(bf16)
    packed = packed.reshape(8, tiles, TILE).transpose(1, 0, 2)

    low = line(packed, 1)
    high = line(packed, -1)
    tx, ty = sx.reshape(tiles, TILE), sy.reshape(tiles, TILE)
    own_units, own_list = both_lists(*reached(tx, ty, tx < 200, REACH, 0), 0)
    three, own_units = lax.optimization_barrier((jnp.stack([low, packed, high]), own_units))
    arrays = jnp.stack([ring(three, 1), three, ring(three, -1)])
    places = arrays[:, :, :, 4:6].astype(jnp.int32)
    shift = jnp.arange(-1, 2, dtype=jnp.int32)
    exists = jnp.stack([has_low, jnp.array(True), has_high])
    exists = exists[None, :] & ~((shift[:, None] == 0) & (shift[None, :] == 0))
    lo, hi = reached(
        places[:, :, :, 0],
        places[:, :, :, 1],
        exists[:, :, None, None],
        CX * shift[:, None, None, None] + REACH,
        CY * shift[None, :, None, None],
    )
    rest_units, rest_list = both_lists(lo, hi, tiles)
    table = arrays.reshape(9 * tiles, 8, TILE)

    pick = jnp.asarray(PICK, bf16)
    half = spread_own_call(own_units, packed, pick)
    _, density, partial, fmat = main_call(rest_units, rest_list, table, pick, field, background, half)
    early = sample_own_call(1, own_list, packed, pick, fmat)
    partial = partial[:, :3].reshape(3, 3, tiles, 3, TILE)
    mixed = partial[1] + ring(partial[2], 1) + ring(partial[0], -1)
    mixed, own_list = lax.optimization_barrier((mixed, own_list))
    late = sample_own_call(2, own_list, packed, pick, fmat)
    mine = (early + late)[:, :3]
    own = mixed[1] + mine + line(mixed[2], 1) + line(mixed[0], -1)
    own = own.transpose(1, 0, 2).reshape(3, total)
    _, *vel = lax.sort((order, own[0], own[1], own[2]), num_keys=1)
    velocity = jnp.stack([v.reshape(9, cap) for v in vel], axis=1)[None]
    return density, velocity


def solution(mesh):
    return jax.shard_map(
        on_device,
        mesh=mesh,
        in_specs=(
            P(("stream", "span"), None, None, None),
            P(("stream", "span"), None, None),
            P(("stream", "span"), None),
            P(),
            P(),
        ),
        out_specs=(P(None, "stream", "span", None), P(("stream", "span"), None, None, None)),
        check_vma=False,
    )
```

time: 192 us -> 156 us (0.81)
  Pallas kernels: 117 us -> 82.6 us
  other arithmetic: 30.7 us -> 20.4 us
  local copies, waits for them, and re-layouts: 4.13 us -> 10.2 us
  waiting for transfers between devices: 5.89 us -> 8.96 us
    pallas_call x4, Pallas kernels: 117 us -> 82.6 us  [the longest x1 52.3 us: main_call(): pl.pallas_call(main_kernel, grid=(steps + 2,), in_specs=[smem()] * 2 + [w...]
    unnamed x8 -> x10, local copies, waits for them, and re-layouts: 0.02 us -> 8.3 us
    another operation x7 -> x1, other arithmetic: 6.96 us -> 0.03 us  [on_device(): jnp.stack([low, packed, high])]
    ppermute x6, starting transfers between devices: 9.38 us -> 13.6 us  [ring(): lax.ppermute(value, 'stream', [(i, (i + steps) % count) for i in range(co...]
    ppermute x6, waiting for transfers between devices: 0.37 us -> 3.78 us  [line(): lax.ppermute(value, 'span', [(i, i + steps) for i in range(first, last)])]
    ppermute x6, starting transfers between devices: 21.5 us -> 18.1 us  [line(): lax.ppermute(value, 'span', [(i, i + steps) for i in range(first, last)])]
    concatenate x3 -> x0, other arithmetic: 2.52 us -> none  [the longest x1 1.26 us: on_device(): jnp.concatenate([coarse, exact - coarse, coarse], axis=0).astype(bf16)]
  transfers between devices with their start and end apart: 12 -> 12, of which waited for: 3 -> 4; matrix products, arithmetic and copies ran while one was open for 4% -> 1% of each run, Pallas kernels for 24% -> 20%
where the time goes in v4:
time: 156 us; the launch traced here: 155 us
  Pallas kernels  82.6 us (53%)
  starting transfers between devices  31.7 us (20%)
  other arithmetic  20.4 us (13%)
  local copies, waits for them, and re-layouts  10.2 us (7%)
  waiting for transfers between devices  8.96 us (6%)
    pallas_call x1, Pallas kernels, main_call(): pl.pallas_call(main_kernel, grid=(steps + 2,), in_specs=[smem()] * 2 + [w...  52.3 us
    ppermute x6, starting transfers between devices, line(): lax.ppermute(value, 'span', [(i, i + steps) for i in range(first, last)])  18.1 us
    pallas_call x1, Pallas kernels, spread_own_call(): pl.pallas_call(spread_own_kernel, grid=(1,), in_specs=[smem(), whole(tabl...  15.4 us
    pallas_call x2, Pallas kernels, sample_own_call(): pl.pallas_call(kernel, grid=(1,), in_specs=[smem(), whole(table.shape), w...  14.9 us
    ppermute x6, starting transfers between devices, ring(): lax.ppermute(value, 'stream', [(i, (i + steps) % count) for i in range(co...  13.6 us
    unnamed x10, local copies, waits for them, and re-layouts  8.3 us
    sort x1, other arithmetic, on_device(): _, *vel = lax.sort((order, own[0], own[1], own[2]), num_keys=1)  7.64 us
    sort x5, other arithmetic, on_device(): lax.sort((key, order) + tuple((inbound[c].astype(f32) for c in range(4)))...  6.36 us
  transfers between devices with their start and end apart: 12, of which 4 were waited for; matrix products, arithmetic and copies ran while one was open for 1% of the time, Pallas kernels for 20%

profile of v4, /device:TPU:1, one launch (start us, length us, event | category | flops | bytes accessed | tf_op | source)
XLA Modules:
  0.0 155.2 jit_solution(17263596602816694557)
XLA Ops:
  0.6 0.0 copy-start.2
  0.7 0.8 fusion.7
  1.5 0.9 fusion.1
  2.4 5.2 %collective-permute-start = (bf16[3,8,512]{2,1,0:T(8,128)(2,1)S(1)}, bf16[3,8,512]{2,1,0:T(8,128)(2,1)S(1)}, u32[]{:S(2)}, u32[]{:S(2)}) collective-permute-start(bf16[3,8,512]{2,1,0:T(8,128)(2,1)S(1)} %get-tuple-element.96), channel_id=1, source_target_pairs={{0,28},{4,0},{8,4},{12,8},{16,12},{20,16},{24,20},{28,24},{1,29},{... | collective-permute-start | bytes 73736 | tf_op jit(solution)/shard_map/ppermute | solution.py:403
  7.5 0.0 collective-permute-start.1
  7.6 0.1 pad_add_fusion.2
  7.6 0.1 not_and_fusion
  7.7 0.7 collective-permute-done
  8.5 4.4 %collective-permute-done.1 = bf16[3,8,512]{2,1,0:T(8,128)(2,1)S(1)} collective-permute-done((bf16[3,8,512]{2,1,0:T(8,128)(2,1)S(1)}, bf16[3,8,512]{2,1,0:T(8,128)(2,1)S(1)}, u32[]{:S(2)}, u32[]{:S(2)}) %collective-permute-start.1) | collective-permute-done | bytes 24608 | tf_op jit(solution)/shard_map/ppermute | solution.py:403
  12.9 4.0 %collective-permute-start.2 = (bf16[3,8,512]{2,1,0:T(8,128)(2,1)S(1)}, bf16[3,8,512]{2,1,0:T(8,128)(2,1)S(1)}, u32[]{:S(2)}, u32[]{:S(2)}) collective-permute-start(bf16[3,8,512]{2,1,0:T(8,128)(2,1)S(1)} %get-tuple-element.93), channel_id=1, source_target_pairs={{1,0},{2,1},{3,2},{5,4},{6,5},{7,6},{9,8},{10,9},{11,10},{13,12},{... | collective-permute-start | bytes 73736 | tf_op jit(solution)/shard_map/ppermute | solution.py:409
  17.0 3.0 %collective-permute-start.3 = (bf16[3,8,512]{2,1,0:T(8,128)(2,1)S(1)}, bf16[3,8,512]{2,1,0:T(8,128)(2,1)S(1)}, u32[]{:S(2)}, u32[]{:S(2)}) collective-permute-start(bf16[3,8,512]{2,1,0:T(8,128)(2,1)S(1)} %get-tuple-element.94), channel_id=1, source_target_pairs={{0,1},{1,2},{2,3},{4,5},{5,6},{6,7},{8,9},{9,10},{10,11},{12,13},{... | collective-permute-start | bytes 73736 | tf_op jit(solution)/shard_map/ppermute | solution.py:409
  20.0 0.0 collective-permute-done.2
  20.0 0.9 collective-permute-done.3
  20.9 0.7 select_bitcast_fusion.1
  21.7 0.1 slice_convert_fusion.2
  21.8 0.1 fusion.61
  22.1 6.3 %sort.78 = (s32[4608]{0:T(1024)S(1)}, s32[4608]{0:T(1024)S(1)}, f32[4608]{0:T(1024)S(1)}, f32[4608]{0:T(1024)S(1)}, f32[4608]{0:T(1024)S(1)}, /*index=5*/f32[4608]{0:T(1024)S(1)}) sort(s32[4608]{0:T(1024)S(1)} %fusion.18, s32[4608]{0:T(1024)S(1)} %iota.121, f32[4608]{0:T(1024)S(1)} %reshape.729, f32[4608]{0:T(1024)S(1)} %reshape.730, f32[4608]{0:T(1024)S(1)} %reshape.731, ...), dimensions={0}, to_apply=%region_0.1 | sort | flops 59904 | bytes 221184 | tf_op jit(solution)/shard_map/sort | solution.py:444
  28.4 0.2 fusion.28
  28.9 0.2 stack.95
  29.2 4.2 %collective-permute-start.4 = (bf16[36,8,128]{2,1,0:T(8,128)(2,1)S(1)}, bf16[36,8,128]{2,1,0:T(8,128)(2,1)S(1)}, u32[]{:S(2)}, u32[]{:S(2)}) collective-permute-start(bf16[36,8,128]{2,1,0:T(8,128)(2,1)S(1)} %bitcast.161), channel_id=1, source_target_pairs={{0,1},{1,2},{2,3},{4,5},{5,6},{6,7},{8,9},{9,10},{10,11},{12,13},{... | collective-permute-start | bytes 221192 | tf_op jit(solution)/shard_map/ppermute | solution.py:409
  33.4 1.9 %collective-permute-start.5 = (bf16[36,8,128]{2,1,0:T(8,128)(2,1)S(1)}, bf16[36,8,128]{2,1,0:T(8,128)(2,1)S(1)}, u32[]{:S(2)}, u32[]{:S(2)}) collective-permute-start(bf16[36,8,128]{2,1,0:T(8,128)(2,1)S(1)} %bitcast.162), channel_id=1, source_target_pairs={{1,0},{2,1},{3,2},{5,4},{6,5},{7,6},{9,8},{10,9},{11,10},{13,12},{... | collective-permute-start | bytes 221192 | tf_op jit(solution)/shard_map/ppermute | solution.py:409
  35.3 0.2 convert_reduce_fusion.3
  35.5 0.1 fusion.57
  35.6 0.2 convert_reduce_fusion.2
  35.8 0.1 add_select_fusion.21
  35.9 0.1 select_reduce_fusion.4.list_ref
  36.0 0.2 select_reduce_fusion.5.refs_0_
  36.2 0.0 collective-permute-done.4
  36.2 2.9 %collective-permute-done.5 = bf16[36,8,128]{2,1,0:T(8,128)(2,1)S(1)} collective-permute-done((bf16[36,8,128]{2,1,0:T(8,128)(2,1)S(1)}, bf16[36,8,128]{2,1,0:T(8,128)(2,1)S(1)}, u32[]{:S(2)}, u32[]{:S(2)}) %collective-permute-start.5) | collective-permute-done | bytes 73760 | tf_op jit(solution)/shard_map/ppermute | solution.py:409
  39.1 0.1 collective-permute-start.6
  39.1 4.1 %collective-permute-start.7 = (bf16[3,36,8,128]{3,2,1,0:T(8,128)(2,1)S(1)}, bf16[3,36,8,128]{3,2,1,0:T(8,128)(2,1)S(1)}, u32[]{:S(2)}, u32[]{:S(2)}) collective-permute-start(bf16[3,36,8,128]{3,2,1,0:T(8,128)(2,1)S(1)} %pad_maximum_fusion.1), channel_id=1, source_target_pairs={{0,28},{4,0},{8,4},{12,8},{16,12},{20,16},{24,20},{28,24},{1,29},{... | collective-permute-start | bytes 663560 | tf_op jit(solution)/shard_map/ppermute | solution.py:403
  43.3 15.4 %spread_own.1.old_ref = f32[84,64,512]{2,1,0:T(8,128)S(1)} custom-call(s32[74]{0:T(128)S(1)} %select_reduce_fusion.4.list_ref, bf16[36,8,128]{2,1,0:T(8,128)(2,1)S(1)} %bitcast.164, bf16[8,384]{1,0:T(8,128)(2,1)S(1)} %copy-done.2), custom_call_target="tpu_custom_call" | custom-call | flops 10000000000 | bytes 30000000 | tf_op jit(solution)/shard_map/spread_own/pallas_call | solution.py:303
  58.7 4.2 %copy-done.3 = f32[84,64,512]{2,1,0:T(8,128)} copy-done((f32[84,64,512]{2,1,0:T(8,128)}, f32[84,64,512]{2,1,0:T(8,128)S(1)}, u32[]{:S(2)}) %copy-start.3) | copy-done | bytes 11010072
  62.9 0.0 collective-permute-done.6
  62.9 0.0 collective-permute-done.7
  62.9 0.1 pad_maximum_fusion
  63.0 0.3 slice_convert_fusion
  63.3 0.3 fusion.60
  63.5 0.5 select_reduce_fusion.3
  64.0 0.1 concatenate.99
  64.1 0.1 reshape.727
  64.2 0.2 convert_reduce_fusion.1
  64.4 0.2 select_reduce_fusion.1
  64.7 0.1 fusion.55
  64.8 0.4 convert_reduce_fusion
  65.2 0.1 add_select_fusion.15
  65.3 0.4 select_reduce_fusion
  65.7 4.1 %copy-done.4 = f32[84,64,512]{2,1,0:T(8,128)S(1)} copy-done((f32[84,64,512]{2,1,0:T(8,128)S(1)}, f32[84,64,512]{2,1,0:T(8,128)}, u32[]{:S(2)}) %copy-start.4) | copy-done | bytes 11010072
  69.9 52.3 %main.1 = (f32[84,64,512]{2,1,0:T(8,128)S(1)}, f32[4,64,16,512]{3,2,1,0:T(8,128)}, f32[324,8,128]{2,1,0:T(8,128)S(1)}, bf16[92,16,1536]{2,1,0:T(8,128)(2,1)S(1)}) custom-call(s32[650]{0:T(1024)S(1)} %select_add_fusion.units_ref, s32[326]{0:T(512)S(1)} %select_add_fusion.1.list_ref, ...), custom_call_target="tpu_custom_call", output_to_operand_aliasing={{0}: (6, {})} | custom-call | flops 40000000000 | bytes 60000000 | tf_op jit(solution)/shard_map/main/pallas_call | solution.py:320
  122.1 0.1 fusion.59
  122.2 0.1 collective-permute-start.8
  122.3 4.1 %collective-permute-start.9 = (f32[3,36,3,128]{3,2,1,0:T(4,128)S(1)}, f32[3,36,3,128]{3,2,1,0:T(4,128)S(1)}, u32[]{:S(2)}, u32[]{:S(2)}) collective-permute-start(f32[3,36,3,128]{3,2,1,0:T(4,128)S(1)} %bitcast.169), channel_id=1, source_target_pairs={{0,28},{4,0},{8,4},{12,8},{16,12},{20,16},{24,20},{28,24},{1,29},{... | collective-permute-start | bytes 497672 | tf_op jit(solution)/shard_map/ppermute | solution.py:403
  126.4 7.4 %sample_own.2 = f32[36,8,128]{2,1,0:T(8,128)S(1)} custom-call(s32[38]{0:T(128)S(1)} %select_reduce_fusion.5.refs_0_, bf16[36,8,128]{2,1,0:T(8,128)(2,1)S(1)} %bitcast.165, bf16[8,384]{1,0:T(8,128)(2,1)S(1)} %copy-done.2, bf16[92,16,1536]{2,1,0:T(8,128)(2,1)S(1)} %get-tuple-element.45.refs_3_), custom_call_target="tpu_custom_call" | custom-call | flops 10000000000 | bytes 30000000 | tf_op jit(solution)/shard_map/sample_own/pallas_call | solution.py:358
  133.8 0.0 collective-permute-done.8
  133.8 0.1 add_add_fusion
  134.0 3.0 %collective-permute-start.10 = (f32[36,3,128]{2,1,0:T(4,128)S(1)}, f32[36,3,128]{2,1,0:T(4,128)S(1)}, u32[]{:S(2)}, u32[]{:S(2)}) collective-permute-start(f32[36,3,128]{2,1,0:T(4,128)S(1)} %get-tuple-element.84), channel_id=1, source_target_pairs={{0,1},{1,2},{2,3},{4,5},{5,6},{6,7},{8,9},{9,10},{10,11},{12,13},{... | collective-permute-start | bytes 165896 | tf_op jit(solution)/shard_map/ppermute | solution.py:409
  137.0 1.9 %collective-permute-start.11 = (f32[36,3,128]{2,1,0:T(4,128)S(1)}, f32[36,3,128]{2,1,0:T(4,128)S(1)}, u32[]{:S(2)}, u32[]{:S(2)}) collective-permute-start(f32[36,3,128]{2,1,0:T(4,128)S(1)} %get-tuple-element.85), channel_id=1, source_target_pairs={{1,0},{2,1},{3,2},{5,4},{6,5},{7,6},{9,8},{10,9},{11,10},{13,12},{... | collective-permute-start | bytes 165896 | tf_op jit(solution)/shard_map/ppermute | solution.py:409
  138.9 7.6 %sample_own.3 = f32[36,8,128]{2,1,0:T(8,128)S(1)} custom-call(s32[38]{0:T(128)S(1)} %select_reduce_fusion.5.refs_0_, bf16[36,8,128]{2,1,0:T(8,128)(2,1)S(1)} %bitcast.166, bf16[8,384]{1,0:T(8,128)(2,1)S(1)} %copy-done.2, bf16[92,16,1536]{2,1,0:T(8,128)(2,1)S(1)} %get-tuple-element.45.refs_3_), custom_call_target="tpu_custom_call" | custom-call | flops 10000000000 | bytes 30000000 | tf_op jit(solution)/shard_map/sample_own/pallas_call | solution.py:358
  146.5 0.0 collective-permute-done.10
  146.5 0.1 fusion.5
  146.6 0.1 slice_reduce_fusion
  146.8 7.6 %sort.79 = (s32[4608]{0:T(1024)}, f32[4608]{0:T(1024)S(1)}, f32[4608]{0:T(1024)S(1)}, f32[4608]{0:T(1024)S(1)}, s32[4608]{0:T(1024)}) sort(s32[4608]{0:T(1024)S(1)} %get-tuple-element.42, f32[4608]{0:T(1024)S(1)} %bitcast.175, f32[4608]{0:T(1024)S(1)} %bitcast.174, f32[4608]{0:T(1024)S(1)} %bitcast.173, s32[4608]{0:T(1024)S(1)} %iota.136), dimensions={0}, to_apply=%region_13.14 | sort | flops 59904 | bytes 184320 | tf_op jit(solution)/shard_map/sort | solution.py:483
  154.5 0.1 pad_maximum_fusion.3
  154.5 0.7 broadcast_in_dim.342
  (70 shorter events, 0.7 us)
Async XLA Ops:
  0.6 42.7 %copy-start.2 = (bf16[8,384]{1,0:T(8,128)(2,1)S(1)}, bf16[8,384]{1,0:T(8,128)(2,1)}, u32[]{:S(2)}) copy-start(bf16[8,384]{1,0:T(8,128)(2,1)} %constant.251.clone.pick_ref.refs_2_) | copy-start | bytes 18436
  2.4 6.1 %collective-permute-start = (bf16[3,8,512]{2,1,0:T(8,128)(2,1)S(1)}, bf16[3,8,512]{2,1,0:T(8,128)(2,1)S(1)}, u32[]{:S(2)}, u32[]{:S(2)}) collective-permute-start(bf16[3,8,512]{2,1,0:T(8,128)(2,1)S(1)} %get-tuple-element.96), channel_id=1, source_target_pairs={{0,28},{4,0},{8,4},{12,8},{16,12},{20,16},{24,20},{28,24},{1,29},{... | collective-permute-start | bytes 73736 | tf_op jit(solution)/shard_map/ppermute | solution.py:403
  7.5 5.4 %collective-permute-start.1 = (bf16[3,8,512]{2,1,0:T(8,128)(2,1)S(1)}, bf16[3,8,512]{2,1,0:T(8,128)(2,1)S(1)}, u32[]{:S(2)}, u32[]{:S(2)}) collective-permute-start(bf16[3,8,512]{2,1,0:T(8,128)(2,1)S(1)} %get-tuple-element.97), channel_id=1, source_target_pairs={{0,4},{4,8},{8,12},{12,16},{16,20},{20,24},{24,28},{28,0},{1,5},{5... | collective-permute-start | bytes 73736 | tf_op jit(solution)/shard_map/ppermute | solution.py:403
  12.9 7.1 %collective-permute-start.2 = (bf16[3,8,512]{2,1,0:T(8,128)(2,1)S(1)}, bf16[3,8,512]{2,1,0:T(8,128)(2,1)S(1)}, u32[]{:S(2)}, u32[]{:S(2)}) collective-permute-start(bf16[3,8,512]{2,1,0:T(8,128)(2,1)S(1)} %get-tuple-element.93), channel_id=1, source_target_pairs={{1,0},{2,1},{3,2},{5,4},{6,5},{7,6},{9,8},{10,9},{11,10},{13,12},{... | collective-permute-start | bytes 73736 | tf_op jit(solution)/shard_map/ppermute | solution.py:409
  17.0 3.9 %collective-permute-start.3 = (bf16[3,8,512]{2,1,0:T(8,128)(2,1)S(1)}, bf16[3,8,512]{2,1,0:T(8,128)(2,1)S(1)}, u32[]{:S(2)}, u32[]{:S(2)}) collective-permute-start(bf16[3,8,512]{2,1,0:T(8,128)(2,1)S(1)} %get-tuple-element.94), channel_id=1, source_target_pairs={{0,1},{1,2},{2,3},{4,5},{5,6},{6,7},{8,9},{9,10},{10,11},{12,13},{... | collective-permute-start | bytes 73736 | tf_op jit(solution)/shard_map/ppermute | solution.py:409
  29.2 7.0 %collective-permute-start.4 = (bf16[36,8,128]{2,1,0:T(8,128)(2,1)S(1)}, bf16[36,8,128]{2,1,0:T(8,128)(2,1)S(1)}, u32[]{:S(2)}, u32[]{:S(2)}) collective-permute-start(bf16[36,8,128]{2,1,0:T(8,128)(2,1)S(1)} %bitcast.161), channel_id=1, source_target_pairs={{0,1},{1,2},{2,3},{4,5},{5,6},{6,7},{8,9},{9,10},{10,11},{12,13},{... | collective-permute-start | bytes 221192 | tf_op jit(solution)/shard_map/ppermute | solution.py:409
  33.4 5.7 %collective-permute-start.5 = (bf16[36,8,128]{2,1,0:T(8,128)(2,1)S(1)}, bf16[36,8,128]{2,1,0:T(8,128)(2,1)S(1)}, u32[]{:S(2)}, u32[]{:S(2)}) collective-permute-start(bf16[36,8,128]{2,1,0:T(8,128)(2,1)S(1)} %bitcast.162), channel_id=1, source_target_pairs={{1,0},{2,1},{3,2},{5,4},{6,5},{7,6},{9,8},{10,9},{11,10},{13,12},{... | collective-permute-start | bytes 221192 | tf_op jit(solution)/shard_map/ppermute | solution.py:409
  39.1 23.8 %collective-permute-start.6 = (bf16[3,36,8,128]{3,2,1,0:T(8,128)(2,1)S(1)}, bf16[3,36,8,128]{3,2,1,0:T(8,128)(2,1)S(1)}, u32[]{:S(2)}, u32[]{:S(2)}) collective-permute-start(bf16[3,36,8,128]{3,2,1,0:T(8,128)(2,1)S(1)} %pad_maximum_fusion.1), channel_id=1, source_target_pairs={{0,4},{4,8},{8,12},{12,16},{16,20},{20,24},{24,28},{28,0},{1,5},{5... | collective-permute-start | bytes 663560 | tf_op jit(solution)/shard_map/ppermute | solution.py:403
  39.1 23.7 %collective-permute-start.7 = (bf16[3,36,8,128]{3,2,1,0:T(8,128)(2,1)S(1)}, bf16[3,36,8,128]{3,2,1,0:T(8,128)(2,1)S(1)}, u32[]{:S(2)}, u32[]{:S(2)}) collective-permute-start(bf16[3,36,8,128]{3,2,1,0:T(8,128)(2,1)S(1)} %pad_maximum_fusion.1), channel_id=1, source_target_pairs={{0,28},{4,0},{8,4},{12,8},{16,12},{20,16},{24,20},{28,24},{1,29},{... | collective-permute-start | bytes 663560 | tf_op jit(solution)/shard_map/ppermute | solution.py:403
  58.7 4.2 %copy-start.3 = (f32[84,64,512]{2,1,0:T(8,128)}, f32[84,64,512]{2,1,0:T(8,128)S(1)}, u32[]{:S(2)}) copy-start(f32[84,64,512]{2,1,0:T(8,128)S(1)} %spread_own.1.old_ref) | copy-start | bytes 33030148
  62.9 2.8 %copy-start = (f32[3,512]{1,0:T(4,128)S(1)}, f32[3,512]{1,0:T(4,128)}, u32[]{:S(2)}) copy-start(f32[3,512]{1,0:T(4,128)} %field_ref.1) | copy-start | bytes 18436
  62.9 2.9 %copy-start.1 = (f32[3,512]{1,0:T(4,128)S(1)}, f32[3,512]{1,0:T(4,128)}, u32[]{:S(2)}) copy-start(f32[3,512]{1,0:T(4,128)} %ground_ref.1) | copy-start | bytes 18436
  65.7 4.1 %copy-start.4 = (f32[84,64,512]{2,1,0:T(8,128)S(1)}, f32[84,64,512]{2,1,0:T(8,128)}, u32[]{:S(2)}) copy-start(f32[84,64,512]{2,1,0:T(8,128)} %copy-done.3) | copy-start | bytes 33030148
  122.2 11.6 %collective-permute-start.8 = (f32[3,36,3,128]{3,2,1,0:T(4,128)S(1)}, f32[3,36,3,128]{3,2,1,0:T(4,128)S(1)}, u32[]{:S(2)}, u32[]{:S(2)}) collective-permute-start(f32[3,36,3,128]{3,2,1,0:T(4,128)S(1)} %bitcast.171), channel_id=1, source_target_pairs={{0,4},{4,8},{8,12},{12,16},{16,20},{20,24},{24,28},{28,0},{1,5},{5... | collective-permute-start | bytes 497672 | tf_op jit(solution)/shard_map/ppermute | solution.py:403
  122.3 11.5 %collective-permute-start.9 = (f32[3,36,3,128]{3,2,1,0:T(4,128)S(1)}, f32[3,36,3,128]{3,2,1,0:T(4,128)S(1)}, u32[]{:S(2)}, u32[]{:S(2)}) collective-permute-start(f32[3,36,3,128]{3,2,1,0:T(4,128)S(1)} %bitcast.169), channel_id=1, source_target_pairs={{0,28},{4,0},{8,4},{12,8},{16,12},{20,16},{24,20},{28,24},{1,29},{... | collective-permute-start | bytes 497672 | tf_op jit(solution)/shard_map/ppermute | solution.py:403
  134.0 12.6 %collective-permute-start.10 = (f32[36,3,128]{2,1,0:T(4,128)S(1)}, f32[36,3,128]{2,1,0:T(4,128)S(1)}, u32[]{:S(2)}, u32[]{:S(2)}) collective-permute-start(f32[36,3,128]{2,1,0:T(4,128)S(1)} %get-tuple-element.84), channel_id=1, source_target_pairs={{0,1},{1,2},{2,3},{4,5},{5,6},{6,7},{8,9},{9,10},{10,11},{12,13},{... | collective-permute-start | bytes 165896 | tf_op jit(solution)/shard_map/ppermute | solution.py:409
  137.0 9.5 %collective-permute-start.11 = (f32[36,3,128]{2,1,0:T(4,128)S(1)}, f32[36,3,128]{2,1,0:T(4,128)S(1)}, u32[]{:S(2)}, u32[]{:S(2)}) collective-permute-start(f32[36,3,128]{2,1,0:T(4,128)S(1)} %get-tuple-element.85), channel_id=1, source_target_pairs={{1,0},{2,1},{3,2},{5,4},{6,5},{7,6},{9,8},{10,9},{11,10},{13,12},{... | collective-permute-start | bytes 165896 | tf_op jit(solution)/shard_map/ppermute | solution.py:409

commit v5 on v4

--- a/solution.py
+++ b/solution.py
@@ -16,6 +16,8 @@
 XROWS = 84
 BUCKETS = 10
 FROWS = 92
+GROUP_D = 4
+GROUP_V = 4
 BP = BX * CY
 
 spread_width = 12.5
@@ -65,15 +67,15 @@
     return i, n, (code >> 7) & 127, code & 127
 
 
-def in_pairs(list_ref, part, width, visit):
+def in_groups(list_ref, part, size, width, visit):
     count = list_ref[1]
     middle = (count + 1) // 2
     begin = middle if part == 2 else 0
     end = middle if part == 1 else count
 
-    def pair(p, _):
-        k = begin + 2 * p
-        visit([tile_codes(list_ref, k)[:3], tile_codes(list_ref, jnp.minimum(k + 1, end - 1))[:3]], k + 1 < end)
+    def group(p, _):
+        k = begin + size * p
+        visit([tile_codes(list_ref, jnp.minimum(k + j, end - 1))[:3] for j in range(size)], end - k)
 
         def leftover(t, _):
             i, n, first, last = tile_codes(list_ref, k + t)
@@ -85,10 +87,10 @@
             lax.fori_loop(1, (last - first) // width + 1, window, 0)
             return 0
 
-        lax.fori_loop(0, jnp.minimum(end - k, 2), leftover, 0)
+        lax.fori_loop(0, jnp.minimum(end - k, size), leftover, 0)
         return 0
 
-    lax.fori_loop(0, (end - begin + 1) // 2, pair, 0)
+    lax.fori_loop(0, (end - begin + size - 1) // size, group, 0)
 
 
 def framed(tab_ref, i, n):
@@ -122,23 +124,23 @@
                 amat[rows, 0:TILE] = parts[c][0] * m
                 amat[rows, TILE : 2 * TILE] = parts[c][1] * m
 
-    def visit(entries, second):
+    def visit(entries, valid):
         for j, (i, n, x0) in enumerate(entries):
-            factors(i, n, x0, amats[j], zmats[j], second if j == 1 else None)
+            factors(i, n, x0, amats[j], zmats[j], None if j == 0 else j < valid)
         for j, (i, n, x0) in enumerate(entries):
             part = jnp.dot(amats[j][...], zmats[j][...], preferred_element_type=jnp.float32)
             acc[pl.ds(x0, BX)] += part.reshape(BX, 4 * CY, NZ)
 
-    in_pairs(list_ref, 0, BX, visit)
-
-
-def spread_own_kernel(list_ref, tab_ref, pick_ref, acc, amat_a, amat_b, zmat_a, zmat_b):
+    in_groups(list_ref, 0, GROUP_D, BX, visit)
+
+
+def spread_own_kernel(list_ref, tab_ref, pick_ref, acc, *mats):
     def clear(i, _):
         acc[i] = jnp.zeros(acc.shape[1:], jnp.float32)
         return 0
 
     lax.fori_loop(0, XROWS, clear, 0)
-    accumulate(list_ref, tab_ref, pick_ref, acc, (amat_a, amat_b), (zmat_a, zmat_b))
+    accumulate(list_ref, tab_ref, pick_ref, acc, mats[:GROUP_D], mats[GROUP_D:])
 
 
 def sampled(list_ref, part, tab_ref, pick_ref, fmat, out_ref):
@@ -170,16 +172,16 @@
                 sums[c] = t if sums[c] is None else sums[c] + t
         return [jnp.sum(v.T, axis=0, keepdims=True) for v in sums]
 
-    def visit(entries, second):
+    def visit(entries, valid):
         got = [contribution(*e) for e in entries]
         for (i, n, x0), rows in zip(entries, got):
             for c in range(3):
-                if second is None:
+                if valid is None:
                     out_ref[i, c : c + 1, :] += rows[c]
                 else:
                     out_ref[i, c : c + 1, :] = rows[c]
 
-    in_pairs(list_ref, part, 2 * BX, visit)
+    in_groups(list_ref, part, GROUP_V, 2 * BX, visit)
 
 
 def main_kernel(
@@ -194,14 +196,11 @@
     dens_ref,
     out_ref,
     fmat,
-    amat_a,
-    amat_b,
-    zmat_a,
-    zmat_b,
     wide_a,
     wide_b,
     band_ref,
     flow,
+    *mats,
 ):
     step = pl.program_id(0)
     steps = CX // XO
@@ -246,7 +245,7 @@
             band_ref[q * 128 : (q + 1) * 128, :] = hi
             band_ref[NZ + q * 128 : NZ + (q + 1) * 128, :] = lo
             band_ref[2 * NZ + q * 128 : 2 * NZ + (q + 1) * 128, :] = hi
-        accumulate(units_ref, tab_ref, pick_ref, acc, (amat_a, amat_b), (zmat_a, zmat_b))
+        accumulate(units_ref, tab_ref, pick_ref, acc, mats[:GROUP_D], mats[GROUP_D:])
         filtered(0, wide_a)
 
     for parity, now, later in ((1, wide_a, wide_b), (0, wide_b, wide_a)):
@@ -263,16 +262,11 @@
     def _():
         def block(b, _):
             for c in range(3):
-
-                def chunk(j, _, c=c):
-                    cols = pl.ds(pl.multiple_of(j * 128, 128), 128)
-                    dest = pl.ds(pl.multiple_of(c * NZ + j * 128, 128), 128)
+                for j in range(NZ // 128):
+                    cols = slice(j * 128, (j + 1) * 128)
                     outs = x_filtered(lambda i: flow[c, b * BX + i, :, cols], UNIT, BX)
                     for o in range(BX):
-                        fmat[b * BX + o, :, dest] = outs[o].astype(jnp.bfloat16)
-                    return 0
-
-                lax.fori_loop(0, NZ // 128, chunk, 0)
+                        fmat[b * BX + o, :, c * NZ + j * 128 : c * NZ + (j + 1) * 128] = outs[o].astype(jnp.bfloat16)
             return 0
 
         lax.fori_loop(0, BUCKETS, block, 0)
@@ -296,7 +290,9 @@
 
 
 def factor_scratch():
-    return [pltpu.VMEM((4 * BP, 2 * TILE), jnp.bfloat16)] * 2 + [pltpu.VMEM((2 * TILE, NZ), jnp.bfloat16)] * 2
+    return [pltpu.VMEM((4 * BP, 2 * TILE), jnp.bfloat16)] * GROUP_D + [
+        pltpu.VMEM((2 * TILE, NZ), jnp.bfloat16)
+    ] * GROUP_D
 
 
 def spread_own_call(listing, table, pick):
@@ -336,13 +332,13 @@
             jax.ShapeDtypeStruct((n, 8, TILE), jnp.float32),
             jax.ShapeDtypeStruct(fshape, jnp.bfloat16),
         ],
-        scratch_shapes=factor_scratch()
-        + [
+        scratch_shapes=[
             pltpu.VMEM((2, 4 * XO * CY, NZ), jnp.bfloat16),
             pltpu.VMEM((2, 4 * XO * CY, NZ), jnp.bfloat16),
             pltpu.VMEM((3 * NZ, NZ), jnp.bfloat16),
             pltpu.VMEM((3, BUCKETS * BX + 12, CY, NZ), jnp.float32),
-        ],
+        ]
+        + factor_scratch(),
         compiler_params=MAIN_PARAMS,
         cost_estimate=pl.CostEstimate(flops=4 * 10**10, transcendentals=0, bytes_accessed=6 * 10**7),
         name="main",

time: 156 us -> 148 us (0.949)
  Pallas kernels: 82.6 us -> 72.7 us
    pallas_call x1, Pallas kernels: 52.3 us -> 46.3 us  [main_call(): pl.pallas_call(main_kernel, grid=(steps + 2,), in_specs=[smem()] * 2 + [w...]
    pallas_call x1, Pallas kernels: 15.4 us -> 12.2 us  [spread_own_call(): pl.pallas_call(spread_own_kernel, grid=(1,), in_specs=[smem(), whole(tabl...]
  transfers between devices with their start and end apart: 12 -> 12, of which waited for: 4 -> 4; matrix products, arithmetic and copies ran while one was open for 1% -> 1% of each run, Pallas kernels for 20% -> 18%
where the time goes in v5:
time: 148 us; the launch traced here: 146 us
  Pallas kernels  72.7 us (49%)
  starting transfers between devices  32.6 us (22%)
  other arithmetic  20.4 us (14%)
  local copies, waits for them, and re-layouts  10.2 us (7%)
  waiting for transfers between devices  8.96 us (6%)
    pallas_call x1, Pallas kernels, main_call(): pl.pallas_call(main_kernel, grid=(steps + 2,), in_specs=[smem()] * 2 + [w...  46.3 us
    ppermute x6, starting transfers between devices, line(): lax.ppermute(value, 'span', [(i, i + steps) for i in range(first, last)])  19 us
    pallas_call x2, Pallas kernels, sample_own_call(): pl.pallas_call(kernel, grid=(1,), in_specs=[smem(), whole(table.shape), w...  14.2 us
    ppermute x6, starting transfers between devices, ring(): lax.ppermute(value, 'stream', [(i, (i + steps) % count) for i in range(co...  13.6 us
    pallas_call x1, Pallas kernels, spread_own_call(): pl.pallas_call(spread_own_kernel, grid=(1,), in_specs=[smem(), whole(tabl...  12.2 us
    unnamed x10, local copies, waits for them, and re-layouts  8.3 us
    sort x1, other arithmetic, on_device(): _, *vel = lax.sort((order, own[0], own[1], own[2]), num_keys=1)  7.64 us
    sort x5, other arithmetic, on_device(): lax.sort((key, order) + tuple((inbound[c].astype(f32) for c in range(4)))...  6.36 us
  transfers between devices with their start and end apart: 12, of which 4 were waited for; matrix products, arithmetic and copies ran while one was open for 1% of the time, Pallas kernels for 18%

profile of v5, /device:TPU:1, one launch (start us, length us, event | category | flops | bytes accessed | tf_op | source)
XLA Modules:
  0.0 146.2 jit_solution(15383855174432832812)
XLA Ops:
  0.6 0.0 copy-start.2
  0.7 0.8 fusion.7
  1.5 0.9 fusion.1
  2.4 5.2 %collective-permute-start = (bf16[3,8,512]{2,1,0:T(8,128)(2,1)S(1)}, bf16[3,8,512]{2,1,0:T(8,128)(2,1)S(1)}, u32[]{:S(2)}, u32[]{:S(2)}) collective-permute-start(bf16[3,8,512]{2,1,0:T(8,128)(2,1)S(1)} %get-tuple-element.96), channel_id=1, source_target_pairs={{0,28},{4,0},{8,4},{12,8},{16,12},{20,16},{24,20},{28,24},{1,29},{... | collective-permute-start | bytes 73736 | tf_op jit(solution)/shard_map/ppermute | solution.py:399
  7.5 0.0 collective-permute-start.1
  7.6 0.1 pad_add_fusion.2
  7.6 0.1 not_and_fusion
  7.7 0.7 collective-permute-done
  8.5 4.4 %collective-permute-done.1 = bf16[3,8,512]{2,1,0:T(8,128)(2,1)S(1)} collective-permute-done((bf16[3,8,512]{2,1,0:T(8,128)(2,1)S(1)}, bf16[3,8,512]{2,1,0:T(8,128)(2,1)S(1)}, u32[]{:S(2)}, u32[]{:S(2)}) %collective-permute-start.1) | collective-permute-done | bytes 24608 | tf_op jit(solution)/shard_map/ppermute | solution.py:399
  12.9 4.0 %collective-permute-start.2 = (bf16[3,8,512]{2,1,0:T(8,128)(2,1)S(1)}, bf16[3,8,512]{2,1,0:T(8,128)(2,1)S(1)}, u32[]{:S(2)}, u32[]{:S(2)}) collective-permute-start(bf16[3,8,512]{2,1,0:T(8,128)(2,1)S(1)} %get-tuple-element.93), channel_id=1, source_target_pairs={{1,0},{2,1},{3,2},{5,4},{6,5},{7,6},{9,8},{10,9},{11,10},{13,12},{... | collective-permute-start | bytes 73736 | tf_op jit(solution)/shard_map/ppermute | solution.py:405
  17.0 3.0 %collective-permute-start.3 = (bf16[3,8,512]{2,1,0:T(8,128)(2,1)S(1)}, bf16[3,8,512]{2,1,0:T(8,128)(2,1)S(1)}, u32[]{:S(2)}, u32[]{:S(2)}) collective-permute-start(bf16[3,8,512]{2,1,0:T(8,128)(2,1)S(1)} %get-tuple-element.94), channel_id=1, source_target_pairs={{0,1},{1,2},{2,3},{4,5},{5,6},{6,7},{8,9},{9,10},{10,11},{12,13},{... | collective-permute-start | bytes 73736 | tf_op jit(solution)/shard_map/ppermute | solution.py:405
  20.0 0.0 collective-permute-done.2
  20.0 0.9 collective-permute-done.3
  20.9 0.7 select_bitcast_fusion.1
  21.7 0.1 slice_convert_fusion.2
  21.8 0.1 fusion.61
  22.1 6.3 %sort.78 = (s32[4608]{0:T(1024)S(1)}, s32[4608]{0:T(1024)S(1)}, f32[4608]{0:T(1024)S(1)}, f32[4608]{0:T(1024)S(1)}, f32[4608]{0:T(1024)S(1)}, /*index=5*/f32[4608]{0:T(1024)S(1)}) sort(s32[4608]{0:T(1024)S(1)} %fusion.18, s32[4608]{0:T(1024)S(1)} %iota.121, f32[4608]{0:T(1024)S(1)} %reshape.729, f32[4608]{0:T(1024)S(1)} %reshape.730, f32[4608]{0:T(1024)S(1)} %reshape.731, ...), dimensions={0}, to_apply=%region_0.1 | sort | flops 59904 | bytes 221184 | tf_op jit(solution)/shard_map/sort | solution.py:440
  28.4 0.2 fusion.28
  28.9 0.2 stack.95
  29.2 4.2 %collective-permute-start.4 = (bf16[36,8,128]{2,1,0:T(8,128)(2,1)S(1)}, bf16[36,8,128]{2,1,0:T(8,128)(2,1)S(1)}, u32[]{:S(2)}, u32[]{:S(2)}) collective-permute-start(bf16[36,8,128]{2,1,0:T(8,128)(2,1)S(1)} %bitcast.161), channel_id=1, source_target_pairs={{0,1},{1,2},{2,3},{4,5},{5,6},{6,7},{8,9},{9,10},{10,11},{12,13},{... | collective-permute-start | bytes 221192 | tf_op jit(solution)/shard_map/ppermute | solution.py:405
  33.4 1.9 %collective-permute-start.5 = (bf16[36,8,128]{2,1,0:T(8,128)(2,1)S(1)}, bf16[36,8,128]{2,1,0:T(8,128)(2,1)S(1)}, u32[]{:S(2)}, u32[]{:S(2)}) collective-permute-start(bf16[36,8,128]{2,1,0:T(8,128)(2,1)S(1)} %bitcast.162), channel_id=1, source_target_pairs={{1,0},{2,1},{3,2},{5,4},{6,5},{7,6},{9,8},{10,9},{11,10},{13,12},{... | collective-permute-start | bytes 221192 | tf_op jit(solution)/shard_map/ppermute | solution.py:405
  35.3 0.2 convert_reduce_fusion.3
  35.5 0.1 fusion.57
  35.6 0.2 convert_reduce_fusion.2
  35.8 0.1 add_select_fusion.21
  35.9 0.1 select_reduce_fusion.4.list_ref
  36.0 0.2 select_reduce_fusion.5.refs_0_
  36.2 0.0 collective-permute-done.4
  36.2 2.9 %collective-permute-done.5 = bf16[36,8,128]{2,1,0:T(8,128)(2,1)S(1)} collective-permute-done((bf16[36,8,128]{2,1,0:T(8,128)(2,1)S(1)}, bf16[36,8,128]{2,1,0:T(8,128)(2,1)S(1)}, u32[]{:S(2)}, u32[]{:S(2)}) %collective-permute-start.5) | collective-permute-done | bytes 73760 | tf_op jit(solution)/shard_map/ppermute | solution.py:405
  39.1 0.1 collective-permute-start.6
  39.1 4.1 %collective-permute-start.7 = (bf16[3,36,8,128]{3,2,1,0:T(8,128)(2,1)S(1)}, bf16[3,36,8,128]{3,2,1,0:T(8,128)(2,1)S(1)}, u32[]{:S(2)}, u32[]{:S(2)}) collective-permute-start(bf16[3,36,8,128]{3,2,1,0:T(8,128)(2,1)S(1)} %pad_maximum_fusion.1), channel_id=1, source_target_pairs={{0,28},{4,0},{8,4},{12,8},{16,12},{20,16},{24,20},{28,24},{1,29},{... | collective-permute-start | bytes 663560 | tf_op jit(solution)/shard_map/ppermute | solution.py:399
  43.3 12.2 %spread_own.1.old_ref = f32[84,64,512]{2,1,0:T(8,128)S(1)} custom-call(s32[74]{0:T(128)S(1)} %select_reduce_fusion.4.list_ref, bf16[36,8,128]{2,1,0:T(8,128)(2,1)S(1)} %bitcast.164, bf16[8,384]{1,0:T(8,128)(2,1)S(1)} %copy-done.2), custom_call_target="tpu_custom_call" | custom-call | flops 10000000000 | bytes 30000000 | tf_op jit(solution)/shard_map/spread_own/pallas_call | solution.py:299
  55.5 4.2 %copy-done.3 = f32[84,64,512]{2,1,0:T(8,128)} copy-done((f32[84,64,512]{2,1,0:T(8,128)}, f32[84,64,512]{2,1,0:T(8,128)S(1)}, u32[]{:S(2)}) %copy-start.3) | copy-done | bytes 11010072
  59.7 0.0 collective-permute-done.6
  59.7 0.0 collective-permute-done.7
  59.7 0.1 pad_maximum_fusion
  59.8 0.3 slice_convert_fusion
  60.1 0.3 fusion.60
  60.4 0.5 select_reduce_fusion.3
  60.8 0.1 concatenate.99
  60.9 0.1 reshape.727
  61.0 0.2 convert_reduce_fusion.1
  61.3 0.2 select_reduce_fusion.1
  61.5 0.1 fusion.55
  61.6 0.4 convert_reduce_fusion
  62.0 0.1 add_select_fusion.15
  62.1 0.4 select_reduce_fusion
  62.6 4.1 %copy-done.4 = f32[84,64,512]{2,1,0:T(8,128)S(1)} copy-done((f32[84,64,512]{2,1,0:T(8,128)S(1)}, f32[84,64,512]{2,1,0:T(8,128)}, u32[]{:S(2)}) %copy-start.4) | copy-done | bytes 11010072
  66.7 46.3 %main.1 = (f32[84,64,512]{2,1,0:T(8,128)S(1)}, f32[4,64,16,512]{3,2,1,0:T(8,128)}, f32[324,8,128]{2,1,0:T(8,128)S(1)}, bf16[92,16,1536]{2,1,0:T(8,128)(2,1)S(1)}) custom-call(s32[650]{0:T(1024)S(1)} %select_add_fusion.units_ref, s32[326]{0:T(512)S(1)} %select_add_fusion.1.list_ref, ...), custom_call_target="tpu_custom_call", output_to_operand_aliasing={{0}: (6, {})} | custom-call | flops 40000000000 | bytes 60000000 | tf_op jit(solution)/shard_map/main/pallas_call | solution.py:316
  113.0 0.1 fusion.59
  113.1 0.1 collective-permute-start.8
  113.1 4.1 %collective-permute-start.9 = (f32[3,36,3,128]{3,2,1,0:T(4,128)S(1)}, f32[3,36,3,128]{3,2,1,0:T(4,128)S(1)}, u32[]{:S(2)}, u32[]{:S(2)}) collective-permute-start(f32[3,36,3,128]{3,2,1,0:T(4,128)S(1)} %bitcast.169), channel_id=1, source_target_pairs={{0,28},{4,0},{8,4},{12,8},{16,12},{20,16},{24,20},{28,24},{1,29},{... | collective-permute-start | bytes 497672 | tf_op jit(solution)/shard_map/ppermute | solution.py:399
  117.3 7.5 %sample_own.2 = f32[36,8,128]{2,1,0:T(8,128)S(1)} custom-call(s32[38]{0:T(128)S(1)} %select_reduce_fusion.5.refs_0_, bf16[36,8,128]{2,1,0:T(8,128)(2,1)S(1)} %bitcast.165, bf16[8,384]{1,0:T(8,128)(2,1)S(1)} %copy-done.2, bf16[92,16,1536]{2,1,0:T(8,128)(2,1)S(1)} %get-tuple-element.45.refs_3_), custom_call_target="tpu_custom_call" | custom-call | flops 10000000000 | bytes 30000000 | tf_op jit(solution)/shard_map/sample_own/pallas_call | solution.py:354
  124.8 0.0 collective-permute-done.8
  124.9 0.0 collective-permute-done.9
  124.9 0.1 add_add_fusion
  125.0 3.9 %collective-permute-start.10 = (f32[36,3,128]{2,1,0:T(4,128)S(1)}, f32[36,3,128]{2,1,0:T(4,128)S(1)}, u32[]{:S(2)}, u32[]{:S(2)}) collective-permute-start(f32[36,3,128]{2,1,0:T(4,128)S(1)} %get-tuple-element.84), channel_id=1, source_target_pairs={{0,1},{1,2},{2,3},{4,5},{5,6},{6,7},{8,9},{9,10},{10,11},{12,13},{... | collective-permute-start | bytes 165896 | tf_op jit(solution)/shard_map/ppermute | solution.py:405
  129.0 1.9 %collective-permute-start.11 = (f32[36,3,128]{2,1,0:T(4,128)S(1)}, f32[36,3,128]{2,1,0:T(4,128)S(1)}, u32[]{:S(2)}, u32[]{:S(2)}) collective-permute-start(f32[36,3,128]{2,1,0:T(4,128)S(1)} %get-tuple-element.85), channel_id=1, source_target_pairs={{1,0},{2,1},{3,2},{5,4},{6,5},{7,6},{9,8},{10,9},{11,10},{13,12},{... | collective-permute-start | bytes 165896 | tf_op jit(solution)/shard_map/ppermute | solution.py:405
  130.9 6.6 %sample_own.3 = f32[36,8,128]{2,1,0:T(8,128)S(1)} custom-call(s32[38]{0:T(128)S(1)} %select_reduce_fusion.5.refs_0_, bf16[36,8,128]{2,1,0:T(8,128)(2,1)S(1)} %bitcast.166, bf16[8,384]{1,0:T(8,128)(2,1)S(1)} %copy-done.2, bf16[92,16,1536]{2,1,0:T(8,128)(2,1)S(1)} %get-tuple-element.45.refs_3_), custom_call_target="tpu_custom_call" | custom-call | flops 10000000000 | bytes 30000000 | tf_op jit(solution)/shard_map/sample_own/pallas_call | solution.py:354
  137.6 0.1 fusion.5
  137.6 0.1 slice_reduce_fusion
  137.8 7.6 %sort.79 = (s32[4608]{0:T(1024)}, f32[4608]{0:T(1024)S(1)}, f32[4608]{0:T(1024)S(1)}, f32[4608]{0:T(1024)S(1)}, s32[4608]{0:T(1024)}) sort(s32[4608]{0:T(1024)S(1)} %get-tuple-element.42, f32[4608]{0:T(1024)S(1)} %bitcast.175, f32[4608]{0:T(1024)S(1)} %bitcast.174, f32[4608]{0:T(1024)S(1)} %bitcast.173, s32[4608]{0:T(1024)S(1)} %iota.136), dimensions={0}, to_apply=%region_13.14 | sort | flops 59904 | bytes 184320 | tf_op jit(solution)/shard_map/sort | solution.py:479
  145.5 0.1 pad_maximum_fusion.3
  145.5 0.7 broadcast_in_dim.342
  (70 shorter events, 0.7 us)
Async XLA Ops:
  0.6 42.7 %copy-start.2 = (bf16[8,384]{1,0:T(8,128)(2,1)S(1)}, bf16[8,384]{1,0:T(8,128)(2,1)}, u32[]{:S(2)}) copy-start(bf16[8,384]{1,0:T(8,128)(2,1)} %constant.251.clone.pick_ref.refs_2_) | copy-start | bytes 18436
  2.4 6.1 %collective-permute-start = (bf16[3,8,512]{2,1,0:T(8,128)(2,1)S(1)}, bf16[3,8,512]{2,1,0:T(8,128)(2,1)S(1)}, u32[]{:S(2)}, u32[]{:S(2)}) collective-permute-start(bf16[3,8,512]{2,1,0:T(8,128)(2,1)S(1)} %get-tuple-element.96), channel_id=1, source_target_pairs={{0,28},{4,0},{8,4},{12,8},{16,12},{20,16},{24,20},{28,24},{1,29},{... | collective-permute-start | bytes 73736 | tf_op jit(solution)/shard_map/ppermute | solution.py:399
  7.5 5.4 %collective-permute-start.1 = (bf16[3,8,512]{2,1,0:T(8,128)(2,1)S(1)}, bf16[3,8,512]{2,1,0:T(8,128)(2,1)S(1)}, u32[]{:S(2)}, u32[]{:S(2)}) collective-permute-start(bf16[3,8,512]{2,1,0:T(8,128)(2,1)S(1)} %get-tuple-element.97), channel_id=1, source_target_pairs={{0,4},{4,8},{8,12},{12,16},{16,20},{20,24},{24,28},{28,0},{1,5},{5... | collective-permute-start | bytes 73736 | tf_op jit(solution)/shard_map/ppermute | solution.py:399
  12.9 7.1 %collective-permute-start.2 = (bf16[3,8,512]{2,1,0:T(8,128)(2,1)S(1)}, bf16[3,8,512]{2,1,0:T(8,128)(2,1)S(1)}, u32[]{:S(2)}, u32[]{:S(2)}) collective-permute-start(bf16[3,8,512]{2,1,0:T(8,128)(2,1)S(1)} %get-tuple-element.93), channel_id=1, source_target_pairs={{1,0},{2,1},{3,2},{5,4},{6,5},{7,6},{9,8},{10,9},{11,10},{13,12},{... | collective-permute-start | bytes 73736 | tf_op jit(solution)/shard_map/ppermute | solution.py:405
  17.0 3.9 %collective-permute-start.3 = (bf16[3,8,512]{2,1,0:T(8,128)(2,1)S(1)}, bf16[3,8,512]{2,1,0:T(8,128)(2,1)S(1)}, u32[]{:S(2)}, u32[]{:S(2)}) collective-permute-start(bf16[3,8,512]{2,1,0:T(8,128)(2,1)S(1)} %get-tuple-element.94), channel_id=1, source_target_pairs={{0,1},{1,2},{2,3},{4,5},{5,6},{6,7},{8,9},{9,10},{10,11},{12,13},{... | collective-permute-start | bytes 73736 | tf_op jit(solution)/shard_map/ppermute | solution.py:405
  29.2 7.0 %collective-permute-start.4 = (bf16[36,8,128]{2,1,0:T(8,128)(2,1)S(1)}, bf16[36,8,128]{2,1,0:T(8,128)(2,1)S(1)}, u32[]{:S(2)}, u32[]{:S(2)}) collective-permute-start(bf16[36,8,128]{2,1,0:T(8,128)(2,1)S(1)} %bitcast.161), channel_id=1, source_target_pairs={{0,1},{1,2},{2,3},{4,5},{5,6},{6,7},{8,9},{9,10},{10,11},{12,13},{... | collective-permute-start | bytes 221192 | tf_op jit(solution)/shard_map/ppermute | solution.py:405
  33.4 5.7 %collective-permute-start.5 = (bf16[36,8,128]{2,1,0:T(8,128)(2,1)S(1)}, bf16[36,8,128]{2,1,0:T(8,128)(2,1)S(1)}, u32[]{:S(2)}, u32[]{:S(2)}) collective-permute-start(bf16[36,8,128]{2,1,0:T(8,128)(2,1)S(1)} %bitcast.162), channel_id=1, source_target_pairs={{1,0},{2,1},{3,2},{5,4},{6,5},{7,6},{9,8},{10,9},{11,10},{13,12},{... | collective-permute-start | bytes 221192 | tf_op jit(solution)/shard_map/ppermute | solution.py:405
  39.1 20.6 %collective-permute-start.6 = (bf16[3,36,8,128]{3,2,1,0:T(8,128)(2,1)S(1)}, bf16[3,36,8,128]{3,2,1,0:T(8,128)(2,1)S(1)}, u32[]{:S(2)}, u32[]{:S(2)}) collective-permute-start(bf16[3,36,8,128]{3,2,1,0:T(8,128)(2,1)S(1)} %pad_maximum_fusion.1), channel_id=1, source_target_pairs={{0,4},{4,8},{8,12},{12,16},{16,20},{20,24},{24,28},{28,0},{1,5},{5... | collective-permute-start | bytes 663560 | tf_op jit(solution)/shard_map/ppermute | solution.py:399
  39.1 20.6 %collective-permute-start.7 = (bf16[3,36,8,128]{3,2,1,0:T(8,128)(2,1)S(1)}, bf16[3,36,8,128]{3,2,1,0:T(8,128)(2,1)S(1)}, u32[]{:S(2)}, u32[]{:S(2)}) collective-permute-start(bf16[3,36,8,128]{3,2,1,0:T(8,128)(2,1)S(1)} %pad_maximum_fusion.1), channel_id=1, source_target_pairs={{0,28},{4,0},{8,4},{12,8},{16,12},{20,16},{24,20},{28,24},{1,29},{... | collective-permute-start | bytes 663560 | tf_op jit(solution)/shard_map/ppermute | solution.py:399
  55.5 4.2 %copy-start.3 = (f32[84,64,512]{2,1,0:T(8,128)}, f32[84,64,512]{2,1,0:T(8,128)S(1)}, u32[]{:S(2)}) copy-start(f32[84,64,512]{2,1,0:T(8,128)S(1)} %spread_own.1.old_ref) | copy-start | bytes 33030148
  59.7 2.8 %copy-start = (f32[3,512]{1,0:T(4,128)S(1)}, f32[3,512]{1,0:T(4,128)}, u32[]{:S(2)}) copy-start(f32[3,512]{1,0:T(4,128)} %field_ref.1) | copy-start | bytes 18436
  59.7 2.9 %copy-start.1 = (f32[3,512]{1,0:T(4,128)S(1)}, f32[3,512]{1,0:T(4,128)}, u32[]{:S(2)}) copy-start(f32[3,512]{1,0:T(4,128)} %ground_ref.1) | copy-start | bytes 18436
  62.6 4.1 %copy-start.4 = (f32[84,64,512]{2,1,0:T(8,128)S(1)}, f32[84,64,512]{2,1,0:T(8,128)}, u32[]{:S(2)}) copy-start(f32[84,64,512]{2,1,0:T(8,128)} %copy-done.3) | copy-start | bytes 33030148
  113.1 11.8 %collective-permute-start.8 = (f32[3,36,3,128]{3,2,1,0:T(4,128)S(1)}, f32[3,36,3,128]{3,2,1,0:T(4,128)S(1)}, u32[]{:S(2)}, u32[]{:S(2)}) collective-permute-start(f32[3,36,3,128]{3,2,1,0:T(4,128)S(1)} %bitcast.171), channel_id=1, source_target_pairs={{0,4},{4,8},{8,12},{12,16},{16,20},{20,24},{24,28},{28,0},{1,5},{5... | collective-permute-start | bytes 497672 | tf_op jit(solution)/shard_map/ppermute | solution.py:399
  113.1 11.7 %collective-permute-start.9 = (f32[3,36,3,128]{3,2,1,0:T(4,128)S(1)}, f32[3,36,3,128]{3,2,1,0:T(4,128)S(1)}, u32[]{:S(2)}, u32[]{:S(2)}) collective-permute-start(f32[3,36,3,128]{3,2,1,0:T(4,128)S(1)} %bitcast.169), channel_id=1, source_target_pairs={{0,28},{4,0},{8,4},{12,8},{16,12},{20,16},{24,20},{28,24},{1,29},{... | collective-permute-start | bytes 497672 | tf_op jit(solution)/shard_map/ppermute | solution.py:399
  125.0 12.5 %collective-permute-start.10 = (f32[36,3,128]{2,1,0:T(4,128)S(1)}, f32[36,3,128]{2,1,0:T(4,128)S(1)}, u32[]{:S(2)}, u32[]{:S(2)}) collective-permute-start(f32[36,3,128]{2,1,0:T(4,128)S(1)} %get-tuple-element.84), channel_id=1, source_target_pairs={{0,1},{1,2},{2,3},{4,5},{5,6},{6,7},{8,9},{9,10},{10,11},{12,13},{... | collective-permute-start | bytes 165896 | tf_op jit(solution)/shard_map/ppermute | solution.py:405
  129.0 8.6 %collective-permute-start.11 = (f32[36,3,128]{2,1,0:T(4,128)S(1)}, f32[36,3,128]{2,1,0:T(4,128)S(1)}, u32[]{:S(2)}, u32[]{:S(2)}) collective-permute-start(f32[36,3,128]{2,1,0:T(4,128)S(1)} %get-tuple-element.85), channel_id=1, source_target_pairs={{1,0},{2,1},{3,2},{5,4},{6,5},{7,6},{9,8},{10,9},{11,10},{13,12},{... | collective-permute-start | bytes 165896 | tf_op jit(solution)/shard_map/ppermute | solution.py:405

commit v6 on v5

--- a/solution.py
+++ b/solution.py
@@ -16,7 +16,8 @@
 XROWS = 84
 BUCKETS = 10
 FROWS = 92
-GROUP_D = 4
+ZW = 384
+GROUP_D = 6
 GROUP_V = 4
 BP = BX * CY
 
@@ -134,13 +135,16 @@
     in_groups(list_ref, 0, GROUP_D, BX, visit)
 
 
-def spread_own_kernel(list_ref, tab_ref, pick_ref, acc, *mats):
+def spread_own_kernel(list_ref, tab_ref, pick_ref, out_ref, acc, sem, *mats):
     def clear(i, _):
         acc[i] = jnp.zeros(acc.shape[1:], jnp.float32)
         return 0
 
     lax.fori_loop(0, XROWS, clear, 0)
     accumulate(list_ref, tab_ref, pick_ref, acc, mats[:GROUP_D], mats[GROUP_D:])
+    copy = pltpu.make_async_copy(acc, out_ref, sem)
+    copy.start()
+    copy.wait()
 
 
 def sampled(list_ref, part, tab_ref, pick_ref, fmat, out_ref):
@@ -192,10 +196,11 @@
     field_ref,
     ground_ref,
     old_ref,
-    acc,
     dens_ref,
     out_ref,
     fmat,
+    acc,
+    sem,
     wide_a,
     wide_b,
     band_ref,
@@ -219,8 +224,9 @@
 
     def finish(b, wide, h):
         cols = slice(h * 256, (h + 1) * 256)
-        full = jnp.concatenate([wide[0], wide[0], wide[1]], axis=1)
-        dens = jnp.dot(full, band_ref[:, cols], preferred_element_type=jnp.float32)
+        zs = slice(h * 128, h * 128 + ZW)
+        full = jnp.concatenate([wide[0, :, zs], wide[0, :, zs], wide[1, :, zs]], axis=1)
+        dens = jnp.dot(full, band_ref[h], preferred_element_type=jnp.float32)
         dens = dens.reshape(4, XO, CY, 256)
         dens_ref[3, :, :, cols] = dens[3]
         for c in range(3):
@@ -230,6 +236,9 @@
 
     @pl.when(step == 0)
     def _():
+        copy = pltpu.make_async_copy(old_ref, acc, sem)
+        copy.start()
+
         def clear(i, _):
             flow[:, i] = jnp.zeros((3, CY, NZ), jnp.float32)
             flow[:, 12 + CX + i] = jnp.zeros((3, CY, NZ), jnp.float32)
@@ -238,13 +247,15 @@
         lax.fori_loop(0, 16, clear, 0)
         for i in range(BUCKETS * BX, FROWS):
             fmat[i] = jnp.zeros(fmat.shape[1:], jnp.bfloat16)
-        for q in range(NZ // 128):
-            row = lax.broadcasted_iota(jnp.int32, (128, NZ), 0) + 128 * q
-            col = lax.broadcasted_iota(jnp.int32, (128, NZ), 1)
-            hi, lo = hi_lo(gauss((row - col).astype(jnp.float32)))
-            band_ref[q * 128 : (q + 1) * 128, :] = hi
-            band_ref[NZ + q * 128 : NZ + (q + 1) * 128, :] = lo
-            band_ref[2 * NZ + q * 128 : 2 * NZ + (q + 1) * 128, :] = hi
+        for h in range(2):
+            for q in range(3):
+                row = lax.broadcasted_iota(jnp.int32, (128, 256), 0) + 128 * (q + h)
+                col = lax.broadcasted_iota(jnp.int32, (128, 256), 1) + 256 * h
+                hi, lo = hi_lo(gauss((row - col).astype(jnp.float32)))
+                band_ref[h, q * 128 : (q + 1) * 128, :] = hi
+                band_ref[h, ZW + q * 128 : ZW + (q + 1) * 128, :] = lo
+                band_ref[h, 2 * ZW + q * 128 : 2 * ZW + (q + 1) * 128, :] = hi
+        copy.wait()
         accumulate(units_ref, tab_ref, pick_ref, acc, mats[:GROUP_D], mats[GROUP_D:])
         filtered(0, wide_a)
 
@@ -285,8 +296,8 @@
     return pl.BlockSpec(shape, lambda i: (0,) * len(shape))
 
 
-PARAMS = pltpu.CompilerParams(vmem_limit_bytes=16 << 20)
-MAIN_PARAMS = pltpu.CompilerParams(vmem_limit_bytes=32 << 20)
+PARAMS = pltpu.CompilerParams(vmem_limit_bytes=24 << 20)
+MAIN_PARAMS = pltpu.CompilerParams(vmem_limit_bytes=40 << 20)
 
 
 def factor_scratch():
@@ -300,9 +311,9 @@
         spread_own_kernel,
         grid=(1,),
         in_specs=[smem(), whole(table.shape), whole(pick.shape)],
-        out_specs=pl.BlockSpec(memory_space=pltpu.VMEM),
-        out_shape=pltpu.VMEM((XROWS, 4 * CY, NZ), jnp.float32),
-        scratch_shapes=factor_scratch(),
+        out_specs=pl.BlockSpec(memory_space=pltpu.HBM),
+        out_shape=pltpu.HBM((XROWS, 4 * CY, NZ), jnp.float32),
+        scratch_shapes=[pltpu.VMEM((XROWS, 4 * CY, NZ), jnp.float32), pltpu.SemaphoreType.DMA] + factor_scratch(),
         compiler_params=PARAMS,
         cost_estimate=pl.CostEstimate(flops=10**10, transcendentals=0, bytes_accessed=3 * 10**7),
         name="spread_own",
@@ -318,24 +329,23 @@
         grid=(steps + 2,),
         in_specs=[smem()] * 2
         + [whole(v.shape) for v in (table, pick, field, ground)]
-        + [pl.BlockSpec(memory_space=pltpu.VMEM)],
+        + [pl.BlockSpec(memory_space=pltpu.HBM)],
         out_specs=[
-            pl.BlockSpec(memory_space=pltpu.VMEM),
             pl.BlockSpec((4, XO, CY, NZ), lambda i: (0, jnp.clip(i - 1, 0, steps - 1), 0, 0)),
             whole((n, 8, TILE)),
             whole(fshape),
         ],
-        input_output_aliases={6: 0},
         out_shape=[
-            pltpu.VMEM(old.shape, jnp.float32),
             jax.ShapeDtypeStruct((4, CX, CY, NZ), jnp.float32),
             jax.ShapeDtypeStruct((n, 8, TILE), jnp.float32),
             jax.ShapeDtypeStruct(fshape, jnp.bfloat16),
         ],
         scratch_shapes=[
+            pltpu.VMEM(old.shape, jnp.float32),
+            pltpu.SemaphoreType.DMA,
             pltpu.VMEM((2, 4 * XO * CY, NZ), jnp.bfloat16),
             pltpu.VMEM((2, 4 * XO * CY, NZ), jnp.bfloat16),
-            pltpu.VMEM((3 * NZ, NZ), jnp.bfloat16),
+            pltpu.VMEM((2, 3 * ZW, 256), jnp.bfloat16),
             pltpu.VMEM((3, BUCKETS * BX + 12, CY, NZ), jnp.float32),
         ]
         + factor_scratch(),
@@ -467,7 +477,7 @@
 
     pick = jnp.asarray(PICK, bf16)
     half = spread_own_call(own_units, packed, pick)
-    _, density, partial, fmat = main_call(rest_units, rest_list, table, pick, field, background, half)
+    density, partial, fmat = main_call(rest_units, rest_list, table, pick, field, background, half)
     early = sample_own_call(1, own_list, packed, pick, fmat)
     partial = partial[:, :3].reshape(3, 3, tiles, 3, TILE)
     mixed = partial[1] + ring(partial[2], 1) + ring(partial[0], -1)

time: 148 us -> 145 us (0.980)
  local copies, waits for them, and re-layouts: 10.2 us -> 1.97 us
  Pallas kernels: 72.7 us -> 79.3 us
  starting transfers between devices: 32.6 us -> 31.1 us
    unnamed x10 -> x6, local copies, waits for them, and re-layouts: 8.3 us -> 0.02 us
    pallas_call x1, Pallas kernels: 46.3 us -> 49.9 us  [main_call(): pl.pallas_call(main_kernel, grid=(steps + 2,), in_specs=[smem()] * 2 + [w...]
    pallas_call x1, Pallas kernels: 12.2 us -> 15.8 us  [spread_own_call(): pl.pallas_call(spread_own_kernel, grid=(1,), in_specs=[smem(), whole(tabl...]
    ppermute x6, starting transfers between devices: 19 us -> 17.5 us  [line(): lax.ppermute(value, 'span', [(i, i + steps) for i in range(first, last)])]
  transfers between devices with their start and end apart: 12 -> 12, of which waited for: 4 -> 4; matrix products, arithmetic and copies ran while one was open for 1% -> 1% of each run, Pallas kernels for 18% -> 21%
where the time goes in v6:
time: 145 us; the launch traced here: 143 us
  Pallas kernels  79.3 us (55%)
  starting transfers between devices  31.1 us (21%)
  other arithmetic  20.4 us (14%)
  waiting for transfers between devices  8.96 us (6%)
  local copies, waits for them, and re-layouts  1.97 us (1%)
    pallas_call x1, Pallas kernels, main_call(): pl.pallas_call(main_kernel, grid=(steps + 2,), in_specs=[smem()] * 2 + [w...  49.9 us
    ppermute x6, starting transfers between devices, line(): lax.ppermute(value, 'span', [(i, i + steps) for i in range(first, last)])  17.5 us
    pallas_call x1, Pallas kernels, spread_own_call(): pl.pallas_call(spread_own_kernel, grid=(1,), in_specs=[smem(), whole(tabl...  15.8 us
    pallas_call x2, Pallas kernels, sample_own_call(): pl.pallas_call(kernel, grid=(1,), in_specs=[smem(), whole(table.shape), w...  13.7 us
    ppermute x6, starting transfers between devices, ring(): lax.ppermute(value, 'stream', [(i, (i + steps) % count) for i in range(co...  13.6 us
    sort x1, other arithmetic, on_device(): _, *vel = lax.sort((order, own[0], own[1], own[2]), num_keys=1)  7.64 us
    sort x5, other arithmetic, on_device(): lax.sort((key, order) + tuple((inbound[c].astype(f32) for c in range(4)))...  6.36 us
    ppermute x6, waiting for transfers between devices, ring(): lax.ppermute(value, 'stream', [(i, (i + steps) % count) for i in range(co...  5.19 us
  transfers between devices with their start and end apart: 12, of which 4 were waited for; matrix products, arithmetic and copies ran while one was open for 1% of the time, Pallas kernels for 21%

profile of v6, /device:TPU:1, one launch (start us, length us, event | category | flops | bytes accessed | tf_op | source)
XLA Modules:
  0.0 143.0 jit_solution(8754761792219428341)
XLA Ops:
  0.6 0.0 copy-start.2
  0.7 0.8 fusion.7
  1.5 0.9 fusion.1
  2.4 5.2 %collective-permute-start = (bf16[3,8,512]{2,1,0:T(8,128)(2,1)S(1)}, bf16[3,8,512]{2,1,0:T(8,128)(2,1)S(1)}, u32[]{:S(2)}, u32[]{:S(2)}) collective-permute-start(bf16[3,8,512]{2,1,0:T(8,128)(2,1)S(1)} %get-tuple-element.96), channel_id=1, source_target_pairs={{0,28},{4,0},{8,4},{12,8},{16,12},{20,16},{24,20},{28,24},{1,29},{... | collective-permute-start | bytes 73736 | tf_op jit(solution)/shard_map/ppermute | solution.py:409
  7.5 0.0 collective-permute-start.1
  7.6 0.1 pad_add_fusion.2
  7.6 0.1 not_and_fusion
  7.7 0.7 collective-permute-done
  8.5 4.4 %collective-permute-done.1 = bf16[3,8,512]{2,1,0:T(8,128)(2,1)S(1)} collective-permute-done((bf16[3,8,512]{2,1,0:T(8,128)(2,1)S(1)}, bf16[3,8,512]{2,1,0:T(8,128)(2,1)S(1)}, u32[]{:S(2)}, u32[]{:S(2)}) %collective-permute-start.1) | collective-permute-done | bytes 24608 | tf_op jit(solution)/shard_map/ppermute | solution.py:409
  12.9 4.0 %collective-permute-start.2 = (bf16[3,8,512]{2,1,0:T(8,128)(2,1)S(1)}, bf16[3,8,512]{2,1,0:T(8,128)(2,1)S(1)}, u32[]{:S(2)}, u32[]{:S(2)}) collective-permute-start(bf16[3,8,512]{2,1,0:T(8,128)(2,1)S(1)} %get-tuple-element.93), channel_id=1, source_target_pairs={{1,0},{2,1},{3,2},{5,4},{6,5},{7,6},{9,8},{10,9},{11,10},{13,12},{... | collective-permute-start | bytes 73736 | tf_op jit(solution)/shard_map/ppermute | solution.py:415
  17.0 3.0 %collective-permute-start.3 = (bf16[3,8,512]{2,1,0:T(8,128)(2,1)S(1)}, bf16[3,8,512]{2,1,0:T(8,128)(2,1)S(1)}, u32[]{:S(2)}, u32[]{:S(2)}) collective-permute-start(bf16[3,8,512]{2,1,0:T(8,128)(2,1)S(1)} %get-tuple-element.94), channel_id=1, source_target_pairs={{0,1},{1,2},{2,3},{4,5},{5,6},{6,7},{8,9},{9,10},{10,11},{12,13},{... | collective-permute-start | bytes 73736 | tf_op jit(solution)/shard_map/ppermute | solution.py:415
  20.0 0.0 collective-permute-done.2
  20.0 0.9 collective-permute-done.3
  20.9 0.7 select_bitcast_fusion.1
  21.7 0.1 slice_convert_fusion.2
  21.8 0.1 fusion.61
  22.1 6.3 %sort.78 = (s32[4608]{0:T(1024)S(1)}, s32[4608]{0:T(1024)S(1)}, f32[4608]{0:T(1024)S(1)}, f32[4608]{0:T(1024)S(1)}, f32[4608]{0:T(1024)S(1)}, /*index=5*/f32[4608]{0:T(1024)S(1)}) sort(s32[4608]{0:T(1024)S(1)} %fusion.18, s32[4608]{0:T(1024)S(1)} %iota.121, f32[4608]{0:T(1024)S(1)} %reshape.729, f32[4608]{0:T(1024)S(1)} %reshape.730, f32[4608]{0:T(1024)S(1)} %reshape.731, ...), dimensions={0}, to_apply=%region_0.1 | sort | flops 59904 | bytes 221184 | tf_op jit(solution)/shard_map/sort | solution.py:450
  28.4 0.2 fusion.28
  28.9 0.2 stack.95
  29.2 4.2 %collective-permute-start.4 = (bf16[36,8,128]{2,1,0:T(8,128)(2,1)S(1)}, bf16[36,8,128]{2,1,0:T(8,128)(2,1)S(1)}, u32[]{:S(2)}, u32[]{:S(2)}) collective-permute-start(bf16[36,8,128]{2,1,0:T(8,128)(2,1)S(1)} %bitcast.161), channel_id=1, source_target_pairs={{0,1},{1,2},{2,3},{4,5},{5,6},{6,7},{8,9},{9,10},{10,11},{12,13},{... | collective-permute-start | bytes 221192 | tf_op jit(solution)/shard_map/ppermute | solution.py:415
  33.4 1.9 %collective-permute-start.5 = (bf16[36,8,128]{2,1,0:T(8,128)(2,1)S(1)}, bf16[36,8,128]{2,1,0:T(8,128)(2,1)S(1)}, u32[]{:S(2)}, u32[]{:S(2)}) collective-permute-start(bf16[36,8,128]{2,1,0:T(8,128)(2,1)S(1)} %bitcast.162), channel_id=1, source_target_pairs={{1,0},{2,1},{3,2},{5,4},{6,5},{7,6},{9,8},{10,9},{11,10},{13,12},{... | collective-permute-start | bytes 221192 | tf_op jit(solution)/shard_map/ppermute | solution.py:415
  35.3 0.2 convert_reduce_fusion.3
  35.5 0.1 fusion.57
  35.6 0.2 convert_reduce_fusion.2
  35.8 0.1 add_select_fusion.21
  35.9 0.1 select_reduce_fusion.4.list_ref
  36.0 0.2 select_reduce_fusion.5.refs_0_
  36.2 0.0 collective-permute-done.4
  36.2 2.9 %collective-permute-done.5 = bf16[36,8,128]{2,1,0:T(8,128)(2,1)S(1)} collective-permute-done((bf16[36,8,128]{2,1,0:T(8,128)(2,1)S(1)}, bf16[36,8,128]{2,1,0:T(8,128)(2,1)S(1)}, u32[]{:S(2)}, u32[]{:S(2)}) %collective-permute-start.5) | collective-permute-done | bytes 73760 | tf_op jit(solution)/shard_map/ppermute | solution.py:415
  39.1 0.1 collective-permute-start.6
  39.1 4.1 %collective-permute-start.7 = (bf16[3,36,8,128]{3,2,1,0:T(8,128)(2,1)S(1)}, bf16[3,36,8,128]{3,2,1,0:T(8,128)(2,1)S(1)}, u32[]{:S(2)}, u32[]{:S(2)}) collective-permute-start(bf16[3,36,8,128]{3,2,1,0:T(8,128)(2,1)S(1)} %pad_maximum_fusion.1), channel_id=1, source_target_pairs={{0,28},{4,0},{8,4},{12,8},{16,12},{20,16},{24,20},{28,24},{1,29},{... | collective-permute-start | bytes 663560 | tf_op jit(solution)/shard_map/ppermute | solution.py:409
  43.3 15.8 %spread_own.1.old_ref = f32[84,64,512]{2,1,0:T(8,128)} custom-call(s32[74]{0:T(128)S(1)} %select_reduce_fusion.4.list_ref, bf16[36,8,128]{2,1,0:T(8,128)(2,1)S(1)} %bitcast.164, bf16[8,384]{1,0:T(8,128)(2,1)S(1)} %copy-done.2), custom_call_target="tpu_custom_call" | custom-call | flops 10000000000 | bytes 30000000 | tf_op jit(solution)/shard_map/spread_own/pallas_call | solution.py:310
  59.1 0.0 copy-start
  59.1 0.0 copy-start.1
  59.1 0.0 collective-permute-done.6
  59.1 0.0 collective-permute-done.7
  59.1 0.1 pad_maximum_fusion
  59.2 0.3 slice_convert_fusion
  59.5 0.3 fusion.60
  59.8 0.5 select_reduce_fusion.3
  60.3 0.1 concatenate.99
  60.3 0.1 reshape.727
  60.5 0.2 convert_reduce_fusion.1
  60.7 0.2 select_reduce_fusion.1
  60.9 0.1 fusion.55
  61.0 0.4 convert_reduce_fusion
  61.5 0.1 add_select_fusion.15
  61.6 0.4 select_reduce_fusion
  62.0 49.9 %main.1 = (f32[4,64,16,512]{3,2,1,0:T(8,128)}, f32[324,8,128]{2,1,0:T(8,128)S(1)}, bf16[92,16,1536]{2,1,0:T(8,128)(2,1)S(1)}) custom-call(s32[650]{0:T(1024)S(1)} %select_add_fusion.units_ref, s32[326]{0:T(512)S(1)} %select_add_fusion.1.list_ref, bf16[324,8,128]{2,1,0:T(8,128)(2,1)S(1)} %bitcast.160, bf16[8,384]{1,0:T(8,128)(2,1)S(1)} %copy-done.2, ...), custom_call_target="tpu_custom_call" | custom-call | flops 40000000000 | bytes 60000000 | tf_op jit(solution)/shard_map/main/pallas_call | solution.py:327
  111.9 0.1 fusion.59
  112.0 0.1 collective-permute-start.8
  112.1 4.1 %collective-permute-start.9 = (f32[3,36,3,128]{3,2,1,0:T(4,128)S(1)}, f32[3,36,3,128]{3,2,1,0:T(4,128)S(1)}, u32[]{:S(2)}, u32[]{:S(2)}) collective-permute-start(f32[3,36,3,128]{3,2,1,0:T(4,128)S(1)} %bitcast.169), channel_id=1, source_target_pairs={{0,28},{4,0},{8,4},{12,8},{16,12},{20,16},{24,20},{28,24},{1,29},{... | collective-permute-start | bytes 497672 | tf_op jit(solution)/shard_map/ppermute | solution.py:409
  116.2 6.9 %sample_own.2 = f32[36,8,128]{2,1,0:T(8,128)S(1)} custom-call(s32[38]{0:T(128)S(1)} %select_reduce_fusion.5.refs_0_, bf16[36,8,128]{2,1,0:T(8,128)(2,1)S(1)} %bitcast.165, bf16[8,384]{1,0:T(8,128)(2,1)S(1)} %copy-done.2, bf16[92,16,1536]{2,1,0:T(8,128)(2,1)S(1)} %get-tuple-element.45.refs_3_), custom_call_target="tpu_custom_call" | custom-call | flops 10000000000 | bytes 30000000 | tf_op jit(solution)/shard_map/sample_own/pallas_call | solution.py:364
  123.2 0.0 collective-permute-done.8
  123.2 0.1 add_add_fusion
  123.3 1.9 %collective-permute-start.10 = (f32[36,3,128]{2,1,0:T(4,128)S(1)}, f32[36,3,128]{2,1,0:T(4,128)S(1)}, u32[]{:S(2)}, u32[]{:S(2)}) collective-permute-start(f32[36,3,128]{2,1,0:T(4,128)S(1)} %get-tuple-element.84), channel_id=1, source_target_pairs={{0,1},{1,2},{2,3},{4,5},{5,6},{6,7},{8,9},{9,10},{10,11},{12,13},{... | collective-permute-start | bytes 165896 | tf_op jit(solution)/shard_map/ppermute | solution.py:415
  125.2 2.4 %collective-permute-start.11 = (f32[36,3,128]{2,1,0:T(4,128)S(1)}, f32[36,3,128]{2,1,0:T(4,128)S(1)}, u32[]{:S(2)}, u32[]{:S(2)}) collective-permute-start(f32[36,3,128]{2,1,0:T(4,128)S(1)} %get-tuple-element.85), channel_id=1, source_target_pairs={{1,0},{2,1},{3,2},{5,4},{6,5},{7,6},{9,8},{10,9},{11,10},{13,12},{... | collective-permute-start | bytes 165896 | tf_op jit(solution)/shard_map/ppermute | solution.py:415
  127.7 6.7 %sample_own.3 = f32[36,8,128]{2,1,0:T(8,128)S(1)} custom-call(s32[38]{0:T(128)S(1)} %select_reduce_fusion.5.refs_0_, bf16[36,8,128]{2,1,0:T(8,128)(2,1)S(1)} %bitcast.166, bf16[8,384]{1,0:T(8,128)(2,1)S(1)} %copy-done.2, bf16[92,16,1536]{2,1,0:T(8,128)(2,1)S(1)} %get-tuple-element.45.refs_3_), custom_call_target="tpu_custom_call" | custom-call | flops 10000000000 | bytes 30000000 | tf_op jit(solution)/shard_map/sample_own/pallas_call | solution.py:364
  134.4 0.0 collective-permute-done.11
  134.4 0.1 fusion.5
  134.4 0.1 slice_reduce_fusion
  134.6 7.6 %sort.79 = (s32[4608]{0:T(1024)}, f32[4608]{0:T(1024)S(1)}, f32[4608]{0:T(1024)S(1)}, f32[4608]{0:T(1024)S(1)}, s32[4608]{0:T(1024)}) sort(s32[4608]{0:T(1024)S(1)} %get-tuple-element.42, f32[4608]{0:T(1024)S(1)} %bitcast.175, f32[4608]{0:T(1024)S(1)} %bitcast.174, f32[4608]{0:T(1024)S(1)} %bitcast.173, s32[4608]{0:T(1024)S(1)} %iota.136), dimensions={0}, to_apply=%region_13.14 | sort | flops 59904 | bytes 184320 | tf_op jit(solution)/shard_map/sort | solution.py:489
  142.3 0.1 pad_maximum_fusion.3
  142.4 0.7 broadcast_in_dim.342
  (66 shorter events, 0.7 us)
Async XLA Ops:
  0.6 42.7 %copy-start.2 = (bf16[8,384]{1,0:T(8,128)(2,1)S(1)}, bf16[8,384]{1,0:T(8,128)(2,1)}, u32[]{:S(2)}) copy-start(bf16[8,384]{1,0:T(8,128)(2,1)} %constant.251.clone.pick_ref.refs_2_) | copy-start | bytes 18436
  2.4 6.1 %collective-permute-start = (bf16[3,8,512]{2,1,0:T(8,128)(2,1)S(1)}, bf16[3,8,512]{2,1,0:T(8,128)(2,1)S(1)}, u32[]{:S(2)}, u32[]{:S(2)}) collective-permute-start(bf16[3,8,512]{2,1,0:T(8,128)(2,1)S(1)} %get-tuple-element.96), channel_id=1, source_target_pairs={{0,28},{4,0},{8,4},{12,8},{16,12},{20,16},{24,20},{28,24},{1,29},{... | collective-permute-start | bytes 73736 | tf_op jit(solution)/shard_map/ppermute | solution.py:409
  7.5 5.4 %collective-permute-start.1 = (bf16[3,8,512]{2,1,0:T(8,128)(2,1)S(1)}, bf16[3,8,512]{2,1,0:T(8,128)(2,1)S(1)}, u32[]{:S(2)}, u32[]{:S(2)}) collective-permute-start(bf16[3,8,512]{2,1,0:T(8,128)(2,1)S(1)} %get-tuple-element.97), channel_id=1, source_target_pairs={{0,4},{4,8},{8,12},{12,16},{16,20},{20,24},{24,28},{28,0},{1,5},{5... | collective-permute-start | bytes 73736 | tf_op jit(solution)/shard_map/ppermute | solution.py:409
  12.9 7.1 %collective-permute-start.2 = (bf16[3,8,512]{2,1,0:T(8,128)(2,1)S(1)}, bf16[3,8,512]{2,1,0:T(8,128)(2,1)S(1)}, u32[]{:S(2)}, u32[]{:S(2)}) collective-permute-start(bf16[3,8,512]{2,1,0:T(8,128)(2,1)S(1)} %get-tuple-element.93), channel_id=1, source_target_pairs={{1,0},{2,1},{3,2},{5,4},{6,5},{7,6},{9,8},{10,9},{11,10},{13,12},{... | collective-permute-start | bytes 73736 | tf_op jit(solution)/shard_map/ppermute | solution.py:415
  17.0 3.9 %collective-permute-start.3 = (bf16[3,8,512]{2,1,0:T(8,128)(2,1)S(1)}, bf16[3,8,512]{2,1,0:T(8,128)(2,1)S(1)}, u32[]{:S(2)}, u32[]{:S(2)}) collective-permute-start(bf16[3,8,512]{2,1,0:T(8,128)(2,1)S(1)} %get-tuple-element.94), channel_id=1, source_target_pairs={{0,1},{1,2},{2,3},{4,5},{5,6},{6,7},{8,9},{9,10},{10,11},{12,13},{... | collective-permute-start | bytes 73736 | tf_op jit(solution)/shard_map/ppermute | solution.py:415
  29.2 7.0 %collective-permute-start.4 = (bf16[36,8,128]{2,1,0:T(8,128)(2,1)S(1)}, bf16[36,8,128]{2,1,0:T(8,128)(2,1)S(1)}, u32[]{:S(2)}, u32[]{:S(2)}) collective-permute-start(bf16[36,8,128]{2,1,0:T(8,128)(2,1)S(1)} %bitcast.161), channel_id=1, source_target_pairs={{0,1},{1,2},{2,3},{4,5},{5,6},{6,7},{8,9},{9,10},{10,11},{12,13},{... | collective-permute-start | bytes 221192 | tf_op jit(solution)/shard_map/ppermute | solution.py:415
  33.4 5.7 %collective-permute-start.5 = (bf16[36,8,128]{2,1,0:T(8,128)(2,1)S(1)}, bf16[36,8,128]{2,1,0:T(8,128)(2,1)S(1)}, u32[]{:S(2)}, u32[]{:S(2)}) collective-permute-start(bf16[36,8,128]{2,1,0:T(8,128)(2,1)S(1)} %bitcast.162), channel_id=1, source_target_pairs={{1,0},{2,1},{3,2},{5,4},{6,5},{7,6},{9,8},{10,9},{11,10},{13,12},{... | collective-permute-start | bytes 221192 | tf_op jit(solution)/shard_map/ppermute | solution.py:415
  39.1 20.0 %collective-permute-start.6 = (bf16[3,36,8,128]{3,2,1,0:T(8,128)(2,1)S(1)}, bf16[3,36,8,128]{3,2,1,0:T(8,128)(2,1)S(1)}, u32[]{:S(2)}, u32[]{:S(2)}) collective-permute-start(bf16[3,36,8,128]{3,2,1,0:T(8,128)(2,1)S(1)} %pad_maximum_fusion.1), channel_id=1, source_target_pairs={{0,4},{4,8},{8,12},{12,16},{16,20},{20,24},{24,28},{28,0},{1,5},{5... | collective-permute-start | bytes 663560 | tf_op jit(solution)/shard_map/ppermute | solution.py:409
  39.1 20.0 %collective-permute-start.7 = (bf16[3,36,8,128]{3,2,1,0:T(8,128)(2,1)S(1)}, bf16[3,36,8,128]{3,2,1,0:T(8,128)(2,1)S(1)}, u32[]{:S(2)}, u32[]{:S(2)}) collective-permute-start(bf16[3,36,8,128]{3,2,1,0:T(8,128)(2,1)S(1)} %pad_maximum_fusion.1), channel_id=1, source_target_pairs={{0,28},{4,0},{8,4},{12,8},{16,12},{20,16},{24,20},{28,24},{1,29},{... | collective-permute-start | bytes 663560 | tf_op jit(solution)/shard_map/ppermute | solution.py:409
  59.1 2.9 %copy-start = (f32[3,512]{1,0:T(4,128)S(1)}, f32[3,512]{1,0:T(4,128)}, u32[]{:S(2)}) copy-start(f32[3,512]{1,0:T(4,128)} %field_ref.1) | copy-start | bytes 18436
  59.1 2.9 %copy-start.1 = (f32[3,512]{1,0:T(4,128)S(1)}, f32[3,512]{1,0:T(4,128)}, u32[]{:S(2)}) copy-start(f32[3,512]{1,0:T(4,128)} %ground_ref.1) | copy-start | bytes 18436
  112.0 11.2 %collective-permute-start.8 = (f32[3,36,3,128]{3,2,1,0:T(4,128)S(1)}, f32[3,36,3,128]{3,2,1,0:T(4,128)S(1)}, u32[]{:S(2)}, u32[]{:S(2)}) collective-permute-start(f32[3,36,3,128]{3,2,1,0:T(4,128)S(1)} %bitcast.171), channel_id=1, source_target_pairs={{0,4},{4,8},{8,12},{12,16},{16,20},{20,24},{24,28},{28,0},{1,5},{5... | collective-permute-start | bytes 497672 | tf_op jit(solution)/shard_map/ppermute | solution.py:409
  112.1 11.1 %collective-permute-start.9 = (f32[3,36,3,128]{3,2,1,0:T(4,128)S(1)}, f32[3,36,3,128]{3,2,1,0:T(4,128)S(1)}, u32[]{:S(2)}, u32[]{:S(2)}) collective-permute-start(f32[3,36,3,128]{3,2,1,0:T(4,128)S(1)} %bitcast.169), channel_id=1, source_target_pairs={{0,28},{4,0},{8,4},{12,8},{16,12},{20,16},{24,20},{28,24},{1,29},{... | collective-permute-start | bytes 497672 | tf_op jit(solution)/shard_map/ppermute | solution.py:409
  123.3 11.1 %collective-permute-start.10 = (f32[36,3,128]{2,1,0:T(4,128)S(1)}, f32[36,3,128]{2,1,0:T(4,128)S(1)}, u32[]{:S(2)}, u32[]{:S(2)}) collective-permute-start(f32[36,3,128]{2,1,0:T(4,128)S(1)} %get-tuple-element.84), channel_id=1, source_target_pairs={{0,1},{1,2},{2,3},{4,5},{5,6},{6,7},{8,9},{9,10},{10,11},{12,13},{... | collective-permute-start | bytes 165896 | tf_op jit(solution)/shard_map/ppermute | solution.py:415
  125.2 9.1 %collective-permute-start.11 = (f32[36,3,128]{2,1,0:T(4,128)S(1)}, f32[36,3,128]{2,1,0:T(4,128)S(1)}, u32[]{:S(2)}, u32[]{:S(2)}) collective-permute-start(f32[36,3,128]{2,1,0:T(4,128)S(1)} %get-tuple-element.85), channel_id=1, source_target_pairs={{1,0},{2,1},{3,2},{5,4},{6,5},{7,6},{9,8},{10,9},{11,10},{13,12},{... | collective-permute-start | bytes 165896 | tf_op jit(solution)/shard_map/ppermute | solution.py:415

commit v7 on v6

--- a/solution.py
+++ b/solution.py
@@ -161,13 +161,13 @@
         ypl = (lane_i % CY).astype(jnp.float32)
         wy = gauss(ypl - (yrep + sy)) * scale
         xoff = xrep - xpl
-        lhs, rhs = [], []
-        for k in range(2):
-            a = jnp.where(xoff == (x0 + k * BX).astype(jnp.float32) - sx, wy, 0.0)
-            lhs.extend(hi_lo(a))
-            f = fmat[pl.ds(x0 + k * BX, BX)].reshape(BP, 3 * NZ)
-            rhs.extend([f, f])
-        g = jnp.dot(jnp.concatenate(lhs, axis=1), jnp.concatenate(rhs, axis=0), preferred_element_type=jnp.float32)
+        near, far = (
+            hi_lo(jnp.where(xoff == (x0 + k * BX).astype(jnp.float32) - sx, wy, 0.0)) for k in range(2)
+        )
+        f = fmat[pl.ds(x0, 2 * BX)].reshape(2 * BP, 3 * NZ)
+        coarse, fine = (jnp.concatenate([near[k], far[k]], axis=1) for k in range(2))
+        g = jnp.dot(jnp.concatenate([coarse, fine], axis=0), f, preferred_element_type=jnp.float32)
+        g = g[:TILE] + g[TILE:]
         sums = [None] * 3
         for q in range(NZ // 128):
             wz = gauss(lane + (128.0 * q) - zrep) * scale

time: 145 us -> 139 us (0.959); the launches traced: 143 us -> 139 us
  Pallas kernels: 79.3 us -> 74.7 us
    pallas_call x1, Pallas kernels: 49.9 us -> 47.1 us  [main_call(): pl.pallas_call(main_kernel, grid=(steps + 2,), in_specs=[smem()] * 2 + [w...]
  transfers between devices with their start and end apart: 12 -> 12, of which waited for: 4 -> 4; matrix products, arithmetic and copies ran while one was open for 1% -> 1% of each run, Pallas kernels for 21% -> 20%
where the time goes in v7:
time: 139 us
  Pallas kernels  74.7 us (54%)
  starting transfers between devices  31.4 us (23%)
  other arithmetic  20.4 us (15%)
  waiting for transfers between devices  8.96 us (6%)
  local copies, waits for them, and re-layouts  1.97 us (1%)
    pallas_call x1, Pallas kernels, main_call(): pl.pallas_call(main_kernel, grid=(steps + 2,), in_specs=[smem()] * 2 + [w...  47.1 us
    ppermute x6, starting transfers between devices, line(): lax.ppermute(value, 'span', [(i, i + steps) for i in range(first, last)])  17.9 us
    pallas_call x1, Pallas kernels, spread_own_call(): pl.pallas_call(spread_own_kernel, grid=(1,), in_specs=[smem(), whole(tabl...  15.4 us
    ppermute x6, starting transfers between devices, ring(): lax.ppermute(value, 'stream', [(i, (i + steps) % count) for i in range(co...  13.6 us
    pallas_call x2, Pallas kernels, sample_own_call(): pl.pallas_call(kernel, grid=(1,), in_specs=[smem(), whole(table.shape), w...  12.2 us
    sort x1, other arithmetic, on_device(): _, *vel = lax.sort((order, own[0], own[1], own[2]), num_keys=1)  7.64 us
    sort x5, other arithmetic, on_device(): lax.sort((key, order) + tuple((inbound[c].astype(f32) for c in range(4)))...  6.36 us
    ppermute x6, waiting for transfers between devices, ring(): lax.ppermute(value, 'stream', [(i, (i + steps) % count) for i in range(co...  5.19 us
  transfers between devices with their start and end apart: 12, of which 4 were waited for; matrix products, arithmetic and copies ran while one was open for 1% of the time, Pallas kernels for 20%

profile of v7, /device:TPU:1, one launch (start us, length us, event | category | flops | bytes accessed | tf_op | source)
XLA Modules:
  0.0 138.8 jit_solution(10969017245670002604)
XLA Ops:
  0.6 0.0 copy-start.2
  0.7 0.8 fusion.7
  1.5 0.9 fusion.1
  2.4 5.2 %collective-permute-start = (bf16[3,8,512]{2,1,0:T(8,128)(2,1)S(1)}, bf16[3,8,512]{2,1,0:T(8,128)(2,1)S(1)}, u32[]{:S(2)}, u32[]{:S(2)}) collective-permute-start(bf16[3,8,512]{2,1,0:T(8,128)(2,1)S(1)} %get-tuple-element.96), channel_id=1, source_target_pairs={{0,28},{4,0},{8,4},{12,8},{16,12},{20,16},{24,20},{28,24},{1,29},{... | collective-permute-start | bytes 73736 | tf_op jit(solution)/shard_map/ppermute | solution.py:409
  7.5 0.0 collective-permute-start.1
  7.6 0.1 pad_add_fusion.2
  7.6 0.1 not_and_fusion
  7.7 0.7 collective-permute-done
  8.5 4.4 %collective-permute-done.1 = bf16[3,8,512]{2,1,0:T(8,128)(2,1)S(1)} collective-permute-done((bf16[3,8,512]{2,1,0:T(8,128)(2,1)S(1)}, bf16[3,8,512]{2,1,0:T(8,128)(2,1)S(1)}, u32[]{:S(2)}, u32[]{:S(2)}) %collective-permute-start.1) | collective-permute-done | bytes 24608 | tf_op jit(solution)/shard_map/ppermute | solution.py:409
  12.9 4.0 %collective-permute-start.2 = (bf16[3,8,512]{2,1,0:T(8,128)(2,1)S(1)}, bf16[3,8,512]{2,1,0:T(8,128)(2,1)S(1)}, u32[]{:S(2)}, u32[]{:S(2)}) collective-permute-start(bf16[3,8,512]{2,1,0:T(8,128)(2,1)S(1)} %get-tuple-element.93), channel_id=1, source_target_pairs={{1,0},{2,1},{3,2},{5,4},{6,5},{7,6},{9,8},{10,9},{11,10},{13,12},{... | collective-permute-start | bytes 73736 | tf_op jit(solution)/shard_map/ppermute | solution.py:415
  17.0 3.0 %collective-permute-start.3 = (bf16[3,8,512]{2,1,0:T(8,128)(2,1)S(1)}, bf16[3,8,512]{2,1,0:T(8,128)(2,1)S(1)}, u32[]{:S(2)}, u32[]{:S(2)}) collective-permute-start(bf16[3,8,512]{2,1,0:T(8,128)(2,1)S(1)} %get-tuple-element.94), channel_id=1, source_target_pairs={{0,1},{1,2},{2,3},{4,5},{5,6},{6,7},{8,9},{9,10},{10,11},{12,13},{... | collective-permute-start | bytes 73736 | tf_op jit(solution)/shard_map/ppermute | solution.py:415
  20.0 0.0 collective-permute-done.2
  20.0 0.9 collective-permute-done.3
  20.9 0.7 select_bitcast_fusion.1
  21.7 0.1 slice_convert_fusion.2
  21.8 0.1 fusion.61
  22.1 6.3 %sort.78 = (s32[4608]{0:T(1024)S(1)}, s32[4608]{0:T(1024)S(1)}, f32[4608]{0:T(1024)S(1)}, f32[4608]{0:T(1024)S(1)}, f32[4608]{0:T(1024)S(1)}, /*index=5*/f32[4608]{0:T(1024)S(1)}) sort(s32[4608]{0:T(1024)S(1)} %fusion.18, s32[4608]{0:T(1024)S(1)} %iota.121, f32[4608]{0:T(1024)S(1)} %reshape.729, f32[4608]{0:T(1024)S(1)} %reshape.730, f32[4608]{0:T(1024)S(1)} %reshape.731, ...), dimensions={0}, to_apply=%region_0.1 | sort | flops 59904 | bytes 221184 | tf_op jit(solution)/shard_map/sort | solution.py:450
  28.4 0.2 fusion.28
  28.9 0.2 stack.95
  29.2 4.2 %collective-permute-start.4 = (bf16[36,8,128]{2,1,0:T(8,128)(2,1)S(1)}, bf16[36,8,128]{2,1,0:T(8,128)(2,1)S(1)}, u32[]{:S(2)}, u32[]{:S(2)}) collective-permute-start(bf16[36,8,128]{2,1,0:T(8,128)(2,1)S(1)} %bitcast.161), channel_id=1, source_target_pairs={{0,1},{1,2},{2,3},{4,5},{5,6},{6,7},{8,9},{9,10},{10,11},{12,13},{... | collective-permute-start | bytes 221192 | tf_op jit(solution)/shard_map/ppermute | solution.py:415
  33.4 1.9 %collective-permute-start.5 = (bf16[36,8,128]{2,1,0:T(8,128)(2,1)S(1)}, bf16[36,8,128]{2,1,0:T(8,128)(2,1)S(1)}, u32[]{:S(2)}, u32[]{:S(2)}) collective-permute-start(bf16[36,8,128]{2,1,0:T(8,128)(2,1)S(1)} %bitcast.162), channel_id=1, source_target_pairs={{1,0},{2,1},{3,2},{5,4},{6,5},{7,6},{9,8},{10,9},{11,10},{13,12},{... | collective-permute-start | bytes 221192 | tf_op jit(solution)/shard_map/ppermute | solution.py:415
  35.3 0.2 convert_reduce_fusion.3
  35.5 0.1 fusion.57
  35.6 0.2 convert_reduce_fusion.2
  35.8 0.1 add_select_fusion.21
  35.9 0.1 select_reduce_fusion.4.list_ref
  36.0 0.2 select_reduce_fusion.5.refs_0_
  36.2 0.0 collective-permute-done.4
  36.2 2.9 %collective-permute-done.5 = bf16[36,8,128]{2,1,0:T(8,128)(2,1)S(1)} collective-permute-done((bf16[36,8,128]{2,1,0:T(8,128)(2,1)S(1)}, bf16[36,8,128]{2,1,0:T(8,128)(2,1)S(1)}, u32[]{:S(2)}, u32[]{:S(2)}) %collective-permute-start.5) | collective-permute-done | bytes 73760 | tf_op jit(solution)/shard_map/ppermute | solution.py:415
  39.1 0.1 collective-permute-start.6
  39.1 4.1 %collective-permute-start.7 = (bf16[3,36,8,128]{3,2,1,0:T(8,128)(2,1)S(1)}, bf16[3,36,8,128]{3,2,1,0:T(8,128)(2,1)S(1)}, u32[]{:S(2)}, u32[]{:S(2)}) collective-permute-start(bf16[3,36,8,128]{3,2,1,0:T(8,128)(2,1)S(1)} %pad_maximum_fusion.1), channel_id=1, source_target_pairs={{0,28},{4,0},{8,4},{12,8},{16,12},{20,16},{24,20},{28,24},{1,29},{... | collective-permute-start | bytes 663560 | tf_op jit(solution)/shard_map/ppermute | solution.py:409
  43.3 15.4 %spread_own.1.old_ref = f32[84,64,512]{2,1,0:T(8,128)} custom-call(s32[74]{0:T(128)S(1)} %select_reduce_fusion.4.list_ref, bf16[36,8,128]{2,1,0:T(8,128)(2,1)S(1)} %bitcast.164, bf16[8,384]{1,0:T(8,128)(2,1)S(1)} %copy-done.2), custom_call_target="tpu_custom_call" | custom-call | flops 10000000000 | bytes 30000000 | tf_op jit(solution)/shard_map/spread_own/pallas_call | solution.py:310
  58.7 0.0 copy-start
  58.7 0.0 copy-start.1
  58.7 0.0 collective-permute-done.7
  58.7 0.1 pad_maximum_fusion
  58.8 0.3 slice_convert_fusion
  59.1 0.3 fusion.60
  59.4 0.5 select_reduce_fusion.3
  59.9 0.1 concatenate.99
  59.9 0.1 reshape.727
  60.0 0.2 convert_reduce_fusion.1
  60.3 0.2 select_reduce_fusion.1
  60.5 0.1 fusion.55
  60.6 0.4 convert_reduce_fusion
  61.1 0.1 add_select_fusion.15
  61.1 0.4 select_reduce_fusion
  61.6 47.1 %main.1 = (f32[4,64,16,512]{3,2,1,0:T(8,128)}, f32[324,8,128]{2,1,0:T(8,128)S(1)}, bf16[92,16,1536]{2,1,0:T(8,128)(2,1)S(1)}) custom-call(s32[650]{0:T(1024)S(1)} %select_add_fusion.units_ref, s32[326]{0:T(512)S(1)} %select_add_fusion.1.list_ref, bf16[324,8,128]{2,1,0:T(8,128)(2,1)S(1)} %bitcast.160, bf16[8,384]{1,0:T(8,128)(2,1)S(1)} %copy-done.2, ...), custom_call_target="tpu_custom_call" | custom-call | flops 40000000000 | bytes 60000000 | tf_op jit(solution)/shard_map/main/pallas_call | solution.py:327
  108.7 0.1 fusion.59
  108.8 0.1 collective-permute-start.8
  108.9 4.1 %collective-permute-start.9 = (f32[3,36,3,128]{3,2,1,0:T(4,128)S(1)}, f32[3,36,3,128]{3,2,1,0:T(4,128)S(1)}, u32[]{:S(2)}, u32[]{:S(2)}) collective-permute-start(f32[3,36,3,128]{3,2,1,0:T(4,128)S(1)} %bitcast.169), channel_id=1, source_target_pairs={{0,28},{4,0},{8,4},{12,8},{16,12},{20,16},{24,20},{28,24},{1,29},{... | collective-permute-start | bytes 497672 | tf_op jit(solution)/shard_map/ppermute | solution.py:409
  113.0 7.1 %sample_own.2 = f32[36,8,128]{2,1,0:T(8,128)S(1)} custom-call(s32[38]{0:T(128)S(1)} %select_reduce_fusion.5.refs_0_, bf16[36,8,128]{2,1,0:T(8,128)(2,1)S(1)} %bitcast.165, bf16[8,384]{1,0:T(8,128)(2,1)S(1)} %copy-done.2, bf16[92,16,1536]{2,1,0:T(8,128)(2,1)S(1)} %get-tuple-element.45.refs_3_), custom_call_target="tpu_custom_call" | custom-call | flops 10000000000 | bytes 30000000 | tf_op jit(solution)/shard_map/sample_own/pallas_call | solution.py:364
  120.2 0.0 collective-permute-done.8
  120.2 0.0 collective-permute-done.9
  120.2 0.1 add_add_fusion
  120.3 2.8 %collective-permute-start.10 = (f32[36,3,128]{2,1,0:T(4,128)S(1)}, f32[36,3,128]{2,1,0:T(4,128)S(1)}, u32[]{:S(2)}, u32[]{:S(2)}) collective-permute-start(f32[36,3,128]{2,1,0:T(4,128)S(1)} %get-tuple-element.84), channel_id=1, source_target_pairs={{0,1},{1,2},{2,3},{4,5},{5,6},{6,7},{8,9},{9,10},{10,11},{12,13},{... | collective-permute-start | bytes 165896 | tf_op jit(solution)/shard_map/ppermute | solution.py:415
  123.1 1.9 %collective-permute-start.11 = (f32[36,3,128]{2,1,0:T(4,128)S(1)}, f32[36,3,128]{2,1,0:T(4,128)S(1)}, u32[]{:S(2)}, u32[]{:S(2)}) collective-permute-start(f32[36,3,128]{2,1,0:T(4,128)S(1)} %get-tuple-element.85), channel_id=1, source_target_pairs={{1,0},{2,1},{3,2},{5,4},{6,5},{7,6},{9,8},{10,9},{11,10},{13,12},{... | collective-permute-start | bytes 165896 | tf_op jit(solution)/shard_map/ppermute | solution.py:415
  125.0 5.1 %sample_own.3 = f32[36,8,128]{2,1,0:T(8,128)S(1)} custom-call(s32[38]{0:T(128)S(1)} %select_reduce_fusion.5.refs_0_, bf16[36,8,128]{2,1,0:T(8,128)(2,1)S(1)} %bitcast.166, bf16[8,384]{1,0:T(8,128)(2,1)S(1)} %copy-done.2, bf16[92,16,1536]{2,1,0:T(8,128)(2,1)S(1)} %get-tuple-element.45.refs_3_), custom_call_target="tpu_custom_call" | custom-call | flops 10000000000 | bytes 30000000 | tf_op jit(solution)/shard_map/sample_own/pallas_call | solution.py:364
  130.1 0.0 collective-permute-done.11
  130.1 0.1 fusion.5
  130.2 0.1 slice_reduce_fusion
  130.3 7.6 %sort.79 = (s32[4608]{0:T(1024)}, f32[4608]{0:T(1024)S(1)}, f32[4608]{0:T(1024)S(1)}, f32[4608]{0:T(1024)S(1)}, s32[4608]{0:T(1024)}) sort(s32[4608]{0:T(1024)S(1)} %get-tuple-element.42, f32[4608]{0:T(1024)S(1)} %bitcast.175, f32[4608]{0:T(1024)S(1)} %bitcast.174, f32[4608]{0:T(1024)S(1)} %bitcast.173, s32[4608]{0:T(1024)S(1)} %iota.136), dimensions={0}, to_apply=%region_13.14 | sort | flops 59904 | bytes 184320 | tf_op jit(solution)/shard_map/sort | solution.py:489
  138.1 0.1 pad_maximum_fusion.3
  138.1 0.7 broadcast_in_dim.342
  (66 shorter events, 0.7 us)
Async XLA Ops:
  0.6 42.7 %copy-start.2 = (bf16[8,384]{1,0:T(8,128)(2,1)S(1)}, bf16[8,384]{1,0:T(8,128)(2,1)}, u32[]{:S(2)}) copy-start(bf16[8,384]{1,0:T(8,128)(2,1)} %constant.251.clone.pick_ref.refs_2_) | copy-start | bytes 18436
  2.4 6.1 %collective-permute-start = (bf16[3,8,512]{2,1,0:T(8,128)(2,1)S(1)}, bf16[3,8,512]{2,1,0:T(8,128)(2,1)S(1)}, u32[]{:S(2)}, u32[]{:S(2)}) collective-permute-start(bf16[3,8,512]{2,1,0:T(8,128)(2,1)S(1)} %get-tuple-element.96), channel_id=1, source_target_pairs={{0,28},{4,0},{8,4},{12,8},{16,12},{20,16},{24,20},{28,24},{1,29},{... | collective-permute-start | bytes 73736 | tf_op jit(solution)/shard_map/ppermute | solution.py:409
  7.5 5.4 %collective-permute-start.1 = (bf16[3,8,512]{2,1,0:T(8,128)(2,1)S(1)}, bf16[3,8,512]{2,1,0:T(8,128)(2,1)S(1)}, u32[]{:S(2)}, u32[]{:S(2)}) collective-permute-start(bf16[3,8,512]{2,1,0:T(8,128)(2,1)S(1)} %get-tuple-element.97), channel_id=1, source_target_pairs={{0,4},{4,8},{8,12},{12,16},{16,20},{20,24},{24,28},{28,0},{1,5},{5... | collective-permute-start | bytes 73736 | tf_op jit(solution)/shard_map/ppermute | solution.py:409
  12.9 7.1 %collective-permute-start.2 = (bf16[3,8,512]{2,1,0:T(8,128)(2,1)S(1)}, bf16[3,8,512]{2,1,0:T(8,128)(2,1)S(1)}, u32[]{:S(2)}, u32[]{:S(2)}) collective-permute-start(bf16[3,8,512]{2,1,0:T(8,128)(2,1)S(1)} %get-tuple-element.93), channel_id=1, source_target_pairs={{1,0},{2,1},{3,2},{5,4},{6,5},{7,6},{9,8},{10,9},{11,10},{13,12},{... | collective-permute-start | bytes 73736 | tf_op jit(solution)/shard_map/ppermute | solution.py:415
  17.0 3.9 %collective-permute-start.3 = (bf16[3,8,512]{2,1,0:T(8,128)(2,1)S(1)}, bf16[3,8,512]{2,1,0:T(8,128)(2,1)S(1)}, u32[]{:S(2)}, u32[]{:S(2)}) collective-permute-start(bf16[3,8,512]{2,1,0:T(8,128)(2,1)S(1)} %get-tuple-element.94), channel_id=1, source_target_pairs={{0,1},{1,2},{2,3},{4,5},{5,6},{6,7},{8,9},{9,10},{10,11},{12,13},{... | collective-permute-start | bytes 73736 | tf_op jit(solution)/shard_map/ppermute | solution.py:415
  29.2 7.0 %collective-permute-start.4 = (bf16[36,8,128]{2,1,0:T(8,128)(2,1)S(1)}, bf16[36,8,128]{2,1,0:T(8,128)(2,1)S(1)}, u32[]{:S(2)}, u32[]{:S(2)}) collective-permute-start(bf16[36,8,128]{2,1,0:T(8,128)(2,1)S(1)} %bitcast.161), channel_id=1, source_target_pairs={{0,1},{1,2},{2,3},{4,5},{5,6},{6,7},{8,9},{9,10},{10,11},{12,13},{... | collective-permute-start | bytes 221192 | tf_op jit(solution)/shard_map/ppermute | solution.py:415
  33.4 5.7 %collective-permute-start.5 = (bf16[36,8,128]{2,1,0:T(8,128)(2,1)S(1)}, bf16[36,8,128]{2,1,0:T(8,128)(2,1)S(1)}, u32[]{:S(2)}, u32[]{:S(2)}) collective-permute-start(bf16[36,8,128]{2,1,0:T(8,128)(2,1)S(1)} %bitcast.162), channel_id=1, source_target_pairs={{1,0},{2,1},{3,2},{5,4},{6,5},{7,6},{9,8},{10,9},{11,10},{13,12},{... | collective-permute-start | bytes 221192 | tf_op jit(solution)/shard_map/ppermute | solution.py:415
  39.1 19.6 %collective-permute-start.6 = (bf16[3,36,8,128]{3,2,1,0:T(8,128)(2,1)S(1)}, bf16[3,36,8,128]{3,2,1,0:T(8,128)(2,1)S(1)}, u32[]{:S(2)}, u32[]{:S(2)}) collective-permute-start(bf16[3,36,8,128]{3,2,1,0:T(8,128)(2,1)S(1)} %pad_maximum_fusion.1), channel_id=1, source_target_pairs={{0,4},{4,8},{8,12},{12,16},{16,20},{20,24},{24,28},{28,0},{1,5},{5... | collective-permute-start | bytes 663560 | tf_op jit(solution)/shard_map/ppermute | solution.py:409
  39.1 19.6 %collective-permute-start.7 = (bf16[3,36,8,128]{3,2,1,0:T(8,128)(2,1)S(1)}, bf16[3,36,8,128]{3,2,1,0:T(8,128)(2,1)S(1)}, u32[]{:S(2)}, u32[]{:S(2)}) collective-permute-start(bf16[3,36,8,128]{3,2,1,0:T(8,128)(2,1)S(1)} %pad_maximum_fusion.1), channel_id=1, source_target_pairs={{0,28},{4,0},{8,4},{12,8},{16,12},{20,16},{24,20},{28,24},{1,29},{... | collective-permute-start | bytes 663560 | tf_op jit(solution)/shard_map/ppermute | solution.py:409
  58.7 2.9 %copy-start = (f32[3,512]{1,0:T(4,128)S(1)}, f32[3,512]{1,0:T(4,128)}, u32[]{:S(2)}) copy-start(f32[3,512]{1,0:T(4,128)} %field_ref.1) | copy-start | bytes 18436
  58.7 2.9 %copy-start.1 = (f32[3,512]{1,0:T(4,128)S(1)}, f32[3,512]{1,0:T(4,128)}, u32[]{:S(2)}) copy-start(f32[3,512]{1,0:T(4,128)} %ground_ref.1) | copy-start | bytes 18436
  108.8 11.4 %collective-permute-start.8 = (f32[3,36,3,128]{3,2,1,0:T(4,128)S(1)}, f32[3,36,3,128]{3,2,1,0:T(4,128)S(1)}, u32[]{:S(2)}, u32[]{:S(2)}) collective-permute-start(f32[3,36,3,128]{3,2,1,0:T(4,128)S(1)} %bitcast.171), channel_id=1, source_target_pairs={{0,4},{4,8},{8,12},{12,16},{16,20},{20,24},{24,28},{28,0},{1,5},{5... | collective-permute-start | bytes 497672 | tf_op jit(solution)/shard_map/ppermute | solution.py:409
  108.9 11.3 %collective-permute-start.9 = (f32[3,36,3,128]{3,2,1,0:T(4,128)S(1)}, f32[3,36,3,128]{3,2,1,0:T(4,128)S(1)}, u32[]{:S(2)}, u32[]{:S(2)}) collective-permute-start(f32[3,36,3,128]{3,2,1,0:T(4,128)S(1)} %bitcast.169), channel_id=1, source_target_pairs={{0,28},{4,0},{8,4},{12,8},{16,12},{20,16},{24,20},{28,24},{1,29},{... | collective-permute-start | bytes 497672 | tf_op jit(solution)/shard_map/ppermute | solution.py:409
  120.3 9.8 %collective-permute-start.10 = (f32[36,3,128]{2,1,0:T(4,128)S(1)}, f32[36,3,128]{2,1,0:T(4,128)S(1)}, u32[]{:S(2)}, u32[]{:S(2)}) collective-permute-start(f32[36,3,128]{2,1,0:T(4,128)S(1)} %get-tuple-element.84), channel_id=1, source_target_pairs={{0,1},{1,2},{2,3},{4,5},{5,6},{6,7},{8,9},{9,10},{10,11},{12,13},{... | collective-permute-start | bytes 165896 | tf_op jit(solution)/shard_map/ppermute | solution.py:415
  123.1 7.0 %collective-permute-start.11 = (f32[36,3,128]{2,1,0:T(4,128)S(1)}, f32[36,3,128]{2,1,0:T(4,128)S(1)}, u32[]{:S(2)}, u32[]{:S(2)}) collective-permute-start(f32[36,3,128]{2,1,0:T(4,128)S(1)} %get-tuple-element.85), channel_id=1, source_target_pairs={{1,0},{2,1},{3,2},{5,4},{6,5},{7,6},{9,8},{10,9},{11,10},{13,12},{... | collective-permute-start | bytes 165896 | tf_op jit(solution)/shard_map/ppermute | solution.py:415

commit v8 on v7

--- a/solution.py
+++ b/solution.py
@@ -17,7 +17,7 @@
 BUCKETS = 10
 FROWS = 92
 ZW = 384
-GROUP_D = 6
+GROUP_D = 5
 GROUP_V = 4
 BP = BX * CY
 

time: 139 us -> 142 us (1.022); the launches traced: 139 us -> 140 us
  transfers between devices with their start and end apart: 12 -> 12, of which waited for: 4 -> 4; matrix products, arithmetic and copies ran while one was open for 1% -> 1% of each run, Pallas kernels for 20% -> 21%
where the time goes in v8:
time: 142 us; the launch traced here: 140 us
  Pallas kernels  75.8 us (53%)
  starting transfers between devices  31.6 us (22%)
  other arithmetic  20.4 us (14%)
  waiting for transfers between devices  8.96 us (6%)
  local copies, waits for them, and re-layouts  1.97 us (1%)
    pallas_call x1, Pallas kernels, main_call(): pl.pallas_call(main_kernel, grid=(steps + 2,), in_specs=[smem()] * 2 + [w...  47 us
    ppermute x6, starting transfers between devices, line(): lax.ppermute(value, 'span', [(i, i + steps) for i in range(first, last)])  18.1 us
    pallas_call x1, Pallas kernels, spread_own_call(): pl.pallas_call(spread_own_kernel, grid=(1,), in_specs=[smem(), whole(tabl...  15.9 us
    ppermute x6, starting transfers between devices, ring(): lax.ppermute(value, 'stream', [(i, (i + steps) % count) for i in range(co...  13.6 us
    pallas_call x2, Pallas kernels, sample_own_call(): pl.pallas_call(kernel, grid=(1,), in_specs=[smem(), whole(table.shape), w...  12.9 us
    sort x1, other arithmetic, on_device(): _, *vel = lax.sort((order, own[0], own[1], own[2]), num_keys=1)  7.64 us
    sort x5, other arithmetic, on_device(): lax.sort((key, order) + tuple((inbound[c].astype(f32) for c in range(4)))...  6.36 us
    ppermute x6, waiting for transfers between devices, ring(): lax.ppermute(value, 'stream', [(i, (i + steps) % count) for i in range(co...  5.19 us
  transfers between devices with their start and end apart: 12, of which 4 were waited for; matrix products, arithmetic and copies ran while one was open for 1% of the time, Pallas kernels for 21%

profile of v8, /device:TPU:1, one launch (start us, length us, event | category | flops | bytes accessed | tf_op | source)
XLA Modules:
  0.0 140.1 jit_solution(16872481910994643218)
XLA Ops:
  0.6 0.0 copy-start.2
  0.7 0.8 fusion.7
  1.5 0.9 fusion.1
  2.4 5.2 %collective-permute-start = (bf16[3,8,512]{2,1,0:T(8,128)(2,1)S(1)}, bf16[3,8,512]{2,1,0:T(8,128)(2,1)S(1)}, u32[]{:S(2)}, u32[]{:S(2)}) collective-permute-start(bf16[3,8,512]{2,1,0:T(8,128)(2,1)S(1)} %get-tuple-element.96), channel_id=1, source_target_pairs={{0,28},{4,0},{8,4},{12,8},{16,12},{20,16},{24,20},{28,24},{1,29},{... | collective-permute-start | bytes 73736 | tf_op jit(solution)/shard_map/ppermute | solution.py:409
  7.5 0.0 collective-permute-start.1
  7.6 0.1 pad_add_fusion.2
  7.6 0.1 not_and_fusion
  7.7 0.7 collective-permute-done
  8.5 4.4 %collective-permute-done.1 = bf16[3,8,512]{2,1,0:T(8,128)(2,1)S(1)} collective-permute-done((bf16[3,8,512]{2,1,0:T(8,128)(2,1)S(1)}, bf16[3,8,512]{2,1,0:T(8,128)(2,1)S(1)}, u32[]{:S(2)}, u32[]{:S(2)}) %collective-permute-start.1) | collective-permute-done | bytes 24608 | tf_op jit(solution)/shard_map/ppermute | solution.py:409
  12.9 4.0 %collective-permute-start.2 = (bf16[3,8,512]{2,1,0:T(8,128)(2,1)S(1)}, bf16[3,8,512]{2,1,0:T(8,128)(2,1)S(1)}, u32[]{:S(2)}, u32[]{:S(2)}) collective-permute-start(bf16[3,8,512]{2,1,0:T(8,128)(2,1)S(1)} %get-tuple-element.93), channel_id=1, source_target_pairs={{1,0},{2,1},{3,2},{5,4},{6,5},{7,6},{9,8},{10,9},{11,10},{13,12},{... | collective-permute-start | bytes 73736 | tf_op jit(solution)/shard_map/ppermute | solution.py:415
  17.0 3.0 %collective-permute-start.3 = (bf16[3,8,512]{2,1,0:T(8,128)(2,1)S(1)}, bf16[3,8,512]{2,1,0:T(8,128)(2,1)S(1)}, u32[]{:S(2)}, u32[]{:S(2)}) collective-permute-start(bf16[3,8,512]{2,1,0:T(8,128)(2,1)S(1)} %get-tuple-element.94), channel_id=1, source_target_pairs={{0,1},{1,2},{2,3},{4,5},{5,6},{6,7},{8,9},{9,10},{10,11},{12,13},{... | collective-permute-start | bytes 73736 | tf_op jit(solution)/shard_map/ppermute | solution.py:415
  20.0 0.0 collective-permute-done.2
  20.0 0.9 collective-permute-done.3
  20.9 0.7 select_bitcast_fusion.1
  21.7 0.1 slice_convert_fusion.2
  21.8 0.1 fusion.61
  22.1 6.3 %sort.78 = (s32[4608]{0:T(1024)S(1)}, s32[4608]{0:T(1024)S(1)}, f32[4608]{0:T(1024)S(1)}, f32[4608]{0:T(1024)S(1)}, f32[4608]{0:T(1024)S(1)}, /*index=5*/f32[4608]{0:T(1024)S(1)}) sort(s32[4608]{0:T(1024)S(1)} %fusion.18, s32[4608]{0:T(1024)S(1)} %iota.121, f32[4608]{0:T(1024)S(1)} %reshape.729, f32[4608]{0:T(1024)S(1)} %reshape.730, f32[4608]{0:T(1024)S(1)} %reshape.731, ...), dimensions={0}, to_apply=%region_0.1 | sort | flops 59904 | bytes 221184 | tf_op jit(solution)/shard_map/sort | solution.py:450
  28.4 0.2 fusion.28
  28.9 0.2 stack.95
  29.2 4.2 %collective-permute-start.4 = (bf16[36,8,128]{2,1,0:T(8,128)(2,1)S(1)}, bf16[36,8,128]{2,1,0:T(8,128)(2,1)S(1)}, u32[]{:S(2)}, u32[]{:S(2)}) collective-permute-start(bf16[36,8,128]{2,1,0:T(8,128)(2,1)S(1)} %bitcast.161), channel_id=1, source_target_pairs={{0,1},{1,2},{2,3},{4,5},{5,6},{6,7},{8,9},{9,10},{10,11},{12,13},{... | collective-permute-start | bytes 221192 | tf_op jit(solution)/shard_map/ppermute | solution.py:415
  33.4 1.9 %collective-permute-start.5 = (bf16[36,8,128]{2,1,0:T(8,128)(2,1)S(1)}, bf16[36,8,128]{2,1,0:T(8,128)(2,1)S(1)}, u32[]{:S(2)}, u32[]{:S(2)}) collective-permute-start(bf16[36,8,128]{2,1,0:T(8,128)(2,1)S(1)} %bitcast.162), channel_id=1, source_target_pairs={{1,0},{2,1},{3,2},{5,4},{6,5},{7,6},{9,8},{10,9},{11,10},{13,12},{... | collective-permute-start | bytes 221192 | tf_op jit(solution)/shard_map/ppermute | solution.py:415
  35.3 0.2 convert_reduce_fusion.3
  35.5 0.1 fusion.57
  35.6 0.2 convert_reduce_fusion.2
  35.8 0.1 add_select_fusion.21
  35.9 0.1 select_reduce_fusion.4.list_ref
  36.0 0.2 select_reduce_fusion.5.refs_0_
  36.2 0.0 collective-permute-done.4
  36.2 2.9 %collective-permute-done.5 = bf16[36,8,128]{2,1,0:T(8,128)(2,1)S(1)} collective-permute-done((bf16[36,8,128]{2,1,0:T(8,128)(2,1)S(1)}, bf16[36,8,128]{2,1,0:T(8,128)(2,1)S(1)}, u32[]{:S(2)}, u32[]{:S(2)}) %collective-permute-start.5) | collective-permute-done | bytes 73760 | tf_op jit(solution)/shard_map/ppermute | solution.py:415
  39.1 0.1 collective-permute-start.6
  39.1 4.1 %collective-permute-start.7 = (bf16[3,36,8,128]{3,2,1,0:T(8,128)(2,1)S(1)}, bf16[3,36,8,128]{3,2,1,0:T(8,128)(2,1)S(1)}, u32[]{:S(2)}, u32[]{:S(2)}) collective-permute-start(bf16[3,36,8,128]{3,2,1,0:T(8,128)(2,1)S(1)} %pad_maximum_fusion.1), channel_id=1, source_target_pairs={{0,28},{4,0},{8,4},{12,8},{16,12},{20,16},{24,20},{28,24},{1,29},{... | collective-permute-start | bytes 663560 | tf_op jit(solution)/shard_map/ppermute | solution.py:409
  43.3 15.9 %spread_own.1.old_ref = f32[84,64,512]{2,1,0:T(8,128)} custom-call(s32[74]{0:T(128)S(1)} %select_reduce_fusion.4.list_ref, bf16[36,8,128]{2,1,0:T(8,128)(2,1)S(1)} %bitcast.164, bf16[8,384]{1,0:T(8,128)(2,1)S(1)} %copy-done.2), custom_call_target="tpu_custom_call" | custom-call | flops 10000000000 | bytes 30000000 | tf_op jit(solution)/shard_map/spread_own/pallas_call | solution.py:310
  59.2 0.0 copy-start
  59.2 0.0 copy-start.1
  59.2 0.0 collective-permute-done.6
  59.2 0.0 collective-permute-done.7
  59.3 0.1 pad_maximum_fusion
  59.3 0.3 slice_convert_fusion
  59.6 0.3 fusion.60
  59.9 0.5 select_reduce_fusion.3
  60.4 0.1 concatenate.99
  60.5 0.1 reshape.727
  60.6 0.2 convert_reduce_fusion.1
  60.8 0.2 select_reduce_fusion.1
  61.1 0.1 fusion.55
  61.1 0.4 convert_reduce_fusion
  61.6 0.1 add_select_fusion.15
  61.7 0.4 select_reduce_fusion
  62.1 47.0 %main.1 = (f32[4,64,16,512]{3,2,1,0:T(8,128)}, f32[324,8,128]{2,1,0:T(8,128)S(1)}, bf16[92,16,1536]{2,1,0:T(8,128)(2,1)S(1)}) custom-call(s32[650]{0:T(1024)S(1)} %select_add_fusion.units_ref, s32[326]{0:T(512)S(1)} %select_add_fusion.1.list_ref, bf16[324,8,128]{2,1,0:T(8,128)(2,1)S(1)} %bitcast.160, bf16[8,384]{1,0:T(8,128)(2,1)S(1)} %copy-done.2, ...), custom_call_target="tpu_custom_call" | custom-call | flops 40000000000 | bytes 60000000 | tf_op jit(solution)/shard_map/main/pallas_call | solution.py:327
  109.1 0.1 fusion.59
  109.2 0.1 collective-permute-start.8
  109.3 4.1 %collective-permute-start.9 = (f32[3,36,3,128]{3,2,1,0:T(4,128)S(1)}, f32[3,36,3,128]{3,2,1,0:T(4,128)S(1)}, u32[]{:S(2)}, u32[]{:S(2)}) collective-permute-start(f32[3,36,3,128]{3,2,1,0:T(4,128)S(1)} %bitcast.169), channel_id=1, source_target_pairs={{0,28},{4,0},{8,4},{12,8},{16,12},{20,16},{24,20},{28,24},{1,29},{... | collective-permute-start | bytes 497672 | tf_op jit(solution)/shard_map/ppermute | solution.py:409
  113.4 6.6 %sample_own.2 = f32[36,8,128]{2,1,0:T(8,128)S(1)} custom-call(s32[38]{0:T(128)S(1)} %select_reduce_fusion.5.refs_0_, bf16[36,8,128]{2,1,0:T(8,128)(2,1)S(1)} %bitcast.165, bf16[8,384]{1,0:T(8,128)(2,1)S(1)} %copy-done.2, bf16[92,16,1536]{2,1,0:T(8,128)(2,1)S(1)} %get-tuple-element.45.refs_3_), custom_call_target="tpu_custom_call" | custom-call | flops 10000000000 | bytes 30000000 | tf_op jit(solution)/shard_map/sample_own/pallas_call | solution.py:364
  120.0 0.0 collective-permute-done.8
  120.0 0.1 add_add_fusion
  120.2 3.0 %collective-permute-start.10 = (f32[36,3,128]{2,1,0:T(4,128)S(1)}, f32[36,3,128]{2,1,0:T(4,128)S(1)}, u32[]{:S(2)}, u32[]{:S(2)}) collective-permute-start(f32[36,3,128]{2,1,0:T(4,128)S(1)} %get-tuple-element.84), channel_id=1, source_target_pairs={{0,1},{1,2},{2,3},{4,5},{5,6},{6,7},{8,9},{9,10},{10,11},{12,13},{... | collective-permute-start | bytes 165896 | tf_op jit(solution)/shard_map/ppermute | solution.py:415
  123.2 1.9 %collective-permute-start.11 = (f32[36,3,128]{2,1,0:T(4,128)S(1)}, f32[36,3,128]{2,1,0:T(4,128)S(1)}, u32[]{:S(2)}, u32[]{:S(2)}) collective-permute-start(f32[36,3,128]{2,1,0:T(4,128)S(1)} %get-tuple-element.85), channel_id=1, source_target_pairs={{1,0},{2,1},{3,2},{5,4},{6,5},{7,6},{9,8},{10,9},{11,10},{13,12},{... | collective-permute-start | bytes 165896 | tf_op jit(solution)/shard_map/ppermute | solution.py:415
  125.1 6.3 %sample_own.3 = f32[36,8,128]{2,1,0:T(8,128)S(1)} custom-call(s32[38]{0:T(128)S(1)} %select_reduce_fusion.5.refs_0_, bf16[36,8,128]{2,1,0:T(8,128)(2,1)S(1)} %bitcast.166, bf16[8,384]{1,0:T(8,128)(2,1)S(1)} %copy-done.2, bf16[92,16,1536]{2,1,0:T(8,128)(2,1)S(1)} %get-tuple-element.45.refs_3_), custom_call_target="tpu_custom_call" | custom-call | flops 10000000000 | bytes 30000000 | tf_op jit(solution)/shard_map/sample_own/pallas_call | solution.py:364
  131.4 0.0 collective-permute-done.10
  131.4 0.1 fusion.5
  131.5 0.1 slice_reduce_fusion
  131.6 7.6 %sort.79 = (s32[4608]{0:T(1024)}, f32[4608]{0:T(1024)S(1)}, f32[4608]{0:T(1024)S(1)}, f32[4608]{0:T(1024)S(1)}, s32[4608]{0:T(1024)}) sort(s32[4608]{0:T(1024)S(1)} %get-tuple-element.42, f32[4608]{0:T(1024)S(1)} %bitcast.175, f32[4608]{0:T(1024)S(1)} %bitcast.174, f32[4608]{0:T(1024)S(1)} %bitcast.173, s32[4608]{0:T(1024)S(1)} %iota.136), dimensions={0}, to_apply=%region_13.14 | sort | flops 59904 | bytes 184320 | tf_op jit(solution)/shard_map/sort | solution.py:489
  139.4 0.1 pad_maximum_fusion.3
  139.4 0.7 broadcast_in_dim.342
  (66 shorter events, 0.7 us)
Async XLA Ops:
  0.6 42.7 %copy-start.2 = (bf16[8,384]{1,0:T(8,128)(2,1)S(1)}, bf16[8,384]{1,0:T(8,128)(2,1)}, u32[]{:S(2)}) copy-start(bf16[8,384]{1,0:T(8,128)(2,1)} %constant.251.clone.pick_ref.refs_2_) | copy-start | bytes 18436
  2.4 6.1 %collective-permute-start = (bf16[3,8,512]{2,1,0:T(8,128)(2,1)S(1)}, bf16[3,8,512]{2,1,0:T(8,128)(2,1)S(1)}, u32[]{:S(2)}, u32[]{:S(2)}) collective-permute-start(bf16[3,8,512]{2,1,0:T(8,128)(2,1)S(1)} %get-tuple-element.96), channel_id=1, source_target_pairs={{0,28},{4,0},{8,4},{12,8},{16,12},{20,16},{24,20},{28,24},{1,29},{... | collective-permute-start | bytes 73736 | tf_op jit(solution)/shard_map/ppermute | solution.py:409
  7.5 5.4 %collective-permute-start.1 = (bf16[3,8,512]{2,1,0:T(8,128)(2,1)S(1)}, bf16[3,8,512]{2,1,0:T(8,128)(2,1)S(1)}, u32[]{:S(2)}, u32[]{:S(2)}) collective-permute-start(bf16[3,8,512]{2,1,0:T(8,128)(2,1)S(1)} %get-tuple-element.97), channel_id=1, source_target_pairs={{0,4},{4,8},{8,12},{12,16},{16,20},{20,24},{24,28},{28,0},{1,5},{5... | collective-permute-start | bytes 73736 | tf_op jit(solution)/shard_map/ppermute | solution.py:409
  12.9 7.1 %collective-permute-start.2 = (bf16[3,8,512]{2,1,0:T(8,128)(2,1)S(1)}, bf16[3,8,512]{2,1,0:T(8,128)(2,1)S(1)}, u32[]{:S(2)}, u32[]{:S(2)}) collective-permute-start(bf16[3,8,512]{2,1,0:T(8,128)(2,1)S(1)} %get-tuple-element.93), channel_id=1, source_target_pairs={{1,0},{2,1},{3,2},{5,4},{6,5},{7,6},{9,8},{10,9},{11,10},{13,12},{... | collective-permute-start | bytes 73736 | tf_op jit(solution)/shard_map/ppermute | solution.py:415
  17.0 3.9 %collective-permute-start.3 = (bf16[3,8,512]{2,1,0:T(8,128)(2,1)S(1)}, bf16[3,8,512]{2,1,0:T(8,128)(2,1)S(1)}, u32[]{:S(2)}, u32[]{:S(2)}) collective-permute-start(bf16[3,8,512]{2,1,0:T(8,128)(2,1)S(1)} %get-tuple-element.94), channel_id=1, source_target_pairs={{0,1},{1,2},{2,3},{4,5},{5,6},{6,7},{8,9},{9,10},{10,11},{12,13},{... | collective-permute-start | bytes 73736 | tf_op jit(solution)/shard_map/ppermute | solution.py:415
  29.2 7.0 %collective-permute-start.4 = (bf16[36,8,128]{2,1,0:T(8,128)(2,1)S(1)}, bf16[36,8,128]{2,1,0:T(8,128)(2,1)S(1)}, u32[]{:S(2)}, u32[]{:S(2)}) collective-permute-start(bf16[36,8,128]{2,1,0:T(8,128)(2,1)S(1)} %bitcast.161), channel_id=1, source_target_pairs={{0,1},{1,2},{2,3},{4,5},{5,6},{6,7},{8,9},{9,10},{10,11},{12,13},{... | collective-permute-start | bytes 221192 | tf_op jit(solution)/shard_map/ppermute | solution.py:415
  33.4 5.7 %collective-permute-start.5 = (bf16[36,8,128]{2,1,0:T(8,128)(2,1)S(1)}, bf16[36,8,128]{2,1,0:T(8,128)(2,1)S(1)}, u32[]{:S(2)}, u32[]{:S(2)}) collective-permute-start(bf16[36,8,128]{2,1,0:T(8,128)(2,1)S(1)} %bitcast.162), channel_id=1, source_target_pairs={{1,0},{2,1},{3,2},{5,4},{6,5},{7,6},{9,8},{10,9},{11,10},{13,12},{... | collective-permute-start | bytes 221192 | tf_op jit(solution)/shard_map/ppermute | solution.py:415
  39.1 20.2 %collective-permute-start.6 = (bf16[3,36,8,128]{3,2,1,0:T(8,128)(2,1)S(1)}, bf16[3,36,8,128]{3,2,1,0:T(8,128)(2,1)S(1)}, u32[]{:S(2)}, u32[]{:S(2)}) collective-permute-start(bf16[3,36,8,128]{3,2,1,0:T(8,128)(2,1)S(1)} %pad_maximum_fusion.1), channel_id=1, source_target_pairs={{0,4},{4,8},{8,12},{12,16},{16,20},{20,24},{24,28},{28,0},{1,5},{5... | collective-permute-start | bytes 663560 | tf_op jit(solution)/shard_map/ppermute | solution.py:409
  39.1 20.1 %collective-permute-start.7 = (bf16[3,36,8,128]{3,2,1,0:T(8,128)(2,1)S(1)}, bf16[3,36,8,128]{3,2,1,0:T(8,128)(2,1)S(1)}, u32[]{:S(2)}, u32[]{:S(2)}) collective-permute-start(bf16[3,36,8,128]{3,2,1,0:T(8,128)(2,1)S(1)} %pad_maximum_fusion.1), channel_id=1, source_target_pairs={{0,28},{4,0},{8,4},{12,8},{16,12},{20,16},{24,20},{28,24},{1,29},{... | collective-permute-start | bytes 663560 | tf_op jit(solution)/shard_map/ppermute | solution.py:409
  59.2 2.9 %copy-start = (f32[3,512]{1,0:T(4,128)S(1)}, f32[3,512]{1,0:T(4,128)}, u32[]{:S(2)}) copy-start(f32[3,512]{1,0:T(4,128)} %field_ref.1) | copy-start | bytes 18436
  59.2 2.9 %copy-start.1 = (f32[3,512]{1,0:T(4,128)S(1)}, f32[3,512]{1,0:T(4,128)}, u32[]{:S(2)}) copy-start(f32[3,512]{1,0:T(4,128)} %ground_ref.1) | copy-start | bytes 18436
  109.2 10.8 %collective-permute-start.8 = (f32[3,36,3,128]{3,2,1,0:T(4,128)S(1)}, f32[3,36,3,128]{3,2,1,0:T(4,128)S(1)}, u32[]{:S(2)}, u32[]{:S(2)}) collective-permute-start(f32[3,36,3,128]{3,2,1,0:T(4,128)S(1)} %bitcast.171), channel_id=1, source_target_pairs={{0,4},{4,8},{8,12},{12,16},{16,20},{20,24},{24,28},{28,0},{1,5},{5... | collective-permute-start | bytes 497672 | tf_op jit(solution)/shard_map/ppermute | solution.py:409
  109.3 10.7 %collective-permute-start.9 = (f32[3,36,3,128]{3,2,1,0:T(4,128)S(1)}, f32[3,36,3,128]{3,2,1,0:T(4,128)S(1)}, u32[]{:S(2)}, u32[]{:S(2)}) collective-permute-start(f32[3,36,3,128]{3,2,1,0:T(4,128)S(1)} %bitcast.169), channel_id=1, source_target_pairs={{0,28},{4,0},{8,4},{12,8},{16,12},{20,16},{24,20},{28,24},{1,29},{... | collective-permute-start | bytes 497672 | tf_op jit(solution)/shard_map/ppermute | solution.py:409
  120.2 11.2 %collective-permute-start.10 = (f32[36,3,128]{2,1,0:T(4,128)S(1)}, f32[36,3,128]{2,1,0:T(4,128)S(1)}, u32[]{:S(2)}, u32[]{:S(2)}) collective-permute-start(f32[36,3,128]{2,1,0:T(4,128)S(1)} %get-tuple-element.84), channel_id=1, source_target_pairs={{0,1},{1,2},{2,3},{4,5},{5,6},{6,7},{8,9},{9,10},{10,11},{12,13},{... | collective-permute-start | bytes 165896 | tf_op jit(solution)/shard_map/ppermute | solution.py:415
  123.2 8.3 %collective-permute-start.11 = (f32[36,3,128]{2,1,0:T(4,128)S(1)}, f32[36,3,128]{2,1,0:T(4,128)S(1)}, u32[]{:S(2)}, u32[]{:S(2)}) collective-permute-start(f32[36,3,128]{2,1,0:T(4,128)S(1)} %get-tuple-element.85), channel_id=1, source_target_pairs={{1,0},{2,1},{3,2},{5,4},{6,5},{7,6},{9,8},{10,9},{11,10},{13,12},{... | collective-permute-start | bytes 165896 | tf_op jit(solution)/shard_map/ppermute | solution.py:415
